TPU v7x, 32 devices: a whole 2x2x4 slice. The times are simulated.
32 devices in a mesh: dp: 8 (over z, core), expert: 4 (over y, x).
Axes of the slice: x: 2, y: 2, z: 4, core: 2. Of those that a mesh axis runs over, the one named last changes fastest.
Arguments:
- inputs: bfloat16 [8, 2, 512, 2048], P('dp', None, 'expert'), may hold values from -6 to 6
- attn_routes: int32 [8, 2, 512, 2], P('dp', None, 'expert'), may hold values from 0 to 3, all different within a row; in each aligned block of 128 rows (0 to 127, 128 to 255, ..., all dimensions but the last counted through in order) at most 64 rows name the same one
- mlp_routes: int32 [8, 2, 512, 2], P('dp', None, 'expert'), may hold values from 0 to 3, all different within a row; in each aligned block of 128 rows (0 to 127, 128 to 255, ..., all dimensions but the last counted through in order) at most 64 rows name the same one
- pic_start: int32 [8], P('dp'), may hold values from 0 to 768, as said below
- kv_weight: bfloat16 [2048, 4096], P(('dp', 'expert')), may hold values from -0.125 to 0.125
- router_weight: bfloat16 [2048, 8], P(('dp', 'expert')), may hold values from -0.09375 to 0.09375
- norm_gains: bfloat16 [2048, 2], P(('dp', 'expert')), may hold values from 0.5 to 1.5
- q_weight: bfloat16 [4, 2048, 2048], P('expert', 'dp'), may hold values from -1 to 1
- o_weight: bfloat16 [4, 2048, 2048], P('expert', 'dp'), may hold values from -1.5 to 1.5
- gate_weight: bfloat16 [4, 2048, 5632], P('expert', 'dp'), may hold values from -0.125 to 0.125
- up_weight: bfloat16 [4, 2048, 5632], P('expert', 'dp'), may hold values from -0.125 to 0.125
- down_weight: bfloat16 [4, 5632, 2048], P('expert', 'dp'), may hold values from -0.078125 to 0.078125
- cotangent: bfloat16 [8, 2, 512, 2048], P('dp', None, 'expert'), may hold values from -6 to 6
Outputs:
- out_act: bfloat16 [8, 2, 512, 2048], P('dp', None, 'expert')
- grad_x: float32 [8, 2, 512, 2048], P('dp', None, 'expert')
- grad_kv: float32 [2048, 4096], P(('dp', 'expert'))
- grad_router: float32 [2048, 8], P(('dp', 'expert'))
- grad_gains: float32 [2048, 2], P(('dp', 'expert'))
- grad_q: float32 [4, 2048, 2048], P('expert', 'dp')
- grad_o: float32 [4, 2048, 2048], P('expert', 'dp')
- grad_gate: float32 [4, 2048, 5632], P('expert', 'dp')
- grad_up: float32 [4, 2048, 5632], P('expert', 'dp')
- grad_down: float32 [4, 5632, 2048], P('expert', 'dp')
- clipped_q: bfloat16 [4, 2048, 2048], P('expert', 'dp')
- clipped_key: bfloat16 [2048, 2048], P(('dp', 'expert'))
Inputs may be any that keep to these rules, and one draw needn't show every extreme that they name: `attn_routes`: in every micro-batch, among the 128 tokens of one device each expert is chosen by exactly 64 (token, choice) pairs; a token's 2 choices differ. `mlp_routes`: in every micro-batch, among the 128 tokens of one device each expert is chosen by exactly 64 (token, choice) pairs; a token's 2 choices differ. `pic_start`: each picture piece lies inside one micro-batch of its sequence.
All inputs are finite; a program needn't handle non-finite values.
Results may differ from a plain program's by a relative error of at most 0.02.
Values may be sent and summed in bfloat16 or wider, within the bound.
No kernel may reach another device: no remote copies, remote signals or barrier semaphores. Data moves between devices by JAX's collectives and lax.ppermute only.
A program may use at most 384 MiB of HBM per device.

v0:
```python
import math

import jax
import jax.numpy as jnp
from jax import lax
from jax.experimental import pallas as pl
from jax.experimental.pallas import tpu as pltpu
from jax.sharding import PartitionSpec as P

HEADS = 16
HSZ = 128
TOPK = 2
PIC = 256
MICRO = 2
ORDER = (1, 0)

norm_eps = 1e-06
logit_cap = 8.0
masked_low = -1e30
bf16 = jnp.bfloat16
f32 = jnp.float32


def mm(left, right):
    return jnp.dot(left, right, preferred_element_type=f32)


def mm_t(left, right):
    return lax.dot_general(left, right, (((1,), (1,)), ((), ())), preferred_element_type=f32)


def t_mm(left, right):
    return lax.dot_general(left, right, (((0,), (0,)), ((), ())), preferred_element_type=f32)


def exact(left, right, dims):
    return lax.dot_general(
        left, right, (dims, ((), ())), precision=lax.Precision.HIGHEST, preferred_element_type=f32
    )


def rope_tables(positions):
    half = HSZ // 2
    freq = jnp.exp(jnp.arange(half, dtype=f32) * (-math.log(10000.0) / half))
    angles = positions.astype(f32)[..., None] * freq
    cosine, sine = jnp.cos(angles), jnp.sin(angles)
    return (
        jnp.concatenate([cosine, cosine], axis=-1),
        jnp.concatenate([-sine, sine], axis=-1),
    )


def inverse_rms(values):
    return lax.rsqrt(jnp.mean(values * values, axis=-1, keepdims=True) + norm_eps)


def norm_back(values, inverse, gain, upstream):
    scaled = upstream * gain
    gain_grad = jnp.sum(upstream * values * inverse, axis=0)
    values_grad = inverse * scaled - values * inverse * inverse * inverse * jnp.mean(
        scaled * values, axis=-1, keepdims=True
    )
    return values_grad, gain_grad


def selection(hot, slots):
    tokens = hot.shape[-1]
    before = jnp.triu(jnp.ones((tokens, tokens), bf16), 1)
    rank = jnp.dot(hot.astype(bf16), before, preferred_element_type=f32)
    slot = jnp.arange(slots, dtype=jnp.int32)[:, None]
    taken = (rank.astype(jnp.int32)[..., None, :] == slot) & (hot[..., None, :] > 0)
    return taken.astype(bf16)


def kv_kernel(a_ref, w_ref, cos_ref, sin_ref, o_ref):
    got = jnp.dot(a_ref[...], w_ref[...], preferred_element_type=f32)
    cosine, sine = cos_ref[0], sin_ref[0]
    for part in range(got.shape[1] // HSZ):
        piece = got[:, part * HSZ : (part + 1) * HSZ]
        turned = piece * cosine + pltpu.roll(piece, HSZ // 2, 1) * sine
        o_ref[0, :, part * HSZ : (part + 1) * HSZ] = turned.astype(bf16)


def project_kv(a_rows, kv_cols, cosine, sine):
    rows, width = a_rows.shape
    group = kv_cols.shape[1] // 2
    step = min(256, group)
    per = group // step
    return pl.pallas_call(
        kv_kernel,
        grid=(2 * per,),
        in_specs=[
            pl.BlockSpec((rows, width), lambda g: (0, 0)),
            pl.BlockSpec((width, step), lambda g: (0, g)),
            pl.BlockSpec((1, rows, HSZ), lambda g: (g // per, 0, 0)),
            pl.BlockSpec((1, rows, HSZ), lambda g: (g // per, 0, 0)),
        ],
        out_specs=pl.BlockSpec((1, rows, step), lambda g: (g // per, 0, g % per)),
        out_shape=jax.ShapeDtypeStruct((2, rows, group), bf16),
        name="project_kv",
    )(a_rows, kv_cols, cosine, sine)


def kv_back_kernel(*refs):
    pieces, (cos_ref, sin_ref, o_ref) = refs[:-3], refs[-3:]
    cosine, sine = cos_ref[0], sin_ref[0]
    total = pieces[0][0].astype(f32)
    for piece in pieces[1:]:
        total = total + piece[0].astype(f32)
    for part in range(total.shape[1] // HSZ):
        cut = total[:, part * HSZ : (part + 1) * HSZ]
        turned = cut * cosine - pltpu.roll(cut, HSZ // 2, 1) * sine
        o_ref[:, part * HSZ : (part + 1) * HSZ] = turned.astype(bf16)


def sum_kv_grads(pieces, cosine, sine):
    _, rows, group = pieces[0].shape
    return pl.pallas_call(
        kv_back_kernel,
        grid=(2,),
        in_specs=[pl.BlockSpec((1, rows, group), lambda g: (g, 0, 0)) for _ in pieces]
        + [pl.BlockSpec((1, rows, HSZ), lambda g: (g, 0, 0))] * 2,
        out_specs=pl.BlockSpec((rows, group), lambda g: (0, g)),
        out_shape=jax.ShapeDtypeStruct((rows, 2 * group), bf16),
        name="sum_kv_grads",
    )(*pieces, cosine, sine)


def scores_of(query, keys, place_ref, qpos, micro, tokens, group_index):
    parts = []
    flip = (place_ref[0] ^ group_index) * tokens
    start = place_ref[1]
    for m in range(micro + 1):
        got = lax.dot_general(
            query, keys[m], (((1,), (1,)), ((), ())), preferred_element_type=f32
        ) * (HSZ**-0.5)
        if m == micro:
            count = got.shape[1]
            kpos = micro * count + (lax.broadcasted_iota(jnp.int32, got.shape, 1) ^ flip)
            inside_q = (qpos >= start) & (qpos < start + PIC)
            inside_k = (kpos >= start) & (kpos < start + PIC)
            keep = (kpos <= qpos) | (inside_q & inside_k)
            got = jnp.where(keep, got, masked_low)
        parts.append(got)
    peak = parts[0].max(axis=1, keepdims=True)
    for got in parts[1:]:
        peak = jnp.maximum(peak, got.max(axis=1, keepdims=True))
    lifted = [jnp.exp(got - peak) for got in parts]
    total = lifted[0].sum(axis=1, keepdims=True)
    for got in lifted[1:]:
        total = total + got.sum(axis=1, keepdims=True)
    scale = 1.0 / total
    return [got * scale for got in lifted], peak


def attend(q_pre, cosine, sine, qpos, kvs, place, tokens):
    micro = len(kvs) - 1
    rows, inner = q_pre.shape
    experts, _, keys, group = kvs[0].shape
    hg = group // HSZ

    def kernel(place_ref, q_ref, cos_ref, sin_ref, pos_ref, *rest):
        kv_refs, (mixed_ref, rot_ref, peak_ref) = rest[:-3], rest[-3:]
        g = pl.program_id(0)
        q = q_ref[...]
        turned = (q * cos_ref[...] + pltpu.roll(q, HSZ // 2, 1) * sin_ref[...]).astype(bf16)
        rot_ref[...] = turned
        probs, peak = scores_of(
            turned, [r[0, 0] for r in kv_refs], place_ref, pos_ref[...], micro, tokens, g // hg
        )
        mixed = jnp.zeros((rows, HSZ), f32)
        for m in range(micro + 1):
            mixed = mixed + jnp.dot(
                probs[m].astype(bf16), kv_refs[m][0, 1], preferred_element_type=f32
            )
        mixed_ref[...] = mixed.astype(bf16)
        peak_ref[...] = jnp.full(peak_ref.shape, jnp.max(peak), f32)

    def head(g, s):
        return (s[0] ^ (g // hg)) * hg + g % hg

    column = pl.BlockSpec((rows, HSZ), lambda g, s: (0, head(g, s)))
    full = lambda shape: pl.BlockSpec(shape, lambda g, s: (0,) * len(shape))
    return pl.pallas_call(
        kernel,
        grid_spec=pltpu.PrefetchScalarGridSpec(
            num_scalar_prefetch=1,
            grid=(HEADS,),
            in_specs=[column, full((rows, HSZ)), full((rows, HSZ)), full((rows, 1))]
            + [
                pl.BlockSpec((1, 2, keys, HSZ), lambda g, s: (g // hg, 0, 0, g % hg))
                for _ in kvs
            ],
            out_specs=[
                column,
                column,
                pl.BlockSpec((1, 8, 128), lambda g, s: (head(g, s), 0, 0)),
            ],
        ),
        out_shape=[
            jax.ShapeDtypeStruct((rows, inner), bf16),
            jax.ShapeDtypeStruct((rows, inner), bf16),
            jax.ShapeDtypeStruct((HEADS, 8, 128), f32),
        ],
        name="attend",
    )(place, q_pre, cosine, sine, qpos, *kvs)


def attend_back(q_rot, d_mixed, cosine, sine, qpos, kvs, later, place, tokens):
    micro = len(kvs) - 1
    rows, inner = q_rot.shape
    experts, _, keys, group = kvs[0].shape
    hg = group // HSZ
    held = len(later)

    def kernel(place_ref, q_ref, dm_ref, cos_ref, sin_ref, pos_ref, *rest):
        kv_refs = rest[: micro + 1]
        later_refs = rest[micro + 1 : micro + 1 + held]
        dq_ref, dkv_refs = rest[micro + 1 + held], rest[micro + 2 + held :]
        g = pl.program_id(0)
        q = q_ref[...]
        dm = dm_ref[...]
        probs, _ = scores_of(
            q, [r[0, 0] for r in kv_refs], place_ref, pos_ref[...], micro, tokens, g // hg
        )
        d_probs = [
            lax.dot_general(dm, r[0, 1], (((1,), (1,)), ((), ())), preferred_element_type=f32)
            for r in kv_refs
        ]
        inner_sum = jnp.sum(d_probs[0] * probs[0], axis=1, keepdims=True)
        for m in range(1, micro + 1):
            inner_sum = inner_sum + jnp.sum(d_probs[m] * probs[m], axis=1, keepdims=True)
        d_q = jnp.zeros((rows, HSZ), f32)
        for m in range(micro + 1):
            d_scores = (probs[m] * (d_probs[m] - inner_sum)).astype(bf16)
            d_q = d_q + jnp.dot(d_scores, kv_refs[m][0, 0], preferred_element_type=f32)
            d_k = lax.dot_general(
                d_scores, q, (((0,), (0,)), ((), ())), preferred_element_type=f32
            ) * (HSZ**-0.5)
            d_v = lax.dot_general(
                probs[m].astype(bf16), dm, (((0,), (0,)), ((), ())), preferred_element_type=f32
            )
            if m < held:
                d_k = d_k + later_refs[m][0, 0].astype(f32)
                d_v = d_v + later_refs[m][0, 1].astype(f32)
            dkv_refs[m][0, 0] = d_k.astype(bf16)
            dkv_refs[m][0, 1] = d_v.astype(bf16)
        d_q = d_q * (HSZ**-0.5)
        dq_ref[...] = (d_q * cos_ref[...] - pltpu.roll(d_q, HSZ // 2, 1) * sin_ref[...]).astype(
            bf16
        )

    def head(g, s):
        return (s[0] ^ (g // hg)) * hg + g % hg

    column = pl.BlockSpec((rows, HSZ), lambda g, s: (0, head(g, s)))
    full = lambda shape: pl.BlockSpec(shape, lambda g, s: (0,) * len(shape))
    kv_spec = pl.BlockSpec((1, 2, keys, HSZ), lambda g, s: (g // hg, 0, 0, g % hg))
    return pl.pallas_call(
        kernel,
        grid_spec=pltpu.PrefetchScalarGridSpec(
            num_scalar_prefetch=1,
            grid=(HEADS,),
            in_specs=[column, column, full((rows, HSZ)), full((rows, HSZ)), full((rows, 1))]
            + [kv_spec] * (micro + 1 + held),
            out_specs=[column] + [kv_spec] * (micro + 1),
        ),
        out_shape=[jax.ShapeDtypeStruct((rows, inner), bf16)]
        + [jax.ShapeDtypeStruct(kvs[0].shape, bf16) for _ in kvs],
        name="attend_back",
    )(place, q_rot, d_mixed, cosine, sine, qpos, *kvs, *later)


def per_device(
    inputs,
    attn_routes,
    mlp_routes,
    pic_start,
    kv_weight,
    router_weight,
    norm_gains,
    q_weight,
    o_weight,
    gate_weight,
    up_weight,
    down_weight,
    cotangent,
):
    experts = lax.axis_size("expert")
    dp_size = lax.axis_size("dp")
    stages = dp_size // 2
    own = lax.axis_index("expert")
    dp_index = lax.axis_index("dp")
    stage, core = dp_index // 2, dp_index % 2
    tokens, width = inputs.shape[2], inputs.shape[3]
    inner = HEADS * HSZ
    group = inner // experts
    slots = tokens * TOPK // experts
    span = tokens * experts
    rows_each = kv_weight.shape[0]
    hidden = gate_weight.shape[2]
    part = hidden // stages
    routed = experts * slots

    def across(block, k):
        if k == 0:
            return block
        return lax.ppermute(block, "expert", [(j, j ^ k) for j in range(experts)])

    def along(block, k):
        if k % stages == 0:
            return block
        return lax.ppermute(
            block, "dp", [(j, ((j // 2 + k) % stages) * 2 + j % 2) for j in range(dp_size)]
        )

    def partner(block):
        return lax.ppermute(block, "dp", [(j, j ^ 1) for j in range(dp_size)])

    def pick(array, index, axis=0):
        return lax.dynamic_index_in_dim(array, index, axis, keepdims=False)

    small = jnp.concatenate(
        [
            attn_routes.reshape(-1).astype(bf16),
            mlp_routes.reshape(-1).astype(bf16),
            router_weight.reshape(-1),
            norm_gains.reshape(-1),
        ]
    )
    length = small.shape[0]
    small = jnp.pad(small, (0, -length % 128)).reshape(-1, 128)
    small = lax.all_gather(lax.all_gather(small, "expert", axis=0), "dp", axis=0)
    small = small.reshape(dp_size, experts, -1)
    count = MICRO * tokens * TOPK
    xor_order = own ^ jnp.arange(experts, dtype=jnp.int32)
    stage_order = (stage - jnp.arange(stages, dtype=jnp.int32)) % stages
    routes_a = pick(small[:, :, :count], dp_index).astype(jnp.int32)
    routes_a = routes_a.reshape(experts, MICRO, tokens, TOPK)[xor_order]
    routes_m = small[:, :, count : 2 * count].reshape(stages, 2, experts, count)
    routes_m = pick(routes_m, core, 1).astype(jnp.int32)
    routes_m = routes_m.reshape(stages, experts, MICRO, tokens, TOPK)[stage_order][:, xor_order]
    router = small[:, :, 2 * count : 2 * count + rows_each * 2 * experts].reshape(
        width, 2 * experts
    )
    gains = small[:, :, 2 * count + rows_each * 2 * experts : length].reshape(width, 2)
    gain_1, gain_2 = gains[:, 0].astype(f32), gains[:, 1].astype(f32)
    router_a, router_m = router[:, :experts], router[:, experts:]

    kv_split = kv_weight.reshape(rows_each, 2, experts, group)
    kv_got = [
        across(pick(kv_split, own ^ k, 2).reshape(rows_each, 2 * group), k) for k in range(experts)
    ]
    kv_rows = jnp.stack(kv_got)[xor_order].reshape(experts * rows_each, 2 * group)
    kv_cols = lax.all_gather(kv_rows, "dp", axis=0, tiled=True)
    q_full = lax.all_gather(q_weight[0], "dp", axis=0, tiled=True)
    o_full = lax.all_gather(o_weight[0], "dp", axis=0, tiled=True)

    x_blocks = jnp.stack([across(inputs[0], k) for k in range(experts)], axis=1)
    x_all = x_blocks.reshape(MICRO, span, width).astype(f32)
    a_all = (x_all * inverse_rms(x_all) * gain_1).astype(bf16)

    def stage_columns(weight):
        split = weight.reshape(weight.shape[0], stages, part)
        got = [along(pick(split, (stage + k) % stages, 1), k) for k in range(stages)]
        mine = jnp.stack(got)[stage_order]
        theirs = partner(mine)
        first = jnp.where(core == 0, mine, theirs)
        second = jnp.where(core == 0, theirs, mine)
        return jnp.stack([first, second], axis=1).reshape(width, part)

    gate_in, up_in, _ = lax.optimization_barrier((gate_weight[0], up_weight[0], q_full))
    gate_w, up_w = stage_columns(gate_in), stage_columns(up_in)
    down_other = partner(down_weight[0])
    down_w = jnp.concatenate(
        [
            jnp.where(core == 0, down_weight[0], down_other),
            jnp.where(core == 0, down_other, down_weight[0]),
        ]
    )

    token = jnp.arange(tokens, dtype=jnp.int32)
    pick_a = selection((routes_a == own).any(-1).astype(f32), slots)
    place_a = jnp.einsum("kmst,t->kms", pick_a, token.astype(bf16), preferred_element_type=f32)
    other_a = jnp.einsum(
        "kmst,kmt->kms",
        pick_a,
        (routes_a.sum(-1) - own).astype(bf16),
        preferred_element_type=f32,
    ).astype(jnp.int32)
    query_pos = (
        place_a.astype(jnp.int32)
        + xor_order[:, None, None] * tokens
        + jnp.arange(MICRO, dtype=jnp.int32)[None, :, None] * span
    )
    home_a = selection(
        (routes_a[0][None] == xor_order[:, None, None, None]).any(-1).astype(f32), slots
    )
    home_m = selection(
        (routes_m[:, 0][:, None] == xor_order[None, :, None, None, None]).any(-1).astype(f32),
        slots,
    )
    pick_m = selection((routes_m == own).any(-1).astype(f32), slots)
    other_m = jnp.einsum(
        "kjmst,kjmt->jkms",
        pick_m,
        (routes_m.sum(-1) - own).astype(bf16),
        preferred_element_type=f32,
    ).astype(jnp.int32)

    def pair_gates(rows_low, router_cols, other):
        logits = mm(rows_low, router_cols)
        column = jnp.arange(experts, dtype=jnp.int32)[None, :]
        mine = (column == own).astype(f32)
        theirs = (column == other[:, None]).astype(f32)
        turn = mine - theirs
        gate = jax.nn.sigmoid(jnp.sum(logits * turn, axis=1, keepdims=True))
        rest = jax.nn.sigmoid(-jnp.sum(logits * turn, axis=1, keepdims=True))
        return gate, rest, turn

    place = jnp.stack([own, pic_start[0]]).astype(jnp.int32)
    sequence_pos = (
        jnp.arange(MICRO, dtype=jnp.int32)[:, None] * span
        + (jnp.arange(span, dtype=jnp.int32) ^ (own * tokens))[None, :]
    )
    key_cos, key_sin = rope_tables(sequence_pos)
    plain_cos, plain_sin = jnp.ones_like(key_cos), jnp.zeros_like(key_sin)
    key_cos = jnp.stack([key_cos, plain_cos], axis=1)
    key_sin = jnp.stack([key_sin, plain_sin], axis=1)
    query_cos, query_sin = rope_tables(query_pos)

    kv_all = []
    for m in range(MICRO):
        mine = project_kv(a_all[m], kv_cols, key_cos[m], key_sin[m])
        kv_all.append(jnp.stack([across(mine, k) for k in range(experts)]))

    kept = {}
    for m in ORDER:
        a_blocks = a_all[m].reshape(experts, tokens, width)
        a_pairs = jnp.einsum(
            "kst,ktd->ksd", pick_a[:, m], a_blocks, preferred_element_type=f32
        ).astype(bf16)
        a_pairs = a_pairs.reshape(routed, width)
        gate, rest, turn = pair_gates(a_pairs, router_a, other_a[:, m].reshape(-1))
        q_cos = query_cos[:, m].reshape(routed, HSZ)
        q_sin = query_sin[:, m].reshape(routed, HSZ)
        q_pos = query_pos[:, m].reshape(routed, 1)
        mixed, q_rot, peak = attend(
            mm(a_pairs, q_full), q_cos, q_sin, q_pos, kv_all[: m + 1], place, tokens
        )
        rows = mm(mixed, o_full)
        kept[m] = (a_pairs, gate, rest, turn, q_cos, q_sin, q_pos, mixed, q_rot, peak, rows)

    g_in, _ = lax.optimization_barrier((cotangent[0], gate_w))
    middles, inverses, routed_rows, routed_grads = {}, {}, {}, {}
    for m in ORDER:
        gated = (kept[m][1] * kept[m][-1]).astype(bf16).reshape(experts, slots, width)
        back = jnp.stack([across(gated[k], k) for k in range(experts)])
        summed = jnp.einsum("kst,ksd->td", home_a[:, m], back, preferred_element_type=f32)
        middle = inputs[0, m].astype(f32) + summed
        inverse = inverse_rms(middle)
        b_low = (middle * inverse * gain_2).astype(bf16)
        middles[m], inverses[m] = middle, inverse

        def dispatch(low):
            stack = jnp.stack([along(low, k) for k in range(stages)])
            sent = []
            for j in range(experts):
                block = jnp.einsum(
                    "kst,ktd->ksd", home_m[:, j, m], stack, preferred_element_type=f32
                ).astype(bf16)
                sent.append(across(block.reshape(stages * slots, width), j))
            return jnp.concatenate(sent)

        routed_rows[m] = dispatch(b_low)
        routed_grads[m] = dispatch(g_in[m])

    def collect(rows, m):
        rows = rows.reshape(experts, stages, slots, width)
        back = jnp.stack([across(rows[j], j) for j in range(experts)])
        summed = jnp.einsum(
            "kjst,jksd->ktd", home_m[:, :, m], back, preferred_element_type=f32
        )
        total = summed[0]
        for k in range(1, stages):
            total = total + along(summed[k].astype(bf16), -k).astype(f32)
        return total

    gate_grad = up_grad = down_grad = None
    router_m_grad = jnp.zeros((width, experts), f32)
    out_rows, d_bs = {}, {}
    for m in ORDER:
        rows, grads = routed_rows[m], routed_grads[m]
        gate, rest, turn = pair_gates(rows, router_m, other_m[:, :, m].reshape(-1))
        d_rows = (gate * grads.astype(f32)).astype(bf16)
        gate_pre, up_pre = mm(rows, gate_w), mm(rows, up_w)
        sigma = jax.nn.sigmoid(gate_pre)
        low = (gate_pre * sigma * up_pre).astype(bf16)
        result = mm(low, down_w)
        out_rows[m] = (gate * result).astype(bf16)
        d_gate_value = jnp.sum(grads.astype(f32) * result, axis=1, keepdims=True)
        d_logits = (gate * rest * d_gate_value) * turn
        d_low = mm_t(d_rows, down_w)
        d_gate = (d_low * up_pre * sigma * (1.0 + gate_pre * (1.0 - sigma))).astype(bf16)
        d_up = (d_low * gate_pre * sigma).astype(bf16)
        d_b = (
            mm_t(d_gate, gate_w)
            + mm_t(d_up, up_w)
            + exact(d_logits, router_m.astype(f32), ((1,), (1,)))
        ).astype(bf16)
        d_bs[m] = collect(d_b, m)
        router_m_grad = router_m_grad + exact(rows.astype(f32), d_logits, ((0,), (0,)))
        here = (t_mm(rows, d_gate), t_mm(rows, d_up), t_mm(low, d_rows))
        if gate_grad is None:
            gate_grad, up_grad, down_grad = here
        else:
            gate_grad, up_grad, down_grad = (
                gate_grad + here[0],
                up_grad + here[1],
                down_grad + here[2],
            )

    def stage_rows(grad):
        split = grad.reshape(stages, 2, width // dp_size, part)
        mine = pick(split, core, 1)
        other = partner(pick(split, 1 - core, 1).astype(bf16))
        total = (mine + other.astype(f32)).astype(bf16)
        got = jnp.stack([along(pick(total, (stage + k) % stages), k) for k in range(stages)])
        got = got[stage_order].astype(f32)
        return jnp.concatenate([got[s] for s in range(stages)], axis=1)[None]

    gate_share, up_share = stage_rows(gate_grad), stage_rows(up_grad)
    down_split = down_grad.reshape(2, part // 2, width)
    down_share = (
        pick(down_split, core) + partner(pick(down_split, 1 - core).astype(bf16)).astype(f32)
    )[None]

    outs = [None] * MICRO
    for m in ORDER:
        outs[m] = middles[m] + collect(out_rows[m], m)
    out_act = jnp.stack(outs)[None].astype(bf16)

    gain_2_grad = jnp.zeros((width,), f32)
    router_a_grad = jnp.zeros((width, experts), f32)
    d_middles, d_queries, d_attn, pair_back, kv_grads = {}, {}, {}, {}, []
    for m in ORDER:
        a_pairs, gate, rest, turn, q_cos, q_sin, q_pos, mixed, q_rot, peak, attn = kept[m]
        norm_grad, gain_part = norm_back(middles[m], inverses[m], gain_2, d_bs[m])
        gain_2_grad = gain_2_grad + gain_part
        d_middle = cotangent[0, m].astype(f32) + norm_grad
        d_middles[m] = d_middle
        sent = jnp.einsum(
            "kst,td->ksd", home_a[:, m], d_middle.astype(bf16), preferred_element_type=f32
        ).astype(bf16)
        got = jnp.concatenate([across(sent[k], k) for k in range(experts)]).astype(f32)
        d_attn[m] = (gate * got).astype(bf16)
        d_gate_value = jnp.sum(got * attn, axis=1, keepdims=True)
        d_logits = (gate * rest * d_gate_value) * turn
        d_mixed = mm_t(d_attn[m], o_full).astype(bf16)
        d_queries[m], *fresh = attend_back(
            q_rot, d_mixed, q_cos, q_sin, q_pos, kv_all[: m + 1], kv_grads[: m + 1], place, tokens
        )
        kv_grads = list(fresh) + list(kv_grads[m + 1 :])
        d_pair = mm_t(d_queries[m], q_full) + exact(
            d_logits, router_a.astype(f32), ((1,), (1,))
        )
        pair_back[m] = jnp.einsum(
            "kst,ksd->ktd",
            pick_a[:, m],
            d_pair.astype(bf16).reshape(experts, slots, width),
            preferred_element_type=f32,
        )
        router_a_grad = router_a_grad + exact(a_pairs.astype(f32), d_logits, ((0,), (0,)))

    def scattered(grad):
        return lax.psum_scatter(grad.astype(bf16), "dp", scatter_dimension=0, tiled=True)

    def both(fn):
        return fn(ORDER[0]) + fn(ORDER[1])

    o_share = scattered(both(lambda m: t_mm(kept[m][7], d_attn[m]))).astype(f32)[None]
    q_share = scattered(both(lambda m: t_mm(kept[m][0], d_queries[m]))).astype(f32)[None]

    kv_grad = jnp.zeros((width, 2 * group), f32)
    gain_1_grad = jnp.zeros((width,), f32)
    grad_x = [None] * MICRO
    for m in ORDER:
        d_kv = sum_kv_grads(
            [across(kv_grads[m][k], k) for k in range(experts)], key_cos[m], key_sin[m]
        )
        kv_grad = kv_grad + t_mm(a_all[m], d_kv)
        d_a = mm_t(d_kv, kv_cols).reshape(experts, tokens, width) + pair_back[m]
        total = d_a[0]
        for k in range(1, experts):
            total = total + across(d_a[k].astype(bf16), k).astype(f32)
        values = inputs[0, m].astype(f32)
        d_x, gain_part = norm_back(values, inverse_rms(values), gain_1, total)
        gain_1_grad = gain_1_grad + gain_part
        grad_x[m] = d_middles[m] + d_x
    grad_x = jnp.stack(grad_x)[None]
    kv_mine = scattered(kv_grad).reshape(experts, rows_each, 2 * group)
    kv_got = [across(pick(kv_mine, own ^ k), k) for k in range(experts)]
    kv_got = jnp.stack(kv_got)[xor_order].reshape(experts, rows_each, 2, group)
    kv_share = kv_got.transpose(1, 2, 0, 3).reshape(rows_each, 2 * inner).astype(f32)

    tail = jnp.concatenate(
        [router_a_grad, router_m_grad, gain_1_grad[:, None], gain_2_grad[:, None]], axis=1
    )
    tail = lax.psum_scatter(tail, "dp", scatter_dimension=0, tiled=True)
    tail = lax.psum_scatter(tail, "expert", scatter_dimension=0, tiled=True)
    router_share, gains_share = tail[:, : 2 * experts], tail[:, 2 * experts :]

    largest = jnp.maximum(kept[0][9], kept[1][9])[:, 0, :]
    hop = 1
    while hop < dp_size:
        largest = jnp.maximum(
            largest, lax.ppermute(largest, "dp", [(j, j ^ hop) for j in range(dp_size)])
        )
        hop *= 2
    largest = jnp.stack([across(largest, k) for k in range(experts)])
    ratio = logit_cap / jnp.maximum(largest, logit_cap)
    root_q = jnp.sqrt(ratio[0]).reshape(1, inner)
    root_k = jnp.sqrt(jnp.min(ratio, axis=0)).reshape(1, inner)
    clipped_q = (q_weight.astype(f32) * root_q[None]).astype(bf16)
    clipped_key = (kv_weight[:, :inner].astype(f32) * root_k).astype(bf16)
    return (
        out_act,
        grad_x,
        kv_share,
        router_share,
        gains_share,
        q_share,
        o_share,
        gate_share,
        up_share,
        down_share,
        clipped_q,
        clipped_key,
    )


def solution(mesh):
    tokens4 = P("dp", None, "expert", None)
    rows2 = P(("dp", "expert"), None)
    weights3 = P("expert", "dp", None)
    return jax.shard_map(
        per_device,
        mesh=mesh,
        in_specs=(tokens4,) * 3 + (P("dp"),) + (rows2,) * 3 + (weights3,) * 5 + (tokens4,),
        out_specs=(tokens4,) * 2 + (rows2,) * 3 + (weights3,) * 6 + (rows2,),
        check_vma=False,
    )
```

profile of v0, /device:TPU:0, one launch (start us, length us, event | category | flops | bytes accessed | tf_op | source)
XLA Modules:
  0.0 1757.3 jit_solution(10699657120446241827)
XLA Ops:
  66.8 136.3 %all-gather = bf16[32,13,128]{2,1,0:T(8,128)(2,1)S(1)} all-gather(bf16[4,13,128]{2,1,0:T(8,128)(2,1)S(1)} %all_gather.18), channel_id=2, replica_groups=mesh['dp'=8,'expert'=4] {'dp'}, dimensions={0}, use_global_device_ids=true | all-gather | bytes 119808 | tf_op jit(solution)/shard_map/all_gather | solution.py:333
  261.7 69.5 %collective-permute-done.23 = bf16[256,1408]{1,0:T(8,128)(2,1)} collective-permute-done((bf16[256,1408]{1,0:T(8,128)(2,1)}, bf16[256,1408]{1,0:T(8,128)(2,1)}, u32[]{:S(2)}, u32[]{:S(2)}) %collective-permute-start.23) | collective-permute-done | bytes 720928 | tf_op jit(solution)/shard_map/ppermute | solution.py:313
  400.4 22.6 %collective-permute-done.67 = bf16[128,2048]{1,0:T(8,128)(2,1)} collective-permute-done((bf16[128,2048]{1,0:T(8,128)(2,1)}, bf16[128,2048]{1,0:T(8,128)(2,1)}, u32[]{:S(2)}, u32[]{:S(2)}) %collective-permute-start.67) | collective-permute-done | bytes 524320 | tf_op jit(solution)/shard_map/ppermute | solution.py:313
  442.8 24.5 %collective-permute-done.52 = bf16[128,2048]{1,0:T(8,128)(2,1)} collective-permute-done((bf16[128,2048]{1,0:T(8,128)(2,1)}, bf16[128,2048]{1,0:T(8,128)(2,1)}, u32[]{:S(2)}, u32[]{:S(2)}) %collective-permute-start.52) | collective-permute-done | bytes 524320 | tf_op jit(solution)/shard_map/ppermute | solution.py:313
  494.6 22.5 %collective-permute-done.34 = bf16[2,512,512]{2,1,0:T(8,128)(2,1)S(1)} collective-permute-done((bf16[2,512,512]{2,1,0:T(8,128)(2,1)}, bf16[2,512,512]{2,1,0:T(8,128)(2,1)S(1)}, u32[]{:S(2)}, u32[]{:S(2)}) %collective-permute-start.34) | collective-permute-done | bytes 1048608 | tf_op jit(solution)/shard_map/ppermute | solution.py:308
  526.4 19.1 %attend.3 = (bf16[256,2048]{1,0:T(8,128)(2,1)}, bf16[256,2048]{1,0:T(8,128)(2,1)}, f32[16,8,128]{2,1,0:T(8,128)}) custom-call(s32[2]{0:T(128)} %pad_add_fusion.place_ref, f32[256,2048]{1,0:T(8,128)} %fusion.267.q_ref, f32[256,128]{1,0:T(8,128)} %bitcast.705, f32[256,128]{1,0:T(8,128)} %bitcast.707, s32[256,1]{1,0:T(8,128)} %reshape_squeeze.33.pos_ref, ...), custom_call_target="tpu_custom_call" | custom-call | tf_op jit(solution)/shard_map/attend/pallas_call | solution.py:184
  553.9 23.4 %collective-permute-start.38 = (bf16[64,2048]{1,0:T(8,128)(2,1)}, bf16[64,2048]{1,0:T(8,128)(2,1)}, u32[]{:S(2)}, u32[]{:S(2)}) collective-permute-start(bf16[64,2048]{1,0:T(8,128)(2,1)} %get-tuple-element.181), channel_id=1, source_target_pairs={{0,3},{1,2},{2,1},{3,0},{4,7},{5,6},{6,5},{7,4},{8,11},{9,10},{10,... | collective-permute-start | bytes 786440 | tf_op jit(solution)/shard_map/ppermute | solution.py:308
  641.8 32.8 %collective-permute-done.40 = bf16[128,2048]{1,0:T(8,128)(2,1)S(1)} collective-permute-done((bf16[128,2048]{1,0:T(8,128)(2,1)S(1)}, bf16[128,2048]{1,0:T(8,128)(2,1)S(1)}, u32[]{:S(2)}, u32[]{:S(2)}) %collective-permute-start.40) | collective-permute-done | bytes 524320 | tf_op jit(solution)/shard_map/ppermute | solution.py:313
  678.0 19.8 %collective-permute-done.13 = bf16[128,2048]{1,0:T(8,128)(2,1)S(1)} collective-permute-done((bf16[128,2048]{1,0:T(8,128)(2,1)S(1)}, bf16[128,2048]{1,0:T(8,128)(2,1)S(1)}, u32[]{:S(2)}, u32[]{:S(2)}) %collective-permute-start.13) | collective-permute-done | bytes 524320 | tf_op jit(solution)/shard_map/ppermute | solution.py:313
  753.7 17.7 %multiply_convert_fusion.2 = (bf16[1024,1408]{1,0:T(8,128)(2,1)}, bf16[1024,1408]{1,0:T(8,128)(2,1)}, bf16[1024,1408]{1,0:T(8,128)(2,1)}) fusion(f32[1024,1408]{1,0:T(8,128)} %fusion.284, f32[1024,1408]{1,0:T(8,128)} %fusion.283, bf16[704,2048]{1,0:T(8,128)(2,1)} %get-tuple-element.93, bf16[704,2048]{1,0:T(8,128)(2,1)} %get-tuple-element.92, ...), kind=kOutput, calls=%fused_computation.53 | convolution fusion | flops 5961154560 | bytes 30150656 | tf_op jit(solution)/shard_map/dot_general | solution.py:29
  843.3 17.7 %multiply_convert_fusion.4 = (bf16[1024,1408]{1,0:T(8,128)(2,1)}, bf16[1024,1408]{1,0:T(8,128)(2,1)}, bf16[1024,1408]{1,0:T(8,128)(2,1)}) fusion(f32[1024,1408]{1,0:T(8,128)} %fusion.288, f32[1024,1408]{1,0:T(8,128)} %fusion.287, bf16[704,2048]{1,0:T(8,128)(2,1)} %get-tuple-element.93, bf16[704,2048]{1,0:T(8,128)(2,1)} %get-tuple-element.92, ...), kind=kOutput, calls=%fused_computation.55 | convolution fusion | flops 5961154560 | bytes 30150656 | tf_op jit(solution)/shard_map/dot_general | solution.py:29
  958.8 20.6 %collective-permute-done.61 = bf16[128,2048]{1,0:T(8,128)(2,1)S(1)} collective-permute-done((bf16[128,2048]{1,0:T(8,128)(2,1)S(1)}, bf16[128,2048]{1,0:T(8,128)(2,1)S(1)}, u32[]{:S(2)}, u32[]{:S(2)}) %collective-permute-start.61) | collective-permute-done | bytes 524320 | tf_op jit(solution)/shard_map/ppermute | solution.py:313
  1001.0 26.0 %attend_back.2 = (bf16[256,2048]{1,0:T(8,128)(2,1)}, bf16[4,2,512,512]{3,2,1,0:T(8,128)(2,1)}, bf16[4,2,512,512]{3,2,1,0:T(8,128)(2,1)}) custom-call(s32[2]{0:T(128)} %pad_add_fusion.place_ref, bf16[256,2048]{1,0:T(8,128)(2,1)} %get-tuple-element.32.q_ref, bf16[256,2048]{1,0:T(8,128)(2,1)} %fusion.69.dm_ref, f32[256,128]{1,0:T(8,128)} %bitcast.706, ...), custom_call_target="tpu_custom_call" | custom-call | tf_op jit(solution)/shard_map/attend_back/pallas_call | solution.py:259
  1034.0 20.0 %attend_back.3 = (bf16[256,2048]{1,0:T(8,128)(2,1)}, bf16[4,2,512,512]{3,2,1,0:T(8,128)(2,1)}) custom-call(s32[2]{0:T(128)} %pad_add_fusion.place_ref, bf16[256,2048]{1,0:T(8,128)(2,1)} %get-tuple-element.31.q_ref, bf16[256,2048]{1,0:T(8,128)(2,1)} %fusion.66.dm_ref, f32[256,128]{1,0:T(8,128)} %bitcast.710, f32[256,128]{1,0:T(8,128)} %bitcast.712, ...), custom_call_target="tpu_custom_call" | custom-call | tf_op jit(solution)/shard_map/attend_back/pallas_call | solution.py:259
  1084.9 21.7 %collective-permute-done.82.refs_2_ = bf16[2,512,512]{2,1,0:T(8,128)(2,1)} collective-permute-done((bf16[2,512,512]{2,1,0:T(8,128)(2,1)S(1)}, bf16[2,512,512]{2,1,0:T(8,128)(2,1)}, u32[]{:S(2)}, u32[]{:S(2)}) %collective-permute-start.82) | collective-permute-done | bytes 1048608 | tf_op jit(solution)/shard_map/ppermute | solution.py:308
  1129.2 33.5 %collective-permute-done.88.refs_2_ = bf16[2,512,512]{2,1,0:T(8,128)(2,1)} collective-permute-done((bf16[2,512,512]{2,1,0:T(8,128)(2,1)}, bf16[2,512,512]{2,1,0:T(8,128)(2,1)}, u32[]{:S(2)}, u32[]{:S(2)}) %collective-permute-start.88) | collective-permute-done | bytes 1048608 | tf_op jit(solution)/shard_map/ppermute | solution.py:308
  1208.2 37.3 %reduce-scatter.10.cloned.1.call-done = f32[256,10]{0,1:T(8,128)} async-done(((f32[2048,10]{0,1:T(8,128)}), f32[256,10]{0,1:T(8,128)}) %reduce-scatter.10.cloned.1.call-update) | async-done | bytes 10256 | tf_op jit(solution)/shard_map/reduce_scatter | solution.py:609
  1460.4 26.1 %collective-permute-done.49 = bf16[128,2048]{1,0:T(8,128)(2,1)S(1)} collective-permute-done((bf16[128,2048]{1,0:T(8,128)(2,1)}, bf16[128,2048]{1,0:T(8,128)(2,1)S(1)}, u32[]{:S(2)}, u32[]{:S(2)}) %collective-permute-start.49) | collective-permute-done | bytes 524320 | tf_op jit(solution)/shard_map/ppermute | solution.py:313
  1487.2 25.0 %collective-permute-start.99 = (bf16[256,1408]{1,0:T(8,128)(2,1)S(1)}, bf16[256,1408]{1,0:T(8,128)(2,1)S(1)}, u32[]{:S(2)}, u32[]{:S(2)}) collective-permute-start(bf16[256,1408]{1,0:T(8,128)(2,1)S(1)} %get-tuple-element.131), channel_id=1, source_target_pairs={{0,24},{4,28},{8,0},{12,4},{16,8},{20,12},{24,16},{28,20},{1,25},{... | collective-permute-start | bytes 2162696 | tf_op jit(solution)/shard_map/ppermute | solution.py:313
  1512.2 25.7 %collective-permute-start.98 = (bf16[256,1408]{1,0:T(8,128)(2,1)S(1)}, bf16[256,1408]{1,0:T(8,128)(2,1)S(1)}, u32[]{:S(2)}, u32[]{:S(2)}) collective-permute-start(bf16[256,1408]{1,0:T(8,128)(2,1)S(1)} %get-tuple-element.132), channel_id=1, source_target_pairs={{0,16},{4,20},{8,24},{12,28},{16,0},{20,4},{24,8},{28,12},{1,17},{... | collective-permute-start | bytes 2162696 | tf_op jit(solution)/shard_map/ppermute | solution.py:313
  1540.8 48.1 %collective-permute-start.97 = (bf16[256,1408]{1,0:T(8,128)(2,1)S(1)}, bf16[256,1408]{1,0:T(8,128)(2,1)}, u32[]{:S(2)}, u32[]{:S(2)}) collective-permute-start(bf16[256,1408]{1,0:T(8,128)(2,1)S(1)} %get-tuple-element.133), channel_id=1, source_target_pairs={{0,8},{4,12},{8,16},{12,20},{16,24},{20,28},{24,0},{28,4},{1,9},{5... | collective-permute-start | bytes 2162696 | tf_op jit(solution)/shard_map/ppermute | solution.py:313
  1588.9 23.8 %collective-permute-start.103 = (bf16[256,1408]{1,0:T(8,128)(2,1)}, bf16[256,1408]{1,0:T(8,128)(2,1)}, u32[]{:S(2)}, u32[]{:S(2)}) collective-permute-start(bf16[256,1408]{1,0:T(8,128)(2,1)} %get-tuple-element.127), channel_id=1, source_target_pairs={{0,24},{4,28},{8,0},{12,4},{16,8},{20,12},{24,16},{28,20},{1,25},{... | collective-permute-start | bytes 2162696 | tf_op jit(solution)/shard_map/ppermute | solution.py:313
  1637.2 47.3 %collective-permute-done.98 = bf16[256,1408]{1,0:T(8,128)(2,1)S(1)} collective-permute-done((bf16[256,1408]{1,0:T(8,128)(2,1)S(1)}, bf16[256,1408]{1,0:T(8,128)(2,1)S(1)}, u32[]{:S(2)}, u32[]{:S(2)}) %collective-permute-start.98) | collective-permute-done | bytes 720928 | tf_op jit(solution)/shard_map/ppermute | solution.py:313
  1694.7 20.4 %collective-permute-done.102 = bf16[256,1408]{1,0:T(8,128)(2,1)} collective-permute-done((bf16[256,1408]{1,0:T(8,128)(2,1)}, bf16[256,1408]{1,0:T(8,128)(2,1)}, u32[]{:S(2)}, u32[]{:S(2)}) %collective-permute-start.102) | collective-permute-done | bytes 720928 | tf_op jit(solution)/shard_map/ppermute | solution.py:313
  (858 shorter events, 958.1 us)
Async XLA Ops:
  7.2 375.8 %all-gather.7.cloned.1.call-start = ((), (), s32[]{:S(2)}) async-start(), calls=%async_computation.5 | async-start | bytes 4718592 | tf_op jit(solution)/shard_map/all_gather | solution.py:355
  24.5 494.9 %all-gather.9.cloned.1.call-start = ((), (), s32[]{:S(2)}) async-start(), calls=%async_computation.10 | async-start | bytes 9437184 | tf_op jit(solution)/shard_map/all_gather | solution.py:356
  25.2 520.3 %all-gather.11.cloned.1.call-start = ((), (), s32[]{:S(2)}) async-start(), calls=%async_computation.11 | async-start | bytes 9437184 | tf_op jit(solution)/shard_map/all_gather | solution.py:357
  25.3 313.8 %collective-permute-start.2 = (bf16[2,128,2048]{2,1,0:T(8,128)(2,1)S(1)}, bf16[2,128,2048]{2,1,0:T(8,128)(2,1)S(1)}, u32[]{:S(2)}, u32[]{:S(2)}) collective-permute-start(bf16[2,128,2048]{2,1,0:T(8,128)(2,1)S(1)} %bitcast.652), channel_id=1, source_target_pairs={{0,3},{1,2},{2,1},{3,0},{4,7},{5,6},{6,5},{7,4},{8,11},{9,10},{10,... | collective-permute-start | bytes 3145736 | tf_op jit(solution)/shard_map/ppermute | solution.py:308
  43.3 190.2 %collective-permute-start.20 = (bf16[256,1408]{1,0:T(8,128)(2,1)}, bf16[256,1408]{1,0:T(8,128)(2,1)}, u32[]{:S(2)}, u32[]{:S(2)}) collective-permute-start(bf16[256,1408]{1,0:T(8,128)(2,1)} %bitcast.732), channel_id=1, source_target_pairs={{0,24},{4,28},{8,0},{12,4},{16,8},{20,12},{24,16},{28,20},{1,25},{... | collective-permute-start | bytes 2162696 | tf_op jit(solution)/shard_map/ppermute | solution.py:313
  49.4 185.9 %collective-permute-start.19 = (bf16[256,1408]{1,0:T(8,128)(2,1)}, bf16[256,1408]{1,0:T(8,128)(2,1)}, u32[]{:S(2)}, u32[]{:S(2)}) collective-permute-start(bf16[256,1408]{1,0:T(8,128)(2,1)} %bitcast.731), channel_id=1, source_target_pairs={{0,16},{4,20},{8,24},{12,28},{16,0},{20,4},{24,8},{28,12},{1,17},{... | collective-permute-start | bytes 2162696 | tf_op jit(solution)/shard_map/ppermute | solution.py:313
  51.7 185.2 %collective-permute-start.18 = (bf16[256,1408]{1,0:T(8,128)(2,1)}, bf16[256,1408]{1,0:T(8,128)(2,1)}, u32[]{:S(2)}, u32[]{:S(2)}) collective-permute-start(bf16[256,1408]{1,0:T(8,128)(2,1)} %bitcast.730), channel_id=1, source_target_pairs={{0,8},{4,12},{8,16},{12,20},{16,24},{20,28},{24,0},{28,4},{1,9},{5... | collective-permute-start | bytes 2162696 | tf_op jit(solution)/shard_map/ppermute | solution.py:313
  54.9 182.7 %collective-permute-start.24 = (bf16[256,1408]{1,0:T(8,128)(2,1)}, bf16[256,1408]{1,0:T(8,128)(2,1)}, u32[]{:S(2)}, u32[]{:S(2)}) collective-permute-start(bf16[256,1408]{1,0:T(8,128)(2,1)} %bitcast.729), channel_id=1, source_target_pairs={{0,24},{4,28},{8,0},{12,4},{16,8},{20,12},{24,16},{28,20},{1,25},{... | collective-permute-start | bytes 2162696 | tf_op jit(solution)/shard_map/ppermute | solution.py:313
  57.8 1187.8 %reduce-scatter.10.cloned.1.call-start = ((), (), s32[]{:S(2)}) async-start(), calls=%async_computation.7 | async-start | bytes 147456 | tf_op jit(solution)/shard_map/reduce_scatter | solution.py:609
  479.1 271.1 %collective-permute-start.71 = (bf16[256,2048]{1,0:T(8,128)(2,1)}, bf16[256,2048]{1,0:T(8,128)(2,1)}, u32[]{:S(2)}, u32[]{:S(2)}) collective-permute-start(bf16[256,2048]{1,0:T(8,128)(2,1)} %bitcast.189), channel_id=1, source_target_pairs={{0,3},{1,2},{2,1},{3,0},{4,7},{5,6},{6,5},{7,4},{8,11},{9,10},{10,... | collective-permute-start | bytes 3145736 | tf_op jit(solution)/shard_map/ppermute | solution.py:308
  481.6 269.8 %collective-permute-start.70 = (bf16[256,2048]{1,0:T(8,128)(2,1)}, bf16[256,2048]{1,0:T(8,128)(2,1)}, u32[]{:S(2)}, u32[]{:S(2)}) collective-permute-start(bf16[256,2048]{1,0:T(8,128)(2,1)} %bitcast.188), channel_id=1, source_target_pairs={{0,2},{1,3},{2,0},{3,1},{4,6},{5,7},{6,4},{7,5},{8,10},{9,11},{10,... | collective-permute-start | bytes 3145736 | tf_op jit(solution)/shard_map/ppermute | solution.py:308
  720.4 122.1 %collective-permute-start.56 = (bf16[256,2048]{1,0:T(8,128)(2,1)}, bf16[256,2048]{1,0:T(8,128)(2,1)}, u32[]{:S(2)}, u32[]{:S(2)}) collective-permute-start(bf16[256,2048]{1,0:T(8,128)(2,1)} %bitcast.162), channel_id=1, source_target_pairs={{0,3},{1,2},{2,1},{3,0},{4,7},{5,6},{6,5},{7,4},{8,11},{9,10},{10,... | collective-permute-start | bytes 3145736 | tf_op jit(solution)/shard_map/ppermute | solution.py:308
  724.6 118.7 %collective-permute-start.55 = (bf16[256,2048]{1,0:T(8,128)(2,1)}, bf16[256,2048]{1,0:T(8,128)(2,1)}, u32[]{:S(2)}, u32[]{:S(2)}) collective-permute-start(bf16[256,2048]{1,0:T(8,128)(2,1)} %bitcast.161), channel_id=1, source_target_pairs={{0,2},{1,3},{2,0},{3,1},{4,6},{5,7},{6,4},{7,5},{8,10},{9,11},{10,... | collective-permute-start | bytes 3145736 | tf_op jit(solution)/shard_map/ppermute | solution.py:308
  1200.3 434.0 %reduce-scatter.16.cloned.1.call-start = ((), (), s32[]{:S(2)}) async-start(), calls=%async_computation.12 | async-start | bytes 163840
  1247.0 483.8 %reduce-scatter.8.cloned.1.call-start = ((), (), s32[]{:S(2)}) async-start(), calls=%async_computation.6 | async-start | bytes 4718592 | tf_op jit(solution)/shard_map/reduce_scatter | solution.py:576
  1256.0 488.7 %reduce-scatter.12.cloned.1.call-start = ((), (), s32[]{:S(2)}) async-start(), calls=%async_computation.8 | async-start | bytes 9437184 | tf_op jit(solution)/shard_map/reduce_scatter | solution.py:576
  1277.0 470.4 %reduce-scatter.14.cloned.1.call-start = ((), (), s32[]{:S(2)}) async-start(), calls=%async_computation.9 | async-start | bytes 9437184 | tf_op jit(solution)/shard_map/reduce_scatter | solution.py:576
  1303.0 107.1 %collective-permute-start.46 = (bf16[4,64,2048]{2,1,0:T(8,128)(2,1)}, bf16[4,64,2048]{2,1,0:T(8,128)(2,1)}, u32[]{:S(2)}, u32[]{:S(2)}) collective-permute-start(bf16[4,64,2048]{2,1,0:T(8,128)(2,1)} %bitcast.143), channel_id=1, source_target_pairs={{0,2},{1,3},{2,0},{3,1},{4,6},{5,7},{6,4},{7,5},{8,10},{9,11},{10,... | collective-permute-start | bytes 3145736 | tf_op jit(solution)/shard_map/ppermute | solution.py:308
  1303.6 107.4 %collective-permute-start.45 = (bf16[4,64,2048]{2,1,0:T(8,128)(2,1)}, bf16[4,64,2048]{2,1,0:T(8,128)(2,1)}, u32[]{:S(2)}, u32[]{:S(2)}) collective-permute-start(bf16[4,64,2048]{2,1,0:T(8,128)(2,1)} %bitcast.141), channel_id=1, source_target_pairs={{0,1},{1,0},{2,3},{3,2},{4,5},{5,4},{6,7},{7,6},{8,9},{9,8},{10,11... | collective-permute-start | bytes 3145736 | tf_op jit(solution)/shard_map/ppermute | solution.py:308
  1447.5 141.5 %collective-permute-start.31 = (bf16[128,2048]{1,0:T(8,128)(2,1)S(1)}, bf16[128,2048]{1,0:T(8,128)(2,1)S(1)}, u32[]{:S(2)}, u32[]{:S(2)}) collective-permute-start(bf16[128,2048]{1,0:T(8,128)(2,1)S(1)} %copy-done.62), channel_id=1, source_target_pairs={{0,16},{4,20},{8,24},{12,28},{16,0},{20,4},{24,8},{28,12},{1,17},{... | collective-permute-start | bytes 1572872 | tf_op jit(solution)/shard_map/ppermute | solution.py:313
  1458.8 153.9 %collective-permute-start.30 = (bf16[128,2048]{1,0:T(8,128)(2,1)S(1)}, bf16[128,2048]{1,0:T(8,128)(2,1)S(1)}, u32[]{:S(2)}, u32[]{:S(2)}) collective-permute-start(bf16[128,2048]{1,0:T(8,128)(2,1)S(1)} %copy-done.61), channel_id=1, source_target_pairs={{0,24},{4,28},{8,0},{12,4},{16,8},{20,12},{24,16},{28,20},{1,25},{... | collective-permute-start | bytes 1572872 | tf_op jit(solution)/shard_map/ppermute | solution.py:313
  1487.2 127.8 %collective-permute-start.99 = (bf16[256,1408]{1,0:T(8,128)(2,1)S(1)}, bf16[256,1408]{1,0:T(8,128)(2,1)S(1)}, u32[]{:S(2)}, u32[]{:S(2)}) collective-permute-start(bf16[256,1408]{1,0:T(8,128)(2,1)S(1)} %get-tuple-element.131), channel_id=1, source_target_pairs={{0,24},{4,28},{8,0},{12,4},{16,8},{20,12},{24,16},{28,20},{1,25},{... | collective-permute-start | bytes 2162696 | tf_op jit(solution)/shard_map/ppermute | solution.py:313
  1512.2 172.3 %collective-permute-start.98 = (bf16[256,1408]{1,0:T(8,128)(2,1)S(1)}, bf16[256,1408]{1,0:T(8,128)(2,1)S(1)}, u32[]{:S(2)}, u32[]{:S(2)}) collective-permute-start(bf16[256,1408]{1,0:T(8,128)(2,1)S(1)} %get-tuple-element.132), channel_id=1, source_target_pairs={{0,16},{4,20},{8,24},{12,28},{16,0},{20,4},{24,8},{28,12},{1,17},{... | collective-permute-start | bytes 2162696 | tf_op jit(solution)/shard_map/ppermute | solution.py:313
  1540.8 143.8 %collective-permute-start.97 = (bf16[256,1408]{1,0:T(8,128)(2,1)S(1)}, bf16[256,1408]{1,0:T(8,128)(2,1)}, u32[]{:S(2)}, u32[]{:S(2)}) collective-permute-start(bf16[256,1408]{1,0:T(8,128)(2,1)S(1)} %get-tuple-element.133), channel_id=1, source_target_pairs={{0,8},{4,12},{8,16},{12,20},{16,24},{20,28},{24,0},{28,4},{1,9},{5... | collective-permute-start | bytes 2162696 | tf_op jit(solution)/shard_map/ppermute | solution.py:313
  (262 other events, 10551.0 us)
Sparse Core Ops, SparseCore 0:
  24.6 63.0 all-gather.6
  89.3 128.7 all-gather.8
  219.6 126.9 all-gather.10
  1200.4 45.1 reduce-scatter.9
  1248.3 21.9 reduce-scatter.15
  1272.5 50.1 reduce-scatter.7
  1325.0 87.9 reduce-scatter.11
  1415.3 190.3 reduce-scatter.13
where the time goes:
time: 1770 us; the launch traced here: 1760 us
  waiting for transfers between devices  536 us (30%)
  matrix products  407 us (23%)
  starting transfers between devices  315 us (18%)
  blocking collectives  144 us (8%)
  local copies, waits for them, and re-layouts  131 us (7%)
  other arithmetic  103 us (6%)
  Pallas kernels  103 us (6%)
  between operations  17.7 us (1%)
    ppermute x36, waiting for transfers between devices, along(): lax.ppermute(block, 'dp', [(j, (j // 2 + k) % stages * 2 + j % 2) for j i...  301 us
    ppermute x36, starting transfers between devices, along(): lax.ppermute(block, 'dp', [(j, (j // 2 + k) % stages * 2 + j % 2) for j i...  215 us
    ppermute x66, waiting for transfers between devices, across(): return lax.ppermute(block, 'expert', [(j, j ^ k) for j in range(experts)])  186 us
    all_gather x1, blocking collectives, per_device(): lax.all_gather(lax.all_gather(small, 'expert', axis=0), 'dp', axis=0)  136 us
    dot_general x12, matrix products, t_mm(): lax.dot_general(left, right, (((0,), (0,)), ((), ())), preferred_element_...  126 us
    dot_general x14, matrix products, mm(): return jnp.dot(left, right, preferred_element_type=f32)  104 us
    dot_general x12, matrix products, mm_t(): lax.dot_general(left, right, (((1,), (1,)), ((), ())), preferred_element_...  101 us
    ppermute x66, starting transfers between devices, across(): return lax.ppermute(block, 'expert', [(j, j ^ k) for j in range(experts)])  98.7 us
  transfers between devices with their start and end apart: 119, of which 46 were waited for; matrix products, arithmetic and copies ran while one was open for 34% of the time, Pallas kernels for 5%

commit v1 on v0

v1 whole, which is shorter than its diff:
```python
import math

import jax
import jax.numpy as jnp
from jax import lax
from jax.experimental import pallas as pl
from jax.experimental.pallas import tpu as pltpu
from jax.sharding import PartitionSpec as P

HEADS = 16
HSZ = 128
TOPK = 2
PIC = 256
MICRO = 2
ORDER = (1, 0)

norm_eps = 1e-06
logit_cap = 8.0
masked_low = -1e30
bf16 = jnp.bfloat16
f32 = jnp.float32


def mm(left, right):
    return jnp.dot(left, right, preferred_element_type=f32)


def mm_t(left, right):
    return lax.dot_general(left, right, (((1,), (1,)), ((), ())), preferred_element_type=f32)


def t_mm(left, right):
    return lax.dot_general(left, right, (((0,), (0,)), ((), ())), preferred_element_type=f32)


def rope_tables(positions):
    half = HSZ // 2
    freq = jnp.exp(jnp.arange(half, dtype=f32) * (-math.log(10000.0) / half))
    angles = positions.astype(f32)[..., None] * freq
    cosine, sine = jnp.cos(angles), jnp.sin(angles)
    return (
        jnp.concatenate([cosine, cosine], axis=-1),
        jnp.concatenate([-sine, sine], axis=-1),
    )


def inverse_rms(values):
    return lax.rsqrt(jnp.mean(values * values, axis=-1, keepdims=True) + norm_eps)


def selection(hot, slots):
    tokens = hot.shape[-1]
    before = jnp.triu(jnp.ones((tokens, tokens), bf16), 1)
    rank = jnp.dot(hot.astype(bf16), before, preferred_element_type=f32)
    slot = jnp.arange(slots, dtype=jnp.int32)[:, None]
    taken = (rank.astype(jnp.int32)[..., None, :] == slot) & (hot[..., None, :] > 0)
    return taken.astype(bf16)


def full_spec(shape):
    return pl.BlockSpec(shape, lambda *_: (0,) * len(shape))


def work(flops, moved, exps=0):
    return pl.CostEstimate(flops=flops, bytes_accessed=moved, transcendentals=exps)


def kv_kernel(a_ref, w_ref, cos_ref, sin_ref, o_ref):
    got = jnp.dot(a_ref[0], w_ref[...], preferred_element_type=f32)
    cosine, sine = cos_ref[0, 0], sin_ref[0, 0]
    for part in range(got.shape[1] // HSZ):
        piece = got[:, part * HSZ : (part + 1) * HSZ]
        turned = piece * cosine + pltpu.roll(piece, HSZ // 2, 1) * sine
        o_ref[0, 0, :, part * HSZ : (part + 1) * HSZ] = turned.astype(bf16)


def project_kv(a_all, kv_cols, cosine, sine):
    micro, rows, width = a_all.shape
    group = kv_cols.shape[1] // 2
    step = min(256, group)
    per = group // step
    table = pl.BlockSpec((1, 1, rows, HSZ), lambda m, g: (m, g // per, 0, 0))
    return pl.pallas_call(
        kv_kernel,
        grid=(micro, 2 * per),
        in_specs=[
            pl.BlockSpec((1, rows, width), lambda m, g: (m, 0, 0)),
            pl.BlockSpec((width, step), lambda m, g: (0, g)),
            table,
            table,
        ],
        out_specs=pl.BlockSpec((1, 1, rows, step), lambda m, g: (m, g // per, 0, g % per)),
        out_shape=jax.ShapeDtypeStruct((micro, 2, rows, group), bf16),
        name="project_kv",
        cost_estimate=work(4 * micro * rows * width * group, 2 * (micro * rows * width + 2 * width * group + 2 * micro * rows * group)),
    )(a_all, kv_cols, cosine, sine)


def probabilities(query, keys, start, qpos, micro):
    parts = []
    for m in range(micro + 1):
        got = lax.dot_general(
            query, keys[m], (((1,), (1,)), ((), ())), preferred_element_type=f32
        ) * (HSZ**-0.5)
        if m == micro:
            kpos = micro * got.shape[1] + lax.broadcasted_iota(jnp.int32, got.shape, 1)
            inside_q = (qpos >= start) & (qpos < start + PIC)
            inside_k = (kpos >= start) & (kpos < start + PIC)
            keep = (kpos <= qpos) | (inside_q & inside_k)
            got = jnp.where(keep, got, masked_low)
        parts.append(got)
    peak = parts[0].max(axis=1, keepdims=True)
    for got in parts[1:]:
        peak = jnp.maximum(peak, got.max(axis=1, keepdims=True))
    lifted = [jnp.exp(got - peak) for got in parts]
    total = lifted[0].sum(axis=1, keepdims=True)
    for got in lifted[1:]:
        total = total + got.sum(axis=1, keepdims=True)
    scale = 1.0 / total
    return [got * scale for got in lifted], peak


def project_q(a_pairs, q_full, cosine, sine, micro, experts):
    total, width = a_pairs.shape
    inner = q_full.shape[1]
    group = inner // experts
    step = min(256, group)
    per = group // step
    rows = total // micro

    def kernel(a_ref, w_ref, cos_ref, sin_ref, o_ref):
        got = jnp.dot(a_ref[...], w_ref[...], preferred_element_type=f32)
        for h in range(step // HSZ):
            lanes = slice(h * HSZ, (h + 1) * HSZ)
            piece = got[:, lanes]
            turned = piece * cos_ref[...] + pltpu.roll(piece, HSZ // 2, 1) * sin_ref[...]
            o_ref[:, 0, :, lanes] = turned.astype(bf16).reshape(micro, rows, HSZ)

    return pl.pallas_call(
        kernel,
        grid=(inner // step,),
        in_specs=[
            full_spec((total, width)),
            pl.BlockSpec((width, step), lambda g: (0, g)),
            full_spec((total, HSZ)),
            full_spec((total, HSZ)),
        ],
        out_specs=pl.BlockSpec((micro, 1, rows, step), lambda g: (0, g // per, 0, g % per)),
        out_shape=jax.ShapeDtypeStruct((micro, experts, rows, group), bf16),
        name="project_q",
        cost_estimate=work(2 * total * width * inner, 2 * (total * width + width * inner + total * inner)),
    )(a_pairs, q_full, cosine, sine)


def attend(query, qpos, kvs, start):
    micro = len(kvs) - 1
    experts, rows, group = query.shape
    hg = group // HSZ
    keys_seen = sum(kv.shape[1] for kv in kvs)

    def kernel(start_ref, q_ref, pos_ref, *rest):
        kv_refs, (mixed_ref, peak_ref) = rest[:-2], rest[-2:]
        for h in range(hg):
            lanes = slice(h * HSZ, (h + 1) * HSZ)
            probs, peak = probabilities(
                q_ref[0, :, lanes],
                [r[0, :, lanes] for r in kv_refs],
                start_ref[0],
                pos_ref[0],
                micro,
            )
            mixed = jnp.zeros((rows, HSZ), f32)
            for m in range(micro + 1):
                mixed = mixed + jnp.dot(
                    probs[m].astype(bf16), kv_refs[m][1, :, lanes], preferred_element_type=f32
                )
            mixed_ref[0, :, lanes] = mixed.astype(bf16)
            peak_ref[0, h] = jnp.full(peak_ref.shape[2:], jnp.max(peak), f32)

    return pl.pallas_call(
        kernel,
        grid_spec=pltpu.PrefetchScalarGridSpec(
            num_scalar_prefetch=1,
            grid=(experts,),
            in_specs=[
                pl.BlockSpec((1, rows, group), lambda g, s: (g, 0, 0)),
                pl.BlockSpec((1, rows, 1), lambda g, s: (g, 0, 0)),
            ]
            + [full_spec(kv.shape) for kv in kvs],
            out_specs=[
                pl.BlockSpec((1, rows, group), lambda g, s: (g, 0, 0)),
                pl.BlockSpec((1, hg, 8, 128), lambda g, s: (g, 0, 0, 0)),
            ],
        ),
        out_shape=[
            jax.ShapeDtypeStruct((experts, rows, group), bf16),
            jax.ShapeDtypeStruct((experts, hg, 8, 128), f32),
        ],
        name="attend",
        cost_estimate=work(4 * experts * rows * group * keys_seen, 4 * experts * rows * group, experts * rows * hg * keys_seen),
    )(start, query, qpos, *kvs)


def attend_back(query, d_mixed, cosine, sine, qpos, kvs, key_cos, key_sin, later, start):
    micro = len(kvs) - 1
    experts, rows, group = query.shape
    keys = kvs[0].shape[1]
    hg = group // HSZ
    held = len(later)

    def kernel(start_ref, q_ref, dm_ref, cos_ref, sin_ref, pos_ref, kcos_ref, ksin_ref, *rest):
        kv_refs = rest[: micro + 1]
        later_refs = rest[micro + 1 : micro + 1 + held]
        dq_ref, dkv_ref = rest[micro + 1 + held : micro + 3 + held]
        sums = rest[micro + 3 + held :]
        step = pl.program_id(0)

        @pl.when(step == 0)
        def _():
            for m in range(micro + 1):
                if held and m == micro:
                    sums[m][...] = later_refs[0][...]
                else:
                    sums[m][...] = jnp.zeros(sums[m].shape, f32)

        for h in range(hg):
            lanes = slice(h * HSZ, (h + 1) * HSZ)
            q, dm = q_ref[0, :, lanes], dm_ref[0, :, lanes]
            probs, _ = probabilities(
                q, [r[0, :, lanes] for r in kv_refs], start_ref[0], pos_ref[0], micro
            )
            d_probs = [
                lax.dot_general(
                    dm, r[1, :, lanes], (((1,), (1,)), ((), ())), preferred_element_type=f32
                )
                for r in kv_refs
            ]
            total = jnp.sum(d_probs[0] * probs[0], axis=1, keepdims=True)
            for m in range(1, micro + 1):
                total = total + jnp.sum(d_probs[m] * probs[m], axis=1, keepdims=True)
            d_q = jnp.zeros((rows, HSZ), f32)
            for m in range(micro + 1):
                d_scores = (probs[m] * (d_probs[m] - total)).astype(bf16)
                d_q = d_q + jnp.dot(d_scores, kv_refs[m][0, :, lanes], preferred_element_type=f32)
                sums[m][0, :, lanes] += lax.dot_general(
                    d_scores, q, (((0,), (0,)), ((), ())), preferred_element_type=f32
                )
                sums[m][1, :, lanes] += lax.dot_general(
                    probs[m].astype(bf16), dm, (((0,), (0,)), ((), ())), preferred_element_type=f32
                )
            d_q = d_q * (HSZ**-0.5)
            back = d_q * cos_ref[0] - pltpu.roll(d_q, HSZ // 2, 1) * sin_ref[0]
            dq_ref[0, :, lanes] = back.astype(bf16)

        @pl.when(step == experts - 1)
        def _():
            for h in range(hg):
                lanes = slice(h * HSZ, (h + 1) * HSZ)
                d_k = sums[micro][0, :, lanes] * (HSZ**-0.5)
                back = d_k * kcos_ref[...] - pltpu.roll(d_k, HSZ // 2, 1) * ksin_ref[...]
                dkv_ref[:, lanes] = back.astype(bf16)
                dkv_ref[:, group + h * HSZ : group + (h + 1) * HSZ] = sums[micro][
                    1, :, lanes
                ].astype(bf16)

    block = pl.BlockSpec((1, rows, group), lambda g, s: (g, 0, 0))
    table = pl.BlockSpec((1, rows, HSZ), lambda g, s: (g, 0, 0))
    sums_shape = jax.ShapeDtypeStruct((2, keys, group), f32)
    return pl.pallas_call(
        kernel,
        grid_spec=pltpu.PrefetchScalarGridSpec(
            num_scalar_prefetch=1,
            grid=(experts,),
            in_specs=[block, block, table, table]
            + [pl.BlockSpec((1, rows, 1), lambda g, s: (g, 0, 0))]
            + [full_spec((keys, HSZ))] * 2
            + [full_spec((2, keys, group))] * (micro + 1 + held),
            out_specs=[block, full_spec((keys, 2 * group))]
            + [full_spec((2, keys, group))] * micro,
            scratch_shapes=[pltpu.VMEM((2, keys, group), f32)],
        ),
        out_shape=[
            jax.ShapeDtypeStruct((experts, rows, group), bf16),
            jax.ShapeDtypeStruct((keys, 2 * group), bf16),
        ]
        + [sums_shape] * micro,
        name="attend_back",
        cost_estimate=work(10 * experts * rows * group * keys * (micro + 1), 12 * experts * rows * group, experts * rows * hg * keys * (micro + 1)),
    )(start, query, d_mixed, cosine, sine, qpos, key_cos, key_sin, *kvs, *later)


def join_groups(got_ref, flat_ref):
    experts, _, group = got_ref.shape
    for e in range(experts):
        flat_ref[:, e * group : (e + 1) * group] = got_ref[e]


def project_o(mixed, o_full, gate):
    experts, rows, group = mixed.shape
    inner, width = o_full.shape
    step = min(512, width)

    def kernel(mixed_ref, o_ref, gate_ref, attn_ref, gated_ref, flat_ref):
        @pl.when(pl.program_id(0) == 0)
        def _():
            join_groups(mixed_ref, flat_ref)

        got = jnp.dot(flat_ref[...], o_ref[...], preferred_element_type=f32)
        attn_ref[...] = got.astype(bf16)
        gated_ref[...] = (got * gate_ref[...]).astype(bf16)

    column = pl.BlockSpec((rows, step), lambda g: (0, g))
    return pl.pallas_call(
        kernel,
        grid=(width // step,),
        in_specs=[
            full_spec(mixed.shape),
            pl.BlockSpec((inner, step), lambda g: (0, g)),
            full_spec((rows, 1)),
        ],
        out_specs=[column, column, full_spec((rows, inner))],
        out_shape=[
            jax.ShapeDtypeStruct((rows, width), bf16),
            jax.ShapeDtypeStruct((rows, width), bf16),
            jax.ShapeDtypeStruct((rows, inner), bf16),
        ],
        name="project_o",
        cost_estimate=work(2 * rows * inner * width, 2 * (inner * width + 4 * rows * width)),
    )(mixed, o_full, gate)


def back_o(got, attn, gate, rest, turn, o_full, experts):
    rows, width = got.shape
    inner = o_full.shape[0]
    group = inner // experts
    lanes = turn.shape[1]

    def kernel(got_ref, attn_ref, gate_ref, rest_ref, turn_ref, o_ref, da_ref, dm_ref, dl_ref):
        @pl.when(pl.program_id(0) == 0)
        def _():
            upstream = got_ref[...].astype(f32)
            da_ref[...] = (gate_ref[...] * upstream).astype(bf16)
            value = jnp.sum(upstream * attn_ref[...].astype(f32), axis=1, keepdims=True)
            d_logits = (gate_ref[...] * rest_ref[...] * value) * turn_ref[...]
            high = d_logits.astype(bf16)
            dl_ref[:, :lanes] = high
            dl_ref[:, lanes:] = (d_logits - high.astype(f32)).astype(bf16)

        dm_ref[0] = lax.dot_general(
            da_ref[...], o_ref[...], (((1,), (1,)), ((), ())), preferred_element_type=f32
        ).astype(bf16)

    return pl.pallas_call(
        kernel,
        grid=(experts,),
        in_specs=[full_spec((rows, width))] * 2
        + [full_spec((rows, 1))] * 2
        + [full_spec((rows, lanes)), pl.BlockSpec((group, width), lambda g: (g, 0))],
        out_specs=[
            full_spec((rows, width)),
            pl.BlockSpec((1, rows, group), lambda g: (g, 0, 0)),
            full_spec((rows, 2 * lanes)),
        ],
        out_shape=[
            jax.ShapeDtypeStruct((rows, width), bf16),
            jax.ShapeDtypeStruct((experts, rows, group), bf16),
            jax.ShapeDtypeStruct((rows, 2 * lanes), bf16),
        ],
        name="back_o",
        cost_estimate=work(2 * rows * inner * width, 2 * (inner * width + 4 * rows * width)),
    )(got, attn, gate, rest, turn, o_full)


def back_q(d_query, q_full, d_logits, router):
    experts, rows, group = d_query.shape
    width, inner = q_full.shape
    step = min(512, width)
    lanes = router.shape[1]

    def kernel(dq_ref, q_ref, dl_ref, router_ref, pair_ref, flat_ref):
        @pl.when(pl.program_id(0) == 0)
        def _():
            join_groups(dq_ref, flat_ref)

        dims = (((1,), (1,)), ((), ()))
        got = lax.dot_general(flat_ref[...], q_ref[...], dims, preferred_element_type=f32)
        for half in range(2):
            got = got + lax.dot_general(
                dl_ref[:, half * lanes : (half + 1) * lanes],
                router_ref[...],
                dims,
                preferred_element_type=f32,
            )
        pair_ref[...] = got.astype(bf16)

    return pl.pallas_call(
        kernel,
        grid=(width // step,),
        in_specs=[
            full_spec(d_query.shape),
            pl.BlockSpec((step, inner), lambda g: (g, 0)),
            full_spec((rows, 2 * lanes)),
            pl.BlockSpec((step, lanes), lambda g: (g, 0)),
        ],
        out_specs=[pl.BlockSpec((rows, step), lambda g: (0, g)), full_spec((rows, inner))],
        out_shape=[
            jax.ShapeDtypeStruct((rows, width), bf16),
            jax.ShapeDtypeStruct((rows, inner), bf16),
        ],
        name="back_q",
        cost_estimate=work(2 * rows * inner * width, 2 * (inner * width + 4 * rows * width)),
    )(d_query, q_full, d_logits, router)


def token_back(d_kv, kv_cols, d_pair, pick):
    span, line = d_kv.shape
    width = kv_cols.shape[0]
    experts, slots, tokens = pick.shape
    step = min(512, width)

    def kernel(dkv_ref, kv_ref, pair_ref, pick_ref, o_ref):
        got = lax.dot_general(
            dkv_ref[...], kv_ref[...], (((1,), (1,)), ((), ())), preferred_element_type=f32
        )
        for e in range(experts):
            extra = lax.dot_general(
                pick_ref[e],
                pair_ref[e * slots : (e + 1) * slots, :],
                (((0,), (0,)), ((), ())),
                preferred_element_type=f32,
            )
            o_ref[e] = (got[e * tokens : (e + 1) * tokens] + extra).astype(bf16)

    return pl.pallas_call(
        kernel,
        grid=(width // step,),
        in_specs=[
            full_spec((span, line)),
            pl.BlockSpec((step, line), lambda g: (g, 0)),
            pl.BlockSpec((experts * slots, step), lambda g: (0, g)),
            full_spec(pick.shape),
        ],
        out_specs=pl.BlockSpec((experts, tokens, step), lambda g: (0, 0, g)),
        out_shape=jax.ShapeDtypeStruct((experts, tokens, width), bf16),
        name="token_back",
        cost_estimate=work(2 * span * line * width, 2 * (line * width + 2 * span * width)),
    )(d_kv, kv_cols, d_pair, pick)


def input_back_kernel(got_ref, x_ref, gain_ref, dm_ref, gx_ref, dg_ref):
    d_a = got_ref[0].astype(f32)
    for e in range(1, got_ref.shape[0]):
        d_a = d_a + got_ref[e].astype(f32)
    x = x_ref[...].astype(f32)
    inverse = lax.rsqrt(jnp.mean(x * x, axis=1, keepdims=True) + norm_eps)
    scaled = d_a * gain_ref[...]
    dg_ref[...] = jnp.sum(d_a * (x * inverse), axis=0, keepdims=True)
    mean = jnp.mean(scaled * x, axis=1, keepdims=True)
    gx_ref[...] = dm_ref[...] + (inverse * scaled - x * (inverse * inverse * inverse * mean))


def input_back(got, x, gain, d_middle):
    tokens, width = x.shape
    return pl.pallas_call(
        input_back_kernel,
        out_shape=[
            jax.ShapeDtypeStruct((tokens, width), f32),
            jax.ShapeDtypeStruct((1, width), f32),
        ],
        name="input_back",
        cost_estimate=work(10 * tokens * width, 20 * tokens * width),
    )(got, x, gain, d_middle)


def combine_kernel(back_ref, pick_ref, x_ref, gain_ref, middle_ref, inv_ref, b_ref):
    summed = lax.dot_general(
        pick_ref[...], back_ref[...], (((0,), (0,)), ((), ())), preferred_element_type=f32
    )
    middle = x_ref[...].astype(f32) + summed
    inverse = lax.rsqrt(jnp.mean(middle * middle, axis=1, keepdims=True) + norm_eps)
    middle_ref[...] = middle
    inv_ref[...] = inverse
    b_ref[...] = (middle * inverse * gain_ref[...]).astype(bf16)


def combine(back, pick, x, gain):
    tokens, width = x.shape
    return pl.pallas_call(
        combine_kernel,
        out_shape=[
            jax.ShapeDtypeStruct((tokens, width), f32),
            jax.ShapeDtypeStruct((tokens, 1), f32),
            jax.ShapeDtypeStruct((tokens, width), bf16),
        ],
        name="combine",
        cost_estimate=work(2 * back.shape[0] * tokens * width, 2 * back.shape[0] * width + 8 * tokens * width),
    )(back, pick, x, gain)


def middle_back_kernel(*refs):
    pieces = refs[:-8]
    middle_ref, inv_ref, cot_ref, gain_ref, pick_ref, dm_ref, dg_ref, rows_ref = refs[-8:]
    d_b = pieces[0][...].astype(f32)
    for piece in pieces[1:]:
        d_b = d_b + piece[...].astype(f32)
    middle, inverse = middle_ref[...], inv_ref[...]
    scaled = d_b * gain_ref[...]
    dg_ref[...] = jnp.sum(d_b * (middle * inverse), axis=0, keepdims=True)
    mean = jnp.mean(scaled * middle, axis=1, keepdims=True)
    d_middle = cot_ref[...].astype(f32) + (
        inverse * scaled - middle * (inverse * inverse * inverse * mean)
    )
    dm_ref[...] = d_middle
    rows_ref[...] = jnp.dot(
        pick_ref[...], d_middle.astype(bf16), preferred_element_type=f32
    ).astype(bf16)


def middle_back(pieces, middle, inverse, cot, gain, pick):
    tokens, width = middle.shape
    return pl.pallas_call(
        middle_back_kernel,
        out_shape=[
            jax.ShapeDtypeStruct((tokens, width), f32),
            jax.ShapeDtypeStruct((1, width), f32),
            jax.ShapeDtypeStruct((pick.shape[0], width), bf16),
        ],
        name="middle_back",
        cost_estimate=work(2 * pick.shape[0] * tokens * width, 2 * pick.shape[0] * width + 20 * tokens * width),
    )(*pieces, middle, inverse, cot, gain, pick)


def dispatch(blocks, pick):
    stages, pairs, tokens = pick.shape
    width = blocks[0].shape[1]
    step = min(512, width)

    def kernel(pick_ref, *refs):
        for k in range(stages):
            refs[-1][:, k] = (
                jnp.dot(pick_ref[k], refs[k][...], preferred_element_type=f32)
                .astype(bf16)
                .reshape(refs[-1].shape[0], refs[-1].shape[2], step)
            )

    return lambda experts: pl.pallas_call(
        kernel,
        grid=(width // step,),
        in_specs=[full_spec(pick.shape)]
        + [pl.BlockSpec((tokens, step), lambda g: (0, g)) for _ in blocks],
        out_specs=pl.BlockSpec((experts, stages, pairs // experts, step), lambda g: (0, 0, 0, g)),
        out_shape=jax.ShapeDtypeStruct((experts, stages, pairs // experts, width), bf16),
        name="dispatch",
        cost_estimate=work(2 * stages * pairs * tokens * width, 2 * stages * (pairs + tokens) * width),
    )(pick, *blocks)


def collect(rows, pick, order):
    experts, stages, slots, width = rows.shape
    tokens = pick.shape[2]

    def kernel(order_ref, pick_ref, rows_ref, o_ref):
        gathered = rows_ref[...].reshape(experts * slots, width)
        o_ref[0] = lax.dot_general(
            pick_ref[0], gathered, (((0,), (0,)), ((), ())), preferred_element_type=f32
        ).astype(bf16)

    return pl.pallas_call(
        kernel,
        grid_spec=pltpu.PrefetchScalarGridSpec(
            num_scalar_prefetch=1,
            grid=(stages,),
            in_specs=[
                pl.BlockSpec((1, experts * slots, tokens), lambda k, o: (k, 0, 0)),
                pl.BlockSpec((experts, 1, slots, width), lambda k, o: (0, k, 0, 0)),
            ],
            out_specs=pl.BlockSpec((1, tokens, width), lambda k, o: (o[k], 0, 0)),
        ),
        out_shape=jax.ShapeDtypeStruct((stages, tokens, width), bf16),
        name="collect",
        cost_estimate=work(2 * stages * experts * slots * tokens * width, 2 * stages * (experts * slots + tokens) * width),
    )(order, pick, rows)


def collect_each(rows, pick):
    experts, stages, slots, width = rows.shape
    tokens = pick.shape[2]

    def kernel(pick_ref, rows_ref, *outs):
        gathered = rows_ref[...].reshape(experts * slots, width)
        summed = lax.dot_general(
            pick_ref[0], gathered, (((0,), (0,)), ((), ())), preferred_element_type=f32
        ).astype(bf16)
        for k in range(stages):

            @pl.when(pl.program_id(0) == k)
            def _(ref=outs[k]):
                ref[...] = summed

    return pl.pallas_call(
        kernel,
        grid=(stages,),
        in_specs=[
            pl.BlockSpec((1, experts * slots, tokens), lambda k: (k, 0, 0)),
            pl.BlockSpec((experts, 1, slots, width), lambda k: (0, k, 0, 0)),
        ],
        out_specs=[full_spec((tokens, width))] * stages,
        out_shape=[jax.ShapeDtypeStruct((tokens, width), bf16)] * stages,
        name="collect_each",
        cost_estimate=work(2 * stages * experts * slots * tokens * width, 2 * stages * (experts * slots + tokens) * width),
    )(pick, rows)


def feed_grads(rows, d_gates, d_ups, d_logits):
    count, width = rows[0].shape
    part, lanes = d_gates[0].shape[1], d_logits[0].shape[1]
    held = len(rows)
    step = min(256, width)

    def kernel(*refs):
        ins, outs = refs[: 4 * held], refs[4 * held :]
        for kind, out in enumerate(outs):
            total = None
            for m in range(held):
                got = lax.dot_general(
                    ins[m][...],
                    ins[held * (kind + 1) + m][...],
                    (((0,), (0,)), ((), ())),
                    preferred_element_type=f32,
                )
                total = got if total is None else total + got
            out[...] = total.astype(out.dtype)

    def resident(array):
        return pl.BlockSpec(array.shape, lambda g: (0, 0), pipeline_mode=pl.Buffered(1))

    others = (*d_gates, *d_ups, *d_logits)
    return pl.pallas_call(
        kernel,
        grid=(width // step,),
        in_specs=[pl.BlockSpec((count, step), lambda g: (0, g)) for _ in rows]
        + [resident(x) for x in others],
        out_specs=[pl.BlockSpec((step, n), lambda g: (g, 0)) for n in (part, part, lanes)],
        out_shape=[
            jax.ShapeDtypeStruct((width, part), bf16),
            jax.ShapeDtypeStruct((width, part), bf16),
            jax.ShapeDtypeStruct((width, lanes), f32),
        ],
        name="feed_grads",
        cost_estimate=work(4 * held * count * width * part, 2 * (held * count * (width + 2 * part) + 2 * width * part)),
    )(*rows, *others)


def cut(place, gate, up):
    rows, hidden = gate.shape
    stages = place.shape[0] - 2
    part = hidden // stages

    def kernel(place_ref, gate_ref, up_ref, *outs):
        for k in range(stages):

            @pl.when(pl.program_id(0) == k)
            def _(ref=outs[k]):
                ref[0] = gate_ref[...]
                ref[1] = up_ref[...]

    block = pl.BlockSpec((rows, part), lambda g, p: (0, p[2 + g]))
    return pl.pallas_call(
        kernel,
        grid_spec=pltpu.PrefetchScalarGridSpec(
            num_scalar_prefetch=1,
            grid=(stages,),
            in_specs=[block, block],
            out_specs=[full_spec((2, rows, part))] * stages,
        ),
        out_shape=[jax.ShapeDtypeStruct((2, rows, part), bf16)] * stages,
        name="cut",
        cost_estimate=work(0, 8 * stages * rows * part),
    )(place, gate, up)


def other_half(place, gate, up, stages):
    width, part = gate.shape
    rows = width // (2 * stages)

    def kernel(place_ref, gate_ref, up_ref, o_ref):
        o_ref[0, 0] = gate_ref[...]
        o_ref[0, 1] = up_ref[...]

    block = pl.BlockSpec((rows, part), lambda g, p: (2 * g + 1 - p[1], 0))
    return pl.pallas_call(
        kernel,
        grid_spec=pltpu.PrefetchScalarGridSpec(
            num_scalar_prefetch=1,
            grid=(stages,),
            in_specs=[block, block],
            out_specs=pl.BlockSpec((1, 2, rows, part), lambda g, p: (g, 0, 0, 0)),
        ),
        out_shape=jax.ShapeDtypeStruct((stages, 2, rows, part), bf16),
        name="other_half",
        cost_estimate=work(0, 8 * stages * rows * part),
    )(place, gate, up)


def own_half(place, gate, up, other):
    stages, _, rows, part = other.shape

    def kernel(place_ref, gate_ref, up_ref, other_ref, *outs):
        for k in range(stages):

            @pl.when(pl.program_id(0) == k)
            def _(ref=outs[k]):
                ref[0] = (gate_ref[...].astype(f32) + other_ref[0, 0].astype(f32)).astype(bf16)
                ref[1] = (up_ref[...].astype(f32) + other_ref[0, 1].astype(f32)).astype(bf16)

    block = pl.BlockSpec((rows, part), lambda g, p: (2 * p[2 + g] + p[1], 0))
    return pl.pallas_call(
        kernel,
        grid_spec=pltpu.PrefetchScalarGridSpec(
            num_scalar_prefetch=1,
            grid=(stages,),
            in_specs=[
                block,
                block,
                pl.BlockSpec((1, 2, rows, part), lambda g, p: (p[2 + g], 0, 0, 0)),
            ],
            out_specs=[full_spec((2, rows, part))] * stages,
        ),
        out_shape=[jax.ShapeDtypeStruct((2, rows, part), bf16)] * stages,
        name="own_half",
        cost_estimate=work(0, 12 * stages * rows * part),
    )(place, gate, up, other)


def assemble(place, mine, theirs):
    stages = len(mine)
    _, rows, part = mine[0].shape

    def kernel(place_ref, *refs):
        ins, (gate_ref, up_ref) = refs[:-2], refs[-2:]
        step = pl.program_id(0)
        hop = (place_ref[0] - step // 2) % stages
        here = step % 2 == place_ref[1]
        for k in range(stages):
            for which in range(2):

                @pl.when((hop == k) & (here == (which == 0)))
                def _(ref=ins[which * stages + k]):
                    gate_ref[...] = ref[0]
                    up_ref[...] = ref[1]

    block = pl.BlockSpec((rows, part), lambda g, p: (g, 0))
    shape = jax.ShapeDtypeStruct((2 * stages * rows, part), bf16)
    return pl.pallas_call(
        kernel,
        grid_spec=pltpu.PrefetchScalarGridSpec(
            num_scalar_prefetch=1,
            grid=(2 * stages,),
            in_specs=[
                pl.BlockSpec((2, rows, part), lambda g, p: (0, 0, 0), pipeline_mode=pl.Buffered(1))
            ]
            * (2 * stages),
            out_specs=[block, block],
        ),
        out_shape=[shape, shape],
        name="assemble",
        cost_estimate=work(0, 12 * stages * rows * part),
    )(place, *mine, *theirs)


def widen(place, got):
    stages = len(got)
    _, rows, part = got[0].shape

    def kernel(place_ref, *refs):
        hop = (place_ref[0] - pl.program_id(1)) % stages
        for k in range(stages):

            @pl.when(hop == k)
            def _(ref=refs[k]):
                refs[-1][...] = ref[...].astype(f32)

    return pl.pallas_call(
        kernel,
        grid_spec=pltpu.PrefetchScalarGridSpec(
            num_scalar_prefetch=1,
            grid=(2, stages),
            in_specs=[pl.BlockSpec((1, rows, part), lambda w, g, p: (w, 0, 0))] * stages,
            out_specs=pl.BlockSpec((1, rows, part), lambda w, g, p: (w, 0, g)),
        ),
        out_shape=jax.ShapeDtypeStruct((2, rows, stages * part), f32),
        name="widen",
        cost_estimate=work(0, 12 * stages * rows * part),
    )(place, *got)


def feed_kernel(own_ref, r_ref, g_ref, other_ref, router_ref, wg_ref, wu_ref, wd_ref, *outs):
    out_ref, db_ref, low_ref, dg_ref, du_ref, dr_ref, dl_ref = outs
    rows, grads = r_ref[...], g_ref[...].astype(f32)
    router = router_ref[...]
    logits = jnp.dot(rows, router, preferred_element_type=f32)
    column = lax.broadcasted_iota(jnp.int32, logits.shape, 1)
    turn = (column == own_ref[0]).astype(f32) - (column == other_ref[...]).astype(f32)
    lead = jnp.sum(logits * turn, axis=1, keepdims=True)
    gate, rest = jax.nn.sigmoid(lead), jax.nn.sigmoid(-lead)
    d_rows = (gate * grads).astype(bf16)
    dr_ref[...] = d_rows
    gate_pre = jnp.dot(rows, wg_ref[...], preferred_element_type=f32)
    up_pre = jnp.dot(rows, wu_ref[...], preferred_element_type=f32)
    d_low = lax.dot_general(
        d_rows, wd_ref[...], (((1,), (1,)), ((), ())), preferred_element_type=f32
    )
    sigma = jax.nn.sigmoid(gate_pre)
    silu = gate_pre * sigma
    low = (silu * up_pre).astype(bf16)
    low_ref[...] = low
    d_up = (d_low * silu).astype(bf16)
    du_ref[...] = d_up
    d_gate = (d_low * up_pre * (sigma + silu * (1.0 - sigma))).astype(bf16)
    dg_ref[...] = d_gate
    result = jnp.dot(low, wd_ref[...], preferred_element_type=f32)
    out_ref[...] = (gate * result).astype(bf16)
    d_value = jnp.sum(grads * result, axis=1, keepdims=True)
    d_logits = (gate * rest * d_value) * turn
    high = d_logits.astype(bf16)
    small = (d_logits - high.astype(f32)).astype(bf16)
    half = high.shape[1]
    dl_ref[:, :half] = high
    dl_ref[:, half:] = small
    d_b = lax.dot_general(
        d_gate, wg_ref[...], (((1,), (1,)), ((), ())), preferred_element_type=f32
    ) + lax.dot_general(d_up, wu_ref[...], (((1,), (1,)), ((), ())), preferred_element_type=f32)
    for piece in (high, small):
        d_b = d_b + lax.dot_general(
            piece, router, (((1,), (1,)), ((), ())), preferred_element_type=f32
        )
    db_ref[...] = d_b.astype(bf16)


def feed(own, rows, grads, other, router, wg, wu, wd):
    count, width = rows.shape
    part = wg.shape[1]
    step = min(256, count)
    lanes = router.shape[1]

    def by_rows(columns):
        return pl.BlockSpec((step, columns), lambda g, s: (g, 0))

    def held(shape):
        return pl.BlockSpec(shape, lambda g, s: (0, 0), pipeline_mode=pl.Buffered(1))

    def shape(columns):
        return jax.ShapeDtypeStruct((count, columns), bf16)

    widths = (width, width, part, part, part, width, 2 * lanes)
    return pl.pallas_call(
        feed_kernel,
        grid_spec=pltpu.PrefetchScalarGridSpec(
            num_scalar_prefetch=1,
            grid=(count // step,),
            in_specs=[by_rows(width), by_rows(width), by_rows(1)]
            + [held(w.shape) for w in (router, wg, wu, wd)],
            out_specs=[by_rows(w) for w in widths],
        ),
        out_shape=[shape(w) for w in widths],
        name="feed",
        cost_estimate=work(12 * count * width * part, 6 * width * part + 2 * count * (5 * width + 3 * part), count * part),
    )(own, rows, grads, other, router, wg, wu, wd)


def after(array, *others):
    return lax.optimization_barrier((array, *others))[0]


def per_device(
    inputs,
    attn_routes,
    mlp_routes,
    pic_start,
    kv_weight,
    router_weight,
    norm_gains,
    q_weight,
    o_weight,
    gate_weight,
    up_weight,
    down_weight,
    cotangent,
):
    experts = lax.axis_size("expert")
    dp_size = lax.axis_size("dp")
    stages = dp_size // 2
    own = lax.axis_index("expert")
    dp_index = lax.axis_index("dp")
    stage, core = dp_index // 2, dp_index % 2
    tokens, width = inputs.shape[2], inputs.shape[3]
    inner = HEADS * HSZ
    group = inner // experts
    slots = tokens * TOPK // experts
    span = tokens * experts
    rows_each = kv_weight.shape[0]
    hidden = gate_weight.shape[2]
    part = hidden // stages
    routed = experts * slots
    same_core = [[z * 2 + c for z in range(stages)] for c in range(2)]

    def exchange(blocks):
        return lax.all_to_all(blocks, "expert", 0, 0, tiled=True)

    def spread(block):
        return exchange(jnp.broadcast_to(block[None], (experts,) + block.shape))

    def along(block, k):
        if k % stages == 0:
            return block
        return lax.ppermute(
            block, "dp", [(j, ((j // 2 + k) % stages) * 2 + j % 2) for j in range(dp_size)]
        )

    def partner(block):
        return lax.ppermute(block, "dp", [(j, j ^ 1) for j in range(dp_size)])

    def pick(array, index, axis=0):
        return lax.dynamic_index_in_dim(array, index, axis, keepdims=False)

    small = jnp.concatenate(
        [
            attn_routes.reshape(-1).astype(bf16),
            mlp_routes.reshape(-1).astype(bf16),
            router_weight.reshape(-1),
            norm_gains.reshape(-1),
        ]
    )
    length = small.shape[0]
    line = 2 * group
    extra = -(-length // (16 * line)) * 16
    small = jnp.pad(small, (0, extra * line - length)).reshape(1, extra, line)
    kv_split = kv_weight.reshape(rows_each, 2, experts, group).transpose(2, 0, 1, 3)
    first = jnp.concatenate(
        [
            jnp.broadcast_to(inputs, (experts, MICRO, tokens, width)).reshape(experts, -1, width),
            kv_split.reshape(experts, rows_each * line // width, width),
            jnp.broadcast_to(small.reshape(1, -1, width), (experts, extra * line // width, width)),
        ],
        axis=1,
    )
    first = exchange(first)
    x_blocks = first[:, : MICRO * tokens].reshape(experts, MICRO, tokens, width)
    kv_rows = first[:, MICRO * tokens :].reshape(experts, rows_each + extra, line)
    stage_order = (stage - jnp.arange(stages, dtype=jnp.int32)) % stages
    place = jnp.arange(experts, dtype=jnp.int32)
    cot_stages = lax.all_gather(cotangent[0], "dp", axis=0, axis_index_groups=same_core)
    route_rows = mlp_routes[0].reshape(-1).astype(bf16)
    route_rows = jnp.pad(route_rows, (0, -route_rows.shape[0] % 128)).reshape(-1, 128)
    own_routes = jnp.stack([along(route_rows, k) for k in range(stages)]).reshape(stages, -1)
    own_routes = own_routes[:, : MICRO * tokens * TOPK].astype(jnp.int32)
    own_routes = own_routes.reshape(stages, MICRO, tokens, TOPK)
    home_m = selection(
        (own_routes[:, None] == place[None, :, None, None, None]).any(-1).astype(f32), slots
    )
    home_m = home_m.transpose(2, 0, 1, 3, 4).reshape(MICRO, stages, experts * slots, tokens)
    q_full = lax.all_gather(after(q_weight[0], cot_stages, first), "dp", axis=0, tiled=True)
    cot_rows = {}
    for m in ORDER:
        blocks = [pick(cot_stages, stage_order[k])[m] for k in range(stages)]
        cot_rows[m] = exchange(dispatch(blocks, home_m[m])(experts))
    kv_rows = after(kv_rows, q_full, cot_rows[ORDER[0]])
    kv_got = lax.all_gather(kv_rows, "dp", axis=0)

    forward_order = (stage + jnp.arange(stages, dtype=jnp.int32)) % stages
    where = jnp.concatenate([jnp.stack([stage, core]), forward_order]).astype(jnp.int32)
    if part % 128 == 0:
        mine = list(cut(where, gate_weight[0], up_weight[0]))
    else:
        both = jnp.stack([gate_weight[0], up_weight[0]]).reshape(2, -1, stages, part)
        mine = [pick(both, forward_order[k], 2) for k in range(stages)]
    for k in range(1, stages):
        mine[k] = along(after(mine[k], kv_rows), k)
    kv_cols = kv_got[:, :, :rows_each].reshape(width, line)
    small = kv_got[:, :, rows_each:].reshape(dp_size, experts, extra * line)
    count = MICRO * tokens * TOPK
    routes_a = pick(small[:, :, :count], dp_index).astype(jnp.int32)
    routes_a = routes_a.reshape(experts, MICRO, tokens, TOPK)
    routes_m = small[:, :, count : 2 * count].reshape(stages, 2, experts, count)
    routes_m = pick(routes_m, core, 1).astype(jnp.int32)
    routes_m = routes_m.reshape(stages, experts, MICRO, tokens, TOPK)[stage_order]
    router = small[:, :, 2 * count : 2 * count + rows_each * 2 * experts].reshape(
        width, 2 * experts
    )
    gains = small[:, :, 2 * count + rows_each * 2 * experts : length].reshape(width, 2)
    gain_1, gain_2 = gains[:, 0].astype(f32)[None], gains[:, 1].astype(f32)[None]
    router_a = jnp.pad(router[:, :experts], ((0, 0), (0, 128 - experts)))
    router_m = jnp.pad(router[:, experts:], ((0, 0), (0, 128 - experts)))

    x_all = x_blocks.transpose(1, 0, 2, 3).reshape(MICRO, span, width).astype(f32)
    a_all = (x_all * inverse_rms(x_all) * gain_1).astype(bf16)

    token = jnp.arange(tokens, dtype=jnp.int32)
    chosen = (routes_a[None] == place[:, None, None, None, None]).any(-1)
    pick_all = selection(chosen.transpose(0, 2, 1, 3).astype(f32), slots)
    query_pos = jnp.einsum(
        "emkst,t->emks", pick_all, token.astype(bf16), preferred_element_type=f32
    ).astype(jnp.int32)
    query_pos = (
        query_pos
        + place[:, None] * tokens
        + jnp.arange(MICRO, dtype=jnp.int32)[:, None, None] * span
    )
    query_pos = query_pos.transpose(1, 0, 2, 3).reshape(MICRO, experts, routed, 1)
    pick_a = pick(pick_all, own)
    other_a = jnp.einsum(
        "mkst,kmt->mks",
        pick_a,
        (routes_a.sum(-1) - own).astype(bf16),
        preferred_element_type=f32,
    ).astype(jnp.int32)
    other_a = other_a.reshape(MICRO, routed, 1)
    home_a = pick(pick_all, own, 2).transpose(1, 0, 2, 3).reshape(MICRO, routed, tokens)
    pick_m = selection((routes_m == own).any(-1).astype(f32), slots)
    other_m = jnp.einsum(
        "kemst,kemt->mkes",
        pick_m,
        (routes_m.sum(-1) - own).astype(bf16),
        preferred_element_type=f32,
    ).astype(jnp.int32)
    other_m = other_m.transpose(0, 2, 1, 3).reshape(MICRO, experts * stages * slots, 1)

    key_cos, key_sin = rope_tables(jnp.arange(MICRO * span, dtype=jnp.int32).reshape(MICRO, span))
    query_cos, query_sin = rope_tables(query_pos[..., 0])
    kv_own = project_kv(
        a_all,
        kv_cols,
        jnp.stack([key_cos, jnp.ones_like(key_cos)], axis=1),
        jnp.stack([key_sin, jnp.zeros_like(key_sin)], axis=1),
    )
    kvs = [kv_own[m] for m in range(MICRO)]

    a_pairs = jnp.einsum(
        "mest,metd->mesd",
        pick_a,
        a_all.reshape(MICRO, experts, tokens, width),
        preferred_element_type=f32,
    ).astype(bf16)
    a_pairs = a_pairs.reshape(MICRO, routed, width)
    column = jnp.arange(128, dtype=jnp.int32)[None, None, :]
    turn_a = (column == own).astype(f32) - (column == other_a).astype(f32)
    lead = jnp.sum(mm(a_pairs, router_a) * turn_a, axis=-1, keepdims=True)
    gate_a, rest_a = jax.nn.sigmoid(lead), jax.nn.sigmoid(-lead)
    q_out = project_q(
        a_pairs.reshape(MICRO * routed, width),
        q_full,
        pick(query_cos, own, 1).reshape(MICRO * routed, HSZ),
        pick(query_sin, own, 1).reshape(MICRO * routed, HSZ),
        MICRO,
        experts,
    )

    down_other = partner(down_weight[0])
    down_w = jnp.concatenate(
        [
            jnp.where(core == 0, down_weight[0], down_other),
            jnp.where(core == 0, down_other, down_weight[0]),
        ]
    )
    start = after(pic_start.astype(jnp.int32), down_w)
    held = lax.optimization_barrier(
        (o_weight[0], *mine, q_out, *kvs, home_a, cot_rows[ORDER[1]], other_m, gate_a, down_w)
    )
    mine = list(held[1 : 1 + stages])
    o_full = lax.all_gather(held[0], "dp", axis=0, tiled=True)
    queries, mixed, peaks, attn, middles, inverses, feeds = {}, {}, {}, {}, {}, {}, {}
    mixed_got = {}
    for m in ORDER:
        queries[m] = exchange(q_out[m])
        heads, peaks[m] = attend(queries[m], query_pos[m], kvs[: m + 1], start)
        mixed_got[m] = exchange(heads)
    for m in ORDER:
        attn[m], gated, mixed[m] = project_o(mixed_got[m], o_full, gate_a[m])
        back = exchange(gated.reshape(experts, slots, width))
        middles[m], inverses[m], b_low = combine(
            back.reshape(routed, width), home_a[m], inputs[0, m], gain_2
        )
        blocks = [along(b_low, k) for k in range(stages)]
        feeds[m] = exchange(dispatch(blocks, home_m[m])(experts))
    mine = list(lax.optimization_barrier((*mine, b_low)))[:-1]
    gate_w, up_w = assemble(where, mine, [partner(piece) for piece in mine])

    pairs = experts * stages * slots
    own_id = own.reshape(1).astype(jnp.int32)
    outs, d_pieces, d_rows, kept_feed = {}, {}, {}, {}
    for m in ORDER:
        rows = feeds[m].reshape(pairs, width)
        if kept_feed:
            rows = after(rows, kept_feed[ORDER[0]][4])
        outs[m], d_b, *kept_feed[m] = feed(
            own_id,
            rows,
            cot_rows[m].reshape(pairs, width),
            other_m[m],
            router_m,
            gate_w,
            up_w,
            down_w,
        )
        d_rows[m] = exchange(d_b.reshape(experts, stages, slots, width))

    def joined(index):
        return jnp.concatenate([kept_feed[m][index] for m in ORDER])

    def over_stages(rows, m):
        summed = collect(rows, home_m[m], stage_order)
        return summed, lax.psum_scatter(
            summed, "dp", scatter_dimension=0, tiled=True, axis_index_groups=same_core
        )[0]

    gate_grad, up_grad, router_m_grad = feed_grads(
        [feeds[m].reshape(pairs, width) for m in ORDER],
        [kept_feed[m][1] for m in ORDER],
        [kept_feed[m][2] for m in ORDER],
        [kept_feed[m][4] for m in ORDER],
    )
    early, d_pieces[ORDER[0]] = over_stages(after(d_rows[ORDER[0]], gate_grad), ORDER[0])
    late, d_pieces[ORDER[1]] = over_stages(after(d_rows[ORDER[1]], early), ORDER[1])
    down_grad = t_mm(after(joined(0), late), joined(3)).astype(bf16)
    out_rows = exchange(
        after(outs[ORDER[0]], d_rows[ORDER[1]]).reshape(experts, stages, slots, width)
    )
    out_sums = {ORDER[0]: over_stages(after(out_rows, late), ORDER[0])[1]}

    other = partner(other_half(where, gate_grad, after(up_grad, late), stages))
    total = list(own_half(where, gate_grad, up_grad, other))

    total[1] = along(total[1], 1)
    d_pieces[ORDER[0]] = after(d_pieces[ORDER[0]], total[0])
    d_pieces[ORDER[1]] = after(d_pieces[ORDER[1]], total[1], down_grad)

    def scattered(grad):
        return lax.psum_scatter(grad, "dp", scatter_dimension=0, tiled=True)

    def ordered(values):
        return jnp.concatenate([values[m] for m in ORDER])

    gain_2_grad = jnp.zeros((1, width), f32)
    d_middles, d_attn, d_flat, d_pairs, d_kvs, logit_grads, later = {}, {}, {}, {}, {}, {}, []
    for m in ORDER:
        d_middles[m], gain_part, sent = middle_back(
            [d_pieces[m]], middles[m], inverses[m], cotangent[0, m], gain_2, home_a[m]
        )
        gain_2_grad = gain_2_grad + gain_part
        if m == ORDER[0]:
            sent = after(sent, out_rows)
        got = exchange(sent.reshape(experts, slots, width)).reshape(routed, width)
        d_attn[m], d_heads, logit_grads[m] = back_o(
            got, attn[m], gate_a[m], rest_a[m], turn_a[m], o_full, experts
        )
        d_heads = exchange(d_heads)
        if m == ORDER[1]:
            o_grad = t_mm(ordered(mixed), ordered(d_attn)).astype(bf16)
            d_heads = after(d_heads, o_grad)
        d_query, d_kvs[m], *later = attend_back(
            queries[m],
            d_heads,
            query_cos[m],
            query_sin[m],
            query_pos[m],
            kvs[: m + 1],
            key_cos[m],
            key_sin[m],
            later,
            start,
        )
        d_query = exchange(d_query)
        if m == ORDER[1]:
            kv_grad = t_mm(ordered(a_all), ordered(d_kvs)).astype(bf16)
            d_query = after(d_query, kv_grad)
        d_pairs[m], d_flat[m] = back_q(d_query, q_full, logit_grads[m], router_a)

    pair_rows = ordered(a_pairs)
    q_grad = t_mm(pair_rows, ordered(d_flat)).astype(bf16)
    d_pairs[ORDER[1]] = after(d_pairs[ORDER[1]], q_grad)
    router_a_grad = t_mm(pair_rows, ordered(logit_grads))
    router_a_grad = router_a_grad[:, :experts] + router_a_grad[:, 128 : 128 + experts]
    o_mine = scattered(o_grad)
    kv_mine = scattered(kv_grad)
    d_pairs[ORDER[1]] = after(d_pairs[ORDER[1]], o_mine)
    for k in range(2, stages):
        piece = after(total[k], q_grad) if k < 4 else after(total[k], total[k - 2])
        total[k] = along(piece, k)
    d_pairs[ORDER[1]] = after(d_pairs[ORDER[1]], *total[2:3])
    if part % 128 == 0:
        shares = widen(where, total)
    else:
        got = jnp.stack(total)[stage_order].astype(f32)
        shares = jnp.concatenate([got[s] for s in range(stages)], axis=2)
    gate_share, up_share = shares[:1], shares[1:]
    o_share = o_mine.astype(f32)[None]
    q_share = scattered(q_grad).astype(f32)[None]
    router_m_grad = router_m_grad[:, :experts] + router_m_grad[:, 128 : 128 + experts]
    down_split = down_grad.reshape(2, part // 2, width)
    down_share = (
        pick(down_split, core).astype(f32) + partner(pick(down_split, 1 - core)).astype(f32)
    )[None]


    gain_1_grad = jnp.zeros((1, width), f32)
    grad_x = [None] * MICRO
    for m in ORDER:
        d_a = exchange(token_back(d_kvs[m], kv_cols, d_pairs[m], pick_a[m]))
        grad_x[m], gain_part = input_back(d_a, inputs[0, m], gain_1, d_middles[m])
        gain_1_grad = gain_1_grad + gain_part
    grad_x = jnp.stack(grad_x)[None]

    out_rows = exchange(after(outs[ORDER[1]], d_a).reshape(experts, stages, slots, width))
    out_sums[ORDER[1]] = over_stages(out_rows, ORDER[1])[1]
    out_act = jnp.stack([middles[m] + out_sums[m].astype(f32) for m in range(MICRO)])
    out_act = out_act.astype(bf16)[None]
    kv_got = exchange(kv_mine.reshape(experts, rows_each, line)).reshape(experts, rows_each, 2, group)
    kv_share = kv_got.transpose(1, 2, 0, 3).reshape(rows_each, 2 * inner).astype(f32)

    tail = jnp.concatenate(
        [router_a_grad.T, router_m_grad.T, gain_1_grad, gain_2_grad], axis=0
    )
    kinds = 2 * experts + 2
    tail = jnp.pad(tail, ((0, -kinds % 8), (0, 0))).reshape(-1, dp_size, width // dp_size)
    tail = lax.psum_scatter(
        tail.transpose(1, 0, 2), "dp", scatter_dimension=0, tiled=True
    )
    tail = tail.reshape(-1, experts, rows_each).transpose(1, 0, 2)
    tail = lax.psum_scatter(tail, "expert", scatter_dimension=0, tiled=True)[0].T
    router_share, gains_share = tail[:, : 2 * experts], tail[:, 2 * experts : kinds]

    largest = jnp.maximum(peaks[0], peaks[1])[:, :, 0, 0]
    mine_here = jnp.arange(HEADS, dtype=jnp.int32) // (HEADS // experts) == own
    largest = jnp.where(mine_here[None], jnp.tile(largest, (1, experts)), masked_low)
    largest = jnp.pad(largest, ((0, 0), (0, 128 - HEADS)))
    for axis, size in (("dp", dp_size), ("expert", experts)):
        hop = 1
        while hop < size:
            largest = jnp.maximum(
                largest, lax.ppermute(largest, axis, [(j, j ^ hop) for j in range(size)])
            )
            hop *= 2
    ratio = logit_cap / jnp.maximum(largest[:, :HEADS], logit_cap)
    root_q = jnp.repeat(jnp.sqrt(pick(ratio, own)), HSZ)[None]
    root_k = jnp.repeat(jnp.sqrt(jnp.min(ratio, axis=0)), HSZ)[None]
    clipped_q = (q_weight.astype(f32) * root_q[None]).astype(bf16)
    clipped_key = (kv_weight[:, :inner].astype(f32) * root_k).astype(bf16)
    return (
        out_act,
        grad_x,
        kv_share,
        router_share,
        gains_share,
        q_share,
        o_share,
        gate_share,
        up_share,
        down_share,
        clipped_q,
        clipped_key,
    )


def solution(mesh):
    tokens4 = P("dp", None, "expert", None)
    rows2 = P(("dp", "expert"), None)
    weights3 = P("expert", "dp", None)
    return jax.shard_map(
        per_device,
        mesh=mesh,
        in_specs=(tokens4,) * 3 + (P("dp"),) + (rows2,) * 3 + (weights3,) * 5 + (tokens4,),
        out_specs=(tokens4,) * 2 + (rows2,) * 3 + (weights3,) * 6 + (rows2,),
        check_vma=False,
    )
```

time: 1770 us -> 1360 us (0.77)
  matrix products: 407 us -> 53.6 us
  Pallas kernels: 103 us -> 398 us
  starting transfers between devices: 315 us -> 120 us
  waiting for transfers between devices: 536 us -> 491 us
  other arithmetic: 103 us -> 64.2 us
  local copies, waits for them, and re-layouts: 131 us -> 93.1 us
  blocking collectives: 144 us -> 112 us
    pallas_call x4 -> x32, Pallas kernels: 21.1 us -> 330 us  [the longest x2 106 us: feed(): pl.pallas_call(feed_kernel, grid_spec=pltpu.PrefetchScalarGridSpec(num_sc...]
    ppermute x36 -> x15, starting transfers between devices: 215 us -> 23.9 us  [along(): lax.ppermute(block, 'dp', [(j, (j // 2 + k) % stages * 2 + j % 2) for j i...]
    ppermute x69 -> x5, waiting for transfers between devices: 196 us -> 22.9 us  [per_device(): lax.ppermute(largest, axis, [(j, j ^ hop) for j in range(size)])]
    dot_general x51 -> x4, matrix products: 177 us -> 5.24 us  [the longest x1 4.19 us: per_device(): jnp.einsum('mest,metd->mesd', pick_a, a_all.reshape(MICRO, experts, token...]
    all_gather x2 -> x0, blocking collectives: 144 us -> none  [the longest x1 136 us: per_device(): lax.all_gather(lax.all_gather(small, 'expert', axis=0), 'dp', axis=0)]
    ppermute x36 -> x15, waiting for transfers between devices: 301 us -> 167 us  [along(): lax.ppermute(block, 'dp', [(j, (j // 2 + k) % stages * 2 + j % 2) for j i...]
    all_to_all x0 -> x21, waiting for transfers between devices: none -> 131 us  [exchange(): return lax.all_to_all(blocks, 'expert', 0, 0, tiled=True)]
    all_gather x3 -> x4, waiting for transfers between devices: 0.02 us -> 124 us  [the longest x1 87.3 us: per_device(): kv_got = lax.all_gather(kv_rows, 'dp', axis=0)]
  transfers between devices with their start and end apart: 119 -> 60, of which waited for: 46 -> 27; matrix products, arithmetic and copies ran while one was open for 34% -> 14% of each run, Pallas kernels for 5% -> 29%
where the time goes in v1:
time: 1360 us
  waiting for transfers between devices  491 us (36%)
  Pallas kernels  398 us (29%)
  starting transfers between devices  120 us (9%)
  blocking collectives  112 us (8%)
  local copies, waits for them, and re-layouts  93.1 us (7%)
  other arithmetic  64.2 us (5%)
  matrix products  53.6 us (4%)
  between operations  24.1 us (2%)
    ppermute x15, waiting for transfers between devices, along(): lax.ppermute(block, 'dp', [(j, (j // 2 + k) % stages * 2 + j % 2) for j i...  167 us
    all_to_all x21, waiting for transfers between devices, exchange(): return lax.all_to_all(blocks, 'expert', 0, 0, tiled=True)  131 us
    pallas_call x2, Pallas kernels, feed(): pl.pallas_call(feed_kernel, grid_spec=pltpu.PrefetchScalarGridSpec(num_sc...  106 us
    all_to_all x3, blocking collectives, exchange(): return lax.all_to_all(blocks, 'expert', 0, 0, tiled=True)  95 us
    all_to_all x21, starting transfers between devices, exchange(): return lax.all_to_all(blocks, 'expert', 0, 0, tiled=True)  89.9 us
    all_gather x1, waiting for transfers between devices, per_device(): kv_got = lax.all_gather(kv_rows, 'dp', axis=0)  87.3 us
    dot_general x5, matrix products, t_mm(): lax.dot_general(left, right, (((0,), (0,)), ((), ())), preferred_element_...  45.6 us
    reduce_scatter x4, waiting for transfers between devices, over_stages(): lax.psum_scatter(summed, 'dp', scatter_dimension=0, tiled=True, axis_inde...  45.5 us
  transfers between devices with their start and end apart: 60, of which 27 were waited for; matrix products, arithmetic and copies ran while one was open for 14% of the time, Pallas kernels for 29%

profile of v1, /device:TPU:0, one launch (start us, length us, event | category | flops | bytes accessed | tf_op | source)
XLA Modules:
  0.0 1356.2 jit_solution(16331592866061142172)
XLA Ops:
  15.2 59.9 %all_to_all.120 = bf16[4,296,2048]{2,1,0:T(8,128)(2,1)} all-to-all(bf16[4,296,2048]{2,1,0:T(8,128)(2,1)S(1)} %pad_maximum_fusion.2), channel_id=1, replica_groups=mesh['dp'=8,'expert'=4] {'expert'}, dimensions={0} | all-to-all | bytes 9699328 | tf_op jit(solution)/shard_map/all_to_all | solution.py:908
  75.1 18.0 %all-gather.6.cloned.1.call-done = bf16[4,2,128,2048]{3,2,1,0:T(8,128)(2,1)} async-done(((bf16[1,2,128,2048]{3,2,1,0:T(8,128)(2,1)}), bf16[4,2,128,2048]{3,2,1,0:T(8,128)(2,1)}) %all-gather.6.cloned.1.call-update) | async-done | bytes 4194320 | tf_op jit(solution)/shard_map/all_gather | solution.py:952
  123.5 45.4 %all-to-all-done.1 = bf16[4,4,64,2048]{3,2,1,0:T(8,128)(2,1)} async-done(((bf16[4,4,64,2048]{3,2,1,0:T(8,128)(2,1)}), bf16[4,4,64,2048]{3,2,1,0:T(8,128)(2,1)}, u32[]{:S(2)}, u32[]{:S(2)}) %all-to-all-start.1) | async-done | bytes 4194336 | tf_op jit(solution)/shard_map/all_to_all | solution.py:908
  214.8 87.3 %all-gather.12.cloned.1.call-done = bf16[32,80,1024]{2,1,0:T(8,128)(2,1)} async-done(((bf16[4,80,1024]{2,1,0:T(8,128)(2,1)}), bf16[32,80,1024]{2,1,0:T(8,128)(2,1)}) %all-gather.12.cloned.1.call-update) | async-done | bytes 5242896 | tf_op jit(solution)/shard_map/all_gather | solution.py:968
  359.6 18.0 %all_to_all.121.q_ref = bf16[4,256,512]{2,1,0:T(8,128)(2,1)} all-to-all(bf16[4,256,512]{2,1,0:T(8,128)(2,1)S(1)} %get-tuple-element.241), channel_id=1, replica_groups=mesh['dp'=8,'expert'=4] {'expert'}, dimensions={0} | all-to-all | bytes 2097152 | tf_op jit(solution)/shard_map/all_to_all | solution.py:908
  384.0 14.4 %attend.3 = (bf16[4,256,512]{2,1,0:T(8,128)(2,1)}, f32[4,4,8,128]{3,2,1,0:T(8,128)}) custom-call(s32[1]{0:T(128)S(6)} %copy.222.start_ref, bf16[4,256,512]{2,1,0:T(8,128)(2,1)} %all_to_all.121.q_ref, s32[4,256,1]{2,1,0:T(8,128)} %squeeze.285.pos_ref, bf16[2,512,512]{2,1,0:T(8,128)(2,1)} %get-tuple-element.243.rest_0_, ...), custom_call_target="tpu_custom_call" | custom-call | flops 2147483648 | bytes 2097152 | tf_op jit(solution)/shard_map/attend/pallas_call | solution.py:180
  472.9 13.1 collective-permute-done.10.refs_1_
  486.0 20.7 %collective-permute-done.11.refs_2_ = bf16[128,2048]{1,0:T(8,128)(2,1)S(1)} collective-permute-done((bf16[128,2048]{1,0:T(8,128)(2,1)}, bf16[128,2048]{1,0:T(8,128)(2,1)S(1)}, u32[]{:S(2)}, u32[]{:S(2)}) %collective-permute-start.11) | collective-permute-done | bytes 524320 | tf_op jit(solution)/shard_map/ppermute | solution.py:916
  548.9 19.7 %collective-permute-done.8.refs_2_ = bf16[128,2048]{1,0:T(8,128)(2,1)} collective-permute-done((bf16[128,2048]{1,0:T(8,128)(2,1)S(1)}, bf16[128,2048]{1,0:T(8,128)(2,1)}, u32[]{:S(2)}, u32[]{:S(2)}) %collective-permute-start.8) | collective-permute-done | bytes 524320 | tf_op jit(solution)/shard_map/ppermute | solution.py:916
  602.4 53.3 %feed.2 = (bf16[1024,2048]{1,0:T(8,128)(2,1)}, bf16[1024,2048]{1,0:T(8,128)(2,1)}, bf16[1024,1408]{1,0:T(8,128)(2,1)}, bf16[1024,1408]{1,0:T(8,128)(2,1)}, bf16[...) custom-call(s32[1]{0:T(128)} %bitcast.63.own_ref, ...), custom_call_target="tpu_custom_call" | custom-call | flops 35433480192 | bytes 46923776 | tf_op jit(solution)/shard_map/feed/pallas_call | solution.py:856
  660.8 53.2 %feed.3 = (bf16[1024,2048]{1,0:T(8,128)(2,1)}, bf16[1024,2048]{1,0:T(8,128)(2,1)}, bf16[1024,1408]{1,0:T(8,128)(2,1)}, bf16[1024,1408]{1,0:T(8,128)(2,1)}, bf16[...) custom-call(s32[1]{0:T(128)} %bitcast.63.own_ref, ...), custom_call_target="tpu_custom_call" | custom-call | flops 35433480192 | bytes 46923776 | tf_op jit(solution)/shard_map/feed/pallas_call | solution.py:856
  719.3 36.0 %feed_grads.1 = (bf16[2048,1408]{1,0:T(8,128)(2,1)}, bf16[2048,1408]{1,0:T(8,128)(2,1)}, f32[2048,256]{1,0:T(8,128)}) custom-call(bf16[1024,2048]{1,0:T(8,128)(2,1)} %bitcast.72.r_ref.refs_0_, bf16[1024,2048]{1,0:T(8,128)(2,1)} %bitcast.64.r_ref.refs_1_, bf16[1024,1408]{1,0:T(8,128)(2,1)} %get-tuple-element.146.refs_2_, ...), custom_call_target="tpu_custom_call" | custom-call | flops 23622320128 | bytes 31457280 | tf_op jit(solution)/shard_map/feed_grads/pallas_call | solution.py:638
  796.9 12.2 reduce-scatter.11.cloned.1.call-done
  812.5 16.8 %all-to-all-done.15.rows_ref = bf16[4,4,64,2048]{3,2,1,0:T(8,128)(2,1)} async-done(((bf16[4,4,64,2048]{3,2,1,0:T(8,128)(2,1)}), bf16[4,4,64,2048]{3,2,1,0:T(8,128)(2,1)}, u32[]{:S(2)}, u32[]{:S(2)}) %all-to-all-start.15) | async-done | bytes 4194336 | tf_op jit(solution)/shard_map/all_to_all | solution.py:908
  833.0 18.0 %fusion.6 = bf16[1408,2048]{1,0:T(8,128)(2,1)} fusion(bf16[2048,1408]{1,0:T(8,128)(2,1)} %pad_maximum_fusion.1, bf16[1024,2048]{1,0:T(8,128)(2,1)} %get-tuple-element.161, bf16[1024,2048]{1,0:T(8,128)(2,1)} %get-tuple-element.160), kind=kOutput, calls=%fused_computation.11 | convolution fusion | flops 11830820864 | bytes 19922944 | tf_op jit(solution)/shard_map/dot_general | solution.py:33
  851.0 21.0 %reduce-scatter.9.cloned.1.call-done = bf16[1,128,2048]{2,1,0:T(8,128)(2,1)} async-done(((bf16[4,128,2048]{2,1,0:T(8,128)(2,1)}), bf16[1,128,2048]{2,1,0:T(8,128)(2,1)}) %reduce-scatter.9.cloned.1.call-update) | async-done | bytes 524304 | tf_op jit(solution)/shard_map/reduce_scatter | solution.py:1112
  946.5 24.9 %attend_back.2 = (bf16[4,256,512]{2,1,0:T(8,128)(2,1)}, bf16[512,1024]{1,0:T(8,128)(2,1)}, f32[2,512,512]{2,1,0:T(8,128)}) custom-call(s32[1]{0:T(128)S(6)} %copy.222.start_ref, bf16[4,256,512]{2,1,0:T(8,128)(2,1)} %all_to_all.121.q_ref, bf16[4,256,512]{2,1,0:T(8,128)(2,1)} %copy-done.38, f32[4,256,128]{2,1,0:T(8,128)} %get-tuple-element.246.cos_ref, ...), custom_call_target="tpu_custom_call" | custom-call | flops 5368709120 | bytes 6291456 | tf_op jit(solution)/shard_map/attend_back/pallas_call | solution.py:269
  971.5 18.2 %attend_back.3 = (bf16[4,256,512]{2,1,0:T(8,128)(2,1)}, bf16[512,1024]{1,0:T(8,128)(2,1)}) custom-call(s32[1]{0:T(128)S(6)} %copy.222.start_ref, bf16[4,256,512]{2,1,0:T(8,128)(2,1)} %copy-done.37, bf16[4,256,512]{2,1,0:T(8,128)(2,1)} %all-to-all-done.14.dm_ref, f32[4,256,128]{2,1,0:T(8,128)} %get-tuple-element.247.cos_ref, ...), custom_call_target="tpu_custom_call" | custom-call | flops 2684354560 | bytes 6291456 | tf_op jit(solution)/shard_map/attend_back/pallas_call | solution.py:269
  999.4 17.1 %all_to_all.122.dq_ref = bf16[4,256,512]{2,1,0:T(8,128)(2,1)} all-to-all(bf16[4,256,512]{2,1,0:T(8,128)(2,1)S(1)} %copy-done.39), channel_id=1, replica_groups=mesh['dp'=8,'expert'=4] {'expert'}, dimensions={0} | all-to-all | bytes 2097152 | tf_op jit(solution)/shard_map/all_to_all | solution.py:908
  1051.7 97.2 %collective-permute-done.19.refs_2_ = bf16[2,256,1408]{2,1,0:T(8,128)(2,1)S(1)} collective-permute-done((bf16[2,256,1408]{2,1,0:T(8,128)(2,1)S(1)}, bf16[2,256,1408]{2,1,0:T(8,128)(2,1)S(1)}, u32[]{:S(2)}, u32[]{:S(2)}) %collective-permute-start.19) | collective-permute-done | bytes 1441824 | tf_op jit(solution)/shard_map/ppermute | solution.py:916
  1166.5 18.2 %all-to-all-done.20.got_ref = bf16[4,128,2048]{2,1,0:T(8,128)(2,1)S(1)} async-done(((bf16[4,128,2048]{2,1,0:T(8,128)(2,1)}), bf16[4,128,2048]{2,1,0:T(8,128)(2,1)S(1)}, u32[]{:S(2)}, u32[]{:S(2)}) %all-to-all-start.20) | async-done | bytes 2097184 | tf_op jit(solution)/shard_map/all_to_all | solution.py:908
  1241.0 26.5 %all-to-all-done.21.rows_ref = bf16[4,4,64,2048]{3,2,1,0:T(8,128)(2,1)} async-done(((bf16[4,4,64,2048]{3,2,1,0:T(8,128)(2,1)}), bf16[4,4,64,2048]{3,2,1,0:T(8,128)(2,1)}, u32[]{:S(2)}, u32[]{:S(2)}) %all-to-all-start.21) | async-done | bytes 4194336 | tf_op jit(solution)/shard_map/all_to_all | solution.py:908
  1316.2 16.7 %all-reduce.7 = f32[4,16,64]{2,1,0:T(8,128)S(1)} all-reduce(f32[4,16,64]{2,1,0:T(8,128)S(1)} %copy.188), channel_id=10, replica_groups=mesh['dp'=8,'expert'=4] {'expert'}, use_global_device_ids=true, to_apply=%region_14.15.clone | all-reduce | flops 4096 | bytes 32768
  1334.8 12.2 reduce-scatter.15.cloned.1.call-done
  (460 shorter events, 593.9 us)
Async XLA Ops:
  7.2 85.9 %all-gather.6.cloned.1.call-start = ((), (), s32[]{:S(2)}) async-start(), calls=%async_computation.32 | async-start | bytes 5242880 | tf_op jit(solution)/shard_map/all_gather | solution.py:952
  7.9 167.4 %all-gather.8.cloned.1.call-start = ((), (), s32[]{:S(2)}) async-start(), calls=%async_computation.33 | async-start | bytes 9437184 | tf_op jit(solution)/shard_map/all_gather | solution.py:962
  122.2 179.9 %all-gather.12.cloned.1.call-start = ((), (), s32[]{:S(2)}) async-start(), calls=%async_computation.43 | async-start | bytes 5898240 | tf_op jit(solution)/shard_map/all_gather | solution.py:968
  205.8 151.0 %all-to-all-start.4 = ((bf16[4,4,64,2048]{3,2,1,0:T(8,128)(2,1)}), bf16[4,4,64,2048]{3,2,1,0:T(8,128)(2,1)}, u32[]{:S(2)}, u32[]{:S(2)}) async-start(bf16[4,4,64,2048]{3,2,1,0:T(8,128)(2,1)} %dispatch.5), calls=%async_computation.4 | async-start | bytes 8388608 | tf_op jit(solution)/shard_map/all_to_all | solution.py:908
  210.6 226.5 %all-gather.10.cloned.1.call-start = ((), (), s32[]{:S(2)}) async-start(), calls=%async_computation.34 | async-start | bytes 9437184 | tf_op jit(solution)/shard_map/all_gather | solution.py:1070
  210.7 146.1 %collective-permute-start.4 = (bf16[2,256,1408]{2,1,0:T(8,128)(2,1)}, bf16[2,256,1408]{2,1,0:T(8,128)(2,1)}, u32[]{:S(2)}, u32[]{:S(2)}) collective-permute-start(bf16[2,256,1408]{2,1,0:T(8,128)(2,1)} %get-tuple-element.119), channel_id=1, source_target_pairs={{0,8},{4,12},{8,16},{12,20},{16,24},{20,28},{24,0},{28,4},{1,9},{5... | collective-permute-start | bytes 4325384 | tf_op jit(solution)/shard_map/ppermute | solution.py:916
  210.8 146.1 %collective-permute-start.5 = (bf16[2,256,1408]{2,1,0:T(8,128)(2,1)}, bf16[2,256,1408]{2,1,0:T(8,128)(2,1)}, u32[]{:S(2)}, u32[]{:S(2)}) collective-permute-start(bf16[2,256,1408]{2,1,0:T(8,128)(2,1)} %get-tuple-element.121), channel_id=1, source_target_pairs={{0,16},{4,20},{8,24},{12,28},{16,0},{20,4},{24,8},{28,12},{1,17},{... | collective-permute-start | bytes 4325384 | tf_op jit(solution)/shard_map/ppermute | solution.py:916
  211.5 145.4 %collective-permute-start.6 = (bf16[2,256,1408]{2,1,0:T(8,128)(2,1)}, bf16[2,256,1408]{2,1,0:T(8,128)(2,1)}, u32[]{:S(2)}, u32[]{:S(2)}) collective-permute-start(bf16[2,256,1408]{2,1,0:T(8,128)(2,1)} %get-tuple-element.123), channel_id=1, source_target_pairs={{0,24},{4,28},{8,0},{12,4},{16,8},{20,12},{24,16},{28,20},{1,25},{... | collective-permute-start | bytes 4325384 | tf_op jit(solution)/shard_map/ppermute | solution.py:916
  514.6 82.7 %all-to-all-start.10 = ((bf16[4,4,64,2048]{3,2,1,0:T(8,128)(2,1)}), bf16[4,4,64,2048]{3,2,1,0:T(8,128)(2,1)}, u32[]{:S(2)}, u32[]{:S(2)}) async-start(bf16[4,4,64,2048]{3,2,1,0:T(8,128)(2,1)} %dispatch.7), calls=%async_computation.10 | async-start | bytes 8388608 | tf_op jit(solution)/shard_map/all_to_all | solution.py:908
  532.5 54.4 %collective-permute-start.13 = (bf16[2,256,1408]{2,1,0:T(8,128)(2,1)}, bf16[2,256,1408]{2,1,0:T(8,128)(2,1)}, u32[]{:S(2)}, u32[]{:S(2)}) collective-permute-start(bf16[2,256,1408]{2,1,0:T(8,128)(2,1)} %get-tuple-element.135.refs_0_), channel_id=1, source_target_pairs={{0,4},{4,0},{8,12},{12,8},{16,20},{20,16},{24,28},{28,24},{1,5},{5... | collective-permute-start | bytes 4325384 | tf_op jit(solution)/shard_map/ppermute | solution.py:921
  532.6 54.4 %collective-permute-start.14 = (bf16[2,256,1408]{2,1,0:T(8,128)(2,1)}, bf16[2,256,1408]{2,1,0:T(8,128)(2,1)}, u32[]{:S(2)}, u32[]{:S(2)}) collective-permute-start(bf16[2,256,1408]{2,1,0:T(8,128)(2,1)} %collective-permute-done.4.refs_1_), channel_id=1, source_target_pairs={{0,4},{4,0},{8,12},{12,8},{16,20},{20,16},{24,28},{28,24},{1,5},{5... | collective-permute-start | bytes 4325384 | tf_op jit(solution)/shard_map/ppermute | solution.py:921
  533.1 53.9 %collective-permute-start.15 = (bf16[2,256,1408]{2,1,0:T(8,128)(2,1)}, bf16[2,256,1408]{2,1,0:T(8,128)(2,1)}, u32[]{:S(2)}, u32[]{:S(2)}) collective-permute-start(bf16[2,256,1408]{2,1,0:T(8,128)(2,1)} %collective-permute-done.5.refs_2_), channel_id=1, source_target_pairs={{0,4},{4,0},{8,12},{12,8},{16,20},{20,16},{24,28},{28,24},{1,5},{5... | collective-permute-start | bytes 4325384 | tf_op jit(solution)/shard_map/ppermute | solution.py:921
  597.3 58.4 %all-to-all-start.6 = ((bf16[4,4,64,2048]{3,2,1,0:T(8,128)(2,1)}), bf16[4,4,64,2048]{3,2,1,0:T(8,128)(2,1)}, u32[]{:S(2)}, u32[]{:S(2)}) async-start(bf16[4,4,64,2048]{3,2,1,0:T(8,128)(2,1)} %dispatch.6), calls=%async_computation.6 | async-start | bytes 8388608 | tf_op jit(solution)/shard_map/all_to_all | solution.py:908
  655.7 58.3 %all-to-all-start.12 = ((bf16[4,4,64,2048]{3,2,1,0:T(8,128)(2,1)}), bf16[4,4,64,2048]{3,2,1,0:T(8,128)(2,1)}, u32[]{:S(2)}, u32[]{:S(2)}) async-start(bf16[4,4,64,2048]{3,2,1,0:T(8,128)(2,1)} %bitcast.298), calls=%async_computation.12 | async-start | bytes 8388608 | tf_op jit(solution)/shard_map/all_to_all | solution.py:908
  718.8 90.3 %reduce-scatter.11.cloned.1.call-start = ((), (), s32[]{:S(2)}) async-start(), calls=%async_computation.36 | async-start | bytes 2621440 | tf_op jit(solution)/shard_map/reduce_scatter | solution.py:1112
  781.0 91.1 %reduce-scatter.9.cloned.1.call-start = ((), (), s32[]{:S(2)}) async-start(), calls=%async_computation.35 | async-start | bytes 2621440 | tf_op jit(solution)/shard_map/reduce_scatter | solution.py:1112
  796.9 75.2 %collective-permute-start.18 = (bf16[2,256,1408]{2,1,0:T(8,128)(2,1)}, bf16[2,256,1408]{2,1,0:T(8,128)(2,1)S(1)}, u32[]{:S(2)}, u32[]{:S(2)}) collective-permute-start(bf16[2,256,1408]{2,1,0:T(8,128)(2,1)} %get-tuple-element.156), channel_id=1, source_target_pairs={{0,8},{4,12},{8,16},{12,20},{16,24},{20,28},{24,0},{28,4},{1,9},{5... | collective-permute-start | bytes 4325384 | tf_op jit(solution)/shard_map/ppermute | solution.py:916
  879.6 172.1 %reduce-scatter.13.cloned.1.call-start = ((), (), s32[]{:S(2)}) async-start(), calls=%async_computation.37 | async-start | bytes 9437184 | tf_op jit(solution)/shard_map/reduce_scatter | solution.py:1138
  910.8 368.8 %reduce-scatter.17.cloned.1.call-start = ((), (), s32[]{:S(2)}) async-start(), calls=%async_computation.39 | async-start | bytes 2621440 | tf_op jit(solution)/shard_map/reduce_scatter | solution.py:1112
  938.7 351.7 %reduce-scatter.19.cloned.1.call-start = ((), (), s32[]{:S(2)}) async-start(), calls=%async_computation.40 | async-start | bytes 4718592 | tf_op jit(solution)/shard_map/reduce_scatter | solution.py:1138
  1020.0 289.7 %reduce-scatter.23.cloned.1.call-start = ((), (), s32[]{:S(2)}) async-start(), calls=%async_computation.42 | async-start | bytes 9437184 | tf_op jit(solution)/shard_map/reduce_scatter | solution.py:1138
  1049.5 99.5 %collective-permute-start.19 = (bf16[2,256,1408]{2,1,0:T(8,128)(2,1)S(1)}, bf16[2,256,1408]{2,1,0:T(8,128)(2,1)S(1)}, u32[]{:S(2)}, u32[]{:S(2)}) collective-permute-start(bf16[2,256,1408]{2,1,0:T(8,128)(2,1)S(1)} %copy-done.60), channel_id=1, source_target_pairs={{0,16},{4,20},{8,24},{12,28},{16,0},{20,4},{24,8},{28,12},{1,17},{... | collective-permute-start | bytes 4325384 | tf_op jit(solution)/shard_map/ppermute | solution.py:916
  1222.2 93.2 %reduce-scatter.21.cloned.1.call-start = ((), (), s32[]{:S(2)}) async-start(), calls=%async_computation.41 | async-start | bytes 147456 | tf_op jit(solution)/shard_map/reduce_scatter | solution.py:1225
  1240.2 106.7 %reduce-scatter.15.cloned.1.call-start = ((), (), s32[]{:S(2)}) async-start(), calls=%async_computation.38 | async-start | bytes 2621440 | tf_op jit(solution)/shard_map/reduce_scatter | solution.py:1112
  (104 other events, 1750.4 us)
Sparse Core Ops, SparseCore 0:
  9.6 83.4 all-gather.5
  94.7 80.5 all-gather.7
  177.5 124.5 all-gather.11
  357.0 80.0 all-gather.9
  760.9 48.1 reduce-scatter.10
  811.9 60.0 reduce-scatter.8
  910.9 87.1 reduce-scatter.12
  1001.0 42.1 reduce-scatter.16
  1046.2 97.4 reduce-scatter.18
  1146.0 105.0 reduce-scatter.22
  1253.4 49.3 reduce-scatter.20
  1305.0 41.9 reduce-scatter.14

commit v2 on v1

--- a/solution.py
+++ b/solution.py
@@ -412,24 +412,30 @@
     )(d_query, q_full, d_logits, router)
 
 
-def token_back(d_kv, kv_cols, d_pair, pick):
+def token_back(d_kv, kv_cols, d_pair, pick, rows, inverse):
     span, line = d_kv.shape
     width = kv_cols.shape[0]
     experts, slots, tokens = pick.shape
     step = min(512, width)
 
-    def kernel(dkv_ref, kv_ref, pair_ref, pick_ref, o_ref):
+    def kernel(dkv_ref, kv_ref, pair_ref, pick_ref, x_ref, inv_ref, o_ref, dg_ref):
         got = lax.dot_general(
             dkv_ref[...], kv_ref[...], (((1,), (1,)), ((), ())), preferred_element_type=f32
         )
+        gain = jnp.zeros((1, step), f32)
         for e in range(experts):
+            part = slice(e * tokens, (e + 1) * tokens)
             extra = lax.dot_general(
                 pick_ref[e],
                 pair_ref[e * slots : (e + 1) * slots, :],
                 (((0,), (0,)), ((), ())),
                 preferred_element_type=f32,
             )
-            o_ref[e] = (got[e * tokens : (e + 1) * tokens] + extra).astype(bf16)
+            d_a = got[part] + extra
+            o_ref[e] = d_a.astype(bf16)
+            scaled = x_ref[part, :].astype(f32) * inv_ref[part, :]
+            gain = gain + jnp.sum(d_a * scaled, axis=0, keepdims=True)
+        dg_ref[...] = gain
 
     return pl.pallas_call(
         kernel,
@@ -439,22 +445,29 @@
             pl.BlockSpec((step, line), lambda g: (g, 0)),
             pl.BlockSpec((experts * slots, step), lambda g: (0, g)),
             full_spec(pick.shape),
-        ],
-        out_specs=pl.BlockSpec((experts, tokens, step), lambda g: (0, 0, g)),
-        out_shape=jax.ShapeDtypeStruct((experts, tokens, width), bf16),
+            pl.BlockSpec((span, step), lambda g: (0, g)),
+            full_spec((span, 1)),
+        ],
+        out_specs=[
+            pl.BlockSpec((experts, tokens, step), lambda g: (0, 0, g)),
+            pl.BlockSpec((1, step), lambda g: (0, g)),
+        ],
+        out_shape=[
+            jax.ShapeDtypeStruct((experts, tokens, width), bf16),
+            jax.ShapeDtypeStruct((1, width), f32),
+        ],
         name="token_back",
         cost_estimate=work(2 * span * line * width, 2 * (line * width + 2 * span * width)),
-    )(d_kv, kv_cols, d_pair, pick)
-
-
-def input_back_kernel(got_ref, x_ref, gain_ref, dm_ref, gx_ref, dg_ref):
+    )(d_kv, kv_cols, d_pair, pick, rows, inverse)
+
+
+def input_back_kernel(got_ref, x_ref, gain_ref, dm_ref, gx_ref):
     d_a = got_ref[0].astype(f32)
     for e in range(1, got_ref.shape[0]):
         d_a = d_a + got_ref[e].astype(f32)
     x = x_ref[...].astype(f32)
     inverse = lax.rsqrt(jnp.mean(x * x, axis=1, keepdims=True) + norm_eps)
     scaled = d_a * gain_ref[...]
-    dg_ref[...] = jnp.sum(d_a * (x * inverse), axis=0, keepdims=True)
     mean = jnp.mean(scaled * x, axis=1, keepdims=True)
     gx_ref[...] = dm_ref[...] + (inverse * scaled - x * (inverse * inverse * inverse * mean))
 
@@ -463,10 +476,7 @@
     tokens, width = x.shape
     return pl.pallas_call(
         input_back_kernel,
-        out_shape=[
-            jax.ShapeDtypeStruct((tokens, width), f32),
-            jax.ShapeDtypeStruct((1, width), f32),
-        ],
+        out_shape=jax.ShapeDtypeStruct((tokens, width), f32),
         name="input_back",
         cost_estimate=work(10 * tokens * width, 20 * tokens * width),
     )(got, x, gain, d_middle)
@@ -773,22 +783,25 @@
     _, rows, part = got[0].shape
 
     def kernel(place_ref, *refs):
-        hop = (place_ref[0] - pl.program_id(1)) % stages
+        hop = (place_ref[0] - pl.program_id(0)) % stages
         for k in range(stages):
 
             @pl.when(hop == k)
             def _(ref=refs[k]):
-                refs[-1][...] = ref[...].astype(f32)
-
+                for half in range(2):
+                    refs[half - 2][0] = ref[half].astype(f32)
+
+    block = pl.BlockSpec((1, rows, part), lambda g, p: (0, 0, g))
+    shape = jax.ShapeDtypeStruct((1, rows, stages * part), f32)
     return pl.pallas_call(
         kernel,
         grid_spec=pltpu.PrefetchScalarGridSpec(
             num_scalar_prefetch=1,
-            grid=(2, stages),
-            in_specs=[pl.BlockSpec((1, rows, part), lambda w, g, p: (w, 0, 0))] * stages,
-            out_specs=pl.BlockSpec((1, rows, part), lambda w, g, p: (w, 0, g)),
+            grid=(stages,),
+            in_specs=[full_spec((2, rows, part))] * stages,
+            out_specs=[block, block],
         ),
-        out_shape=jax.ShapeDtypeStruct((2, rows, stages * part), f32),
+        out_shape=[shape, shape],
         name="widen",
         cost_estimate=work(0, 12 * stages * rows * part),
     )(place, *got)
@@ -992,8 +1005,10 @@
     router_a = jnp.pad(router[:, :experts], ((0, 0), (0, 128 - experts)))
     router_m = jnp.pad(router[:, experts:], ((0, 0), (0, 128 - experts)))
 
-    x_all = x_blocks.transpose(1, 0, 2, 3).reshape(MICRO, span, width).astype(f32)
-    a_all = (x_all * inverse_rms(x_all) * gain_1).astype(bf16)
+    x_low = x_blocks.transpose(1, 0, 2, 3).reshape(MICRO, span, width)
+    x_all = x_low.astype(f32)
+    x_inverse = inverse_rms(x_all)
+    a_all = (x_all * x_inverse * gain_1).astype(bf16)
 
     token = jnp.arange(tokens, dtype=jnp.int32)
     chosen = (routes_a[None] == place[:, None, None, None, None]).any(-1)
@@ -1074,16 +1089,29 @@
         queries[m] = exchange(q_out[m])
         heads, peaks[m] = attend(queries[m], query_pos[m], kvs[: m + 1], start)
         mixed_got[m] = exchange(heads)
+    gate_w, up_w = assemble(where, mine, [partner(piece) for piece in mine])
+    first_mixed = after(mixed_got[ORDER[0]], gate_w, heads)
+    gated = {}
     for m in ORDER:
-        attn[m], gated, mixed[m] = project_o(mixed_got[m], o_full, gate_a[m])
-        back = exchange(gated.reshape(experts, slots, width))
+        attn[m], gated[m], mixed[m] = project_o(
+            first_mixed if m == ORDER[0] else mixed_got[m], o_full, gate_a[m]
+        )
+
+    b_blocks = {}
+    for m in ORDER:
+        back = exchange(gated[m].reshape(experts, slots, width))
+        if m == ORDER[0]:
+            back = after(back, gated[ORDER[1]])
         middles[m], inverses[m], b_low = combine(
             back.reshape(routed, width), home_a[m], inputs[0, m], gain_2
         )
-        blocks = [along(b_low, k) for k in range(stages)]
-        feeds[m] = exchange(dispatch(blocks, home_m[m])(experts))
-    mine = list(lax.optimization_barrier((*mine, b_low)))[:-1]
-    gate_w, up_w = assemble(where, mine, [partner(piece) for piece in mine])
+        b_blocks[m] = [along(b_low, k) for k in range(stages)]
+    held = lax.optimization_barrier((*b_blocks[ORDER[0]], b_low))
+    b_blocks[ORDER[0]] = list(held[:stages])
+    for m in ORDER:
+        sent = dispatch(b_blocks[m], home_m[m])(experts)
+        feeds[m] = exchange(sent)
+    feeds[ORDER[0]] = after(feeds[ORDER[0]], sent)
 
     pairs = experts * stages * slots
     own_id = own.reshape(1).astype(jnp.int32)
@@ -1113,26 +1141,21 @@
             summed, "dp", scatter_dimension=0, tiled=True, axis_index_groups=same_core
         )[0]
 
+    early, d_pieces[ORDER[0]] = over_stages(after(d_rows[ORDER[0]], d_b), ORDER[0])
+    late, d_pieces[ORDER[1]] = over_stages(
+        after(d_rows[ORDER[1]], d_pieces[ORDER[0]]), ORDER[1]
+    )
+    out_rows = exchange(
+        after(outs[ORDER[0]], d_rows[ORDER[1]]).reshape(experts, stages, slots, width)
+    )
     gate_grad, up_grad, router_m_grad = feed_grads(
-        [feeds[m].reshape(pairs, width) for m in ORDER],
+        [after(feeds[m].reshape(pairs, width), d_pieces[ORDER[1]]) for m in ORDER],
         [kept_feed[m][1] for m in ORDER],
         [kept_feed[m][2] for m in ORDER],
         [kept_feed[m][4] for m in ORDER],
     )
-    early, d_pieces[ORDER[0]] = over_stages(after(d_rows[ORDER[0]], gate_grad), ORDER[0])
-    late, d_pieces[ORDER[1]] = over_stages(after(d_rows[ORDER[1]], early), ORDER[1])
-    down_grad = t_mm(after(joined(0), late), joined(3)).astype(bf16)
-    out_rows = exchange(
-        after(outs[ORDER[0]], d_rows[ORDER[1]]).reshape(experts, stages, slots, width)
-    )
-    out_sums = {ORDER[0]: over_stages(after(out_rows, late), ORDER[0])[1]}
-
-    other = partner(other_half(where, gate_grad, after(up_grad, late), stages))
-    total = list(own_half(where, gate_grad, up_grad, other))
-
-    total[1] = along(total[1], 1)
-    d_pieces[ORDER[0]] = after(d_pieces[ORDER[0]], total[0])
-    d_pieces[ORDER[1]] = after(d_pieces[ORDER[1]], total[1], down_grad)
+    summed, out_sum = over_stages(after(out_rows, d_pieces[ORDER[1]]), ORDER[0])
+    out_sums = {ORDER[0]: out_sum}
 
     def scattered(grad):
         return lax.psum_scatter(grad, "dp", scatter_dimension=0, tiled=True)
@@ -1150,6 +1173,8 @@
         if m == ORDER[0]:
             sent = after(sent, out_rows)
         got = exchange(sent.reshape(experts, slots, width)).reshape(routed, width)
+        if m == ORDER[0]:
+            got = after(got, gate_grad, summed)
         d_attn[m], d_heads, logit_grads[m] = back_o(
             got, attn[m], gate_a[m], rest_a[m], turn_a[m], o_full, experts
         )
@@ -1180,21 +1205,18 @@
     d_pairs[ORDER[1]] = after(d_pairs[ORDER[1]], q_grad)
     router_a_grad = t_mm(pair_rows, ordered(logit_grads))
     router_a_grad = router_a_grad[:, :experts] + router_a_grad[:, 128 : 128 + experts]
-    o_mine = scattered(o_grad)
-    kv_mine = scattered(kv_grad)
-    d_pairs[ORDER[1]] = after(d_pairs[ORDER[1]], o_mine)
-    for k in range(2, stages):
-        piece = after(total[k], q_grad) if k < 4 else after(total[k], total[k - 2])
-        total[k] = along(piece, k)
-    d_pairs[ORDER[1]] = after(d_pairs[ORDER[1]], *total[2:3])
-    if part % 128 == 0:
-        shares = widen(where, total)
-    else:
-        got = jnp.stack(total)[stage_order].astype(f32)
-        shares = jnp.concatenate([got[s] for s in range(stages)], axis=2)
-    gate_share, up_share = shares[:1], shares[1:]
+    o_in, out_sums[ORDER[0]] = lax.optimization_barrier((o_grad, out_sums[ORDER[0]]))
+    o_mine = scattered(o_in)
+    kv_in, o_mine = lax.optimization_barrier((kv_grad, o_mine))
+    kv_mine = scattered(kv_in)
+    q_in, kv_mine = lax.optimization_barrier((q_grad, kv_mine))
+    q_mine = scattered(q_in)
+    other = partner(other_half(where, gate_grad, after(up_grad, q_grad), stages))
+    total = list(own_half(where, gate_grad, up_grad, other))
+    own_ready = total[0]
+    total[1] = along(total[1], 1)
+    down_grad = t_mm(after(joined(0), own_ready), joined(3)).astype(bf16)
     o_share = o_mine.astype(f32)[None]
-    q_share = scattered(q_grad).astype(f32)[None]
     router_m_grad = router_m_grad[:, :experts] + router_m_grad[:, 128 : 128 + experts]
     down_split = down_grad.reshape(2, part // 2, width)
     down_share = (
@@ -1202,16 +1224,39 @@
     )[None]
 
 
-    gain_1_grad = jnp.zeros((1, width), f32)
+    d_pairs[ORDER[0]], total[0] = lax.optimization_barrier((d_pairs[ORDER[0]], total[0]))
+    d_pairs[ORDER[1]], total[1] = lax.optimization_barrier((d_pairs[ORDER[1]], total[1]))
+    for k in range(2, stages):
+        total[k] = along(after(total[k], total[k - 1] if k == 2 else total[k - 2]), k)
     grad_x = [None] * MICRO
+    d_as, gain_1_grad = {}, jnp.zeros((1, width), f32)
     for m in ORDER:
-        d_a = exchange(token_back(d_kvs[m], kv_cols, d_pairs[m], pick_a[m]))
-        grad_x[m], gain_part = input_back(d_a, inputs[0, m], gain_1, d_middles[m])
+        d_a, gain_part = token_back(
+            d_kvs[m], kv_cols, d_pairs[m], pick_a[m], x_low[m], x_inverse[m]
+        )
+        d_as[m] = exchange(d_a)
         gain_1_grad = gain_1_grad + gain_part
+    out_rows = exchange(
+        after(outs[ORDER[1]], d_query).reshape(experts, stages, slots, width)
+    )
+    summed = collect(out_rows, home_m[ORDER[1]], stage_order)
+    out_in, q_mine = lax.optimization_barrier((summed, q_mine))
+    out_sums[ORDER[1]] = lax.psum_scatter(
+        out_in, "dp", scatter_dimension=0, tiled=True, axis_index_groups=same_core
+    )[0]
+    for m in ORDER:
+        got = d_as[m]
+        if m == ORDER[0]:
+            got, total[2] = lax.optimization_barrier((got, total[2]))
+        grad_x[m] = input_back(got, inputs[0, m], gain_1, d_middles[m])
+    if part % 128 == 0:
+        gate_share, up_share = widen(where, total)
+    else:
+        got = jnp.stack(total)[stage_order].astype(f32)
+        shares = jnp.concatenate([got[s] for s in range(stages)], axis=2)
+        gate_share, up_share = shares[:1], shares[1:]
     grad_x = jnp.stack(grad_x)[None]
 
-    out_rows = exchange(after(outs[ORDER[1]], d_a).reshape(experts, stages, slots, width))
-    out_sums[ORDER[1]] = over_stages(out_rows, ORDER[1])[1]
     out_act = jnp.stack([middles[m] + out_sums[m].astype(f32) for m in range(MICRO)])
     out_act = out_act.astype(bf16)[None]
     kv_got = exchange(kv_mine.reshape(experts, rows_each, line)).reshape(experts, rows_each, 2, group)
@@ -1221,7 +1266,9 @@
         [router_a_grad.T, router_m_grad.T, gain_1_grad, gain_2_grad], axis=0
     )
     kinds = 2 * experts + 2
-    tail = jnp.pad(tail, ((0, -kinds % 8), (0, 0))).reshape(-1, dp_size, width // dp_size)
+    tail, q_mine = lax.optimization_barrier((jnp.pad(tail, ((0, -kinds % 8), (0, 0))), q_mine))
+    q_share = q_mine.astype(f32)[None]
+    tail = tail.reshape(-1, dp_size, width // dp_size)
     tail = lax.psum_scatter(
         tail.transpose(1, 0, 2), "dp", scatter_dimension=0, tiled=True
     )
@@ -1229,7 +1276,7 @@
     tail = lax.psum_scatter(tail, "expert", scatter_dimension=0, tiled=True)[0].T
     router_share, gains_share = tail[:, : 2 * experts], tail[:, 2 * experts : kinds]
 
-    largest = jnp.maximum(peaks[0], peaks[1])[:, :, 0, 0]
+    largest = after(jnp.maximum(peaks[0], peaks[1])[:, :, 0, 0], summed, grad_x)
     mine_here = jnp.arange(HEADS, dtype=jnp.int32) // (HEADS // experts) == own
     largest = jnp.where(mine_here[None], jnp.tile(largest, (1, experts)), masked_low)
     largest = jnp.pad(largest, ((0, 0), (0, 128 - HEADS)))

time: 1360 us -> 1350 us (level)
  waiting for transfers between devices: 491 us -> 417 us
  blocking collectives: 112 us -> 162 us
  starting transfers between devices: 120 us -> 138 us
    all_gather x1, waiting for transfers between devices: 87.3 us -> 26.3 us  [per_device(): kv_got = lax.all_gather(kv_rows, 'dp', axis=0)]
    all_to_all x3 -> x4, blocking collectives: 95 us -> 147 us  [exchange(): return lax.all_to_all(blocks, 'expert', 0, 0, tiled=True)]
    reduce_scatter x4 -> x3, waiting for transfers between devices: 45.5 us -> 0.02 us  [over_stages(): lax.psum_scatter(summed, 'dp', scatter_dimension=0, tiled=True, axis_inde...]
    ppermute x15, waiting for transfers between devices: 167 us -> 205 us  [along(): lax.ppermute(block, 'dp', [(j, (j // 2 + k) % stages * 2 + j % 2) for j i...]
    ppermute x5, starting transfers between devices: 3.49 us -> 35.4 us  [per_device(): lax.ppermute(largest, axis, [(j, j ^ hop) for j in range(size)])]
    ppermute x5, waiting for transfers between devices: 22.9 us -> 3.83 us  [per_device(): lax.ppermute(largest, axis, [(j, j ^ hop) for j in range(size)])]
    all_to_all x21 -> x20, waiting for transfers between devices: 131 us -> 136 us  [exchange(): return lax.all_to_all(blocks, 'expert', 0, 0, tiled=True)]
    all_to_all x21 -> x20, starting transfers between devices: 89.9 us -> 84.8 us  [exchange(): return lax.all_to_all(blocks, 'expert', 0, 0, tiled=True)]
  transfers between devices with their start and end apart: 60 -> 59, of which waited for: 27 -> 27; matrix products, arithmetic and copies ran while one was open for 14% -> 14% of each run, Pallas kernels for 29% -> 28%
where the time goes in v2:
time: 1350 us; the launch traced here: 1340 us
  waiting for transfers between devices  417 us (31%)
  Pallas kernels  397 us (29%)
  blocking collectives  162 us (12%)
  starting transfers between devices  138 us (10%)
  local copies, waits for them, and re-layouts  89.7 us (7%)
  other arithmetic  61.6 us (5%)
  matrix products  52.1 us (4%)
  between operations  24.2 us (2%)
    ppermute x15, waiting for transfers between devices, along(): lax.ppermute(block, 'dp', [(j, (j // 2 + k) % stages * 2 + j % 2) for j i...  205 us
    all_to_all x4, blocking collectives, exchange(): return lax.all_to_all(blocks, 'expert', 0, 0, tiled=True)  147 us
    all_to_all x20, waiting for transfers between devices, exchange(): return lax.all_to_all(blocks, 'expert', 0, 0, tiled=True)  136 us
    pallas_call x2, Pallas kernels, feed(): pl.pallas_call(feed_kernel, grid_spec=pltpu.PrefetchScalarGridSpec(num_sc...  106 us
    all_to_all x20, starting transfers between devices, exchange(): return lax.all_to_all(blocks, 'expert', 0, 0, tiled=True)  84.8 us
    dot_general x5, matrix products, t_mm(): lax.dot_general(left, right, (((0,), (0,)), ((), ())), preferred_element_...  44.1 us
    pallas_call x2, Pallas kernels, attend_back(): pl.pallas_call(kernel, grid_spec=pltpu.PrefetchScalarGridSpec(num_scalar_...  42.7 us
    pallas_call x1, Pallas kernels, feed_grads(): pl.pallas_call(kernel, grid=(width // step,), in_specs=[pl.BlockSpec((cou...  36 us
  transfers between devices with their start and end apart: 59, of which 27 were waited for; matrix products, arithmetic and copies ran while one was open for 14% of the time, Pallas kernels for 28%

profile of v2, /device:TPU:0, one launch (start us, length us, event | category | flops | bytes accessed | tf_op | source)
XLA Modules:
  0.0 1342.2 jit_solution(7339542397862510320)
XLA Ops:
  15.2 59.9 %all_to_all.120 = bf16[4,296,2048]{2,1,0:T(8,128)(2,1)} all-to-all(bf16[4,296,2048]{2,1,0:T(8,128)(2,1)S(1)} %pad_maximum_fusion.2), channel_id=1, replica_groups=mesh['dp'=8,'expert'=4] {'expert'}, dimensions={0} | all-to-all | bytes 9699328 | tf_op jit(solution)/shard_map/all_to_all | solution.py:921
  75.1 18.0 %all-gather.6.cloned.1.call-done = bf16[4,2,128,2048]{3,2,1,0:T(8,128)(2,1)} async-done(((bf16[1,2,128,2048]{3,2,1,0:T(8,128)(2,1)}), bf16[4,2,128,2048]{3,2,1,0:T(8,128)(2,1)}) %all-gather.6.cloned.1.call-update) | async-done | bytes 4194320 | tf_op jit(solution)/shard_map/all_gather | solution.py:965
  123.6 45.3 %all-to-all-done.1 = bf16[4,4,64,2048]{3,2,1,0:T(8,128)(2,1)} async-done(((bf16[4,4,64,2048]{3,2,1,0:T(8,128)(2,1)}), bf16[4,4,64,2048]{3,2,1,0:T(8,128)(2,1)}, u32[]{:S(2)}, u32[]{:S(2)}) %all-to-all-start.1) | async-done | bytes 4194336 | tf_op jit(solution)/shard_map/all_to_all | solution.py:921
  214.9 26.3 %all-gather.12.cloned.1.call-done = bf16[32,80,1024]{2,1,0:T(8,128)(2,1)} async-done(((bf16[4,80,1024]{2,1,0:T(8,128)(2,1)}), bf16[32,80,1024]{2,1,0:T(8,128)(2,1)}) %all-gather.12.cloned.1.call-update) | async-done | bytes 5242896 | tf_op jit(solution)/shard_map/all_gather | solution.py:981
  262.6 11.8 project_kv.1
  293.1 61.0 %collective-permute-done.5.refs_2_ = bf16[2,256,1408]{2,1,0:T(8,128)(2,1)} collective-permute-done((bf16[2,256,1408]{2,1,0:T(8,128)(2,1)}, bf16[2,256,1408]{2,1,0:T(8,128)(2,1)}, u32[]{:S(2)}, u32[]{:S(2)}) %collective-permute-start.5) | collective-permute-done | bytes 1441824 | tf_op jit(solution)/shard_map/ppermute | solution.py:929
  356.8 18.0 %all_to_all.121.q_ref = bf16[4,256,512]{2,1,0:T(8,128)(2,1)} all-to-all(bf16[4,256,512]{2,1,0:T(8,128)(2,1)S(1)} %get-tuple-element.283), channel_id=1, replica_groups=mesh['dp'=8,'expert'=4] {'expert'}, dimensions={0} | all-to-all | bytes 2097152 | tf_op jit(solution)/shard_map/all_to_all | solution.py:921
  383.9 14.5 %attend.3 = (bf16[4,256,512]{2,1,0:T(8,128)(2,1)}, f32[4,4,8,128]{3,2,1,0:T(8,128)}) custom-call(s32[1]{0:T(128)S(6)} %copy.235.start_ref, bf16[4,256,512]{2,1,0:T(8,128)(2,1)} %all_to_all.121.q_ref, s32[4,256,1]{2,1,0:T(8,128)} %squeeze.308.pos_ref, bf16[2,512,512]{2,1,0:T(8,128)(2,1)} %get-tuple-element.285.rest_0_, ...), custom_call_target="tpu_custom_call" | custom-call | flops 2147483648 | bytes 2097152 | tf_op jit(solution)/shard_map/attend/pallas_call | solution.py:180
  481.6 31.9 %collective-permute-done.15.refs_2_ = bf16[128,2048]{1,0:T(8,128)(2,1)S(1)} collective-permute-done((bf16[128,2048]{1,0:T(8,128)(2,1)}, bf16[128,2048]{1,0:T(8,128)(2,1)S(1)}, u32[]{:S(2)}, u32[]{:S(2)}) %collective-permute-start.15) | collective-permute-done | bytes 524320 | tf_op jit(solution)/shard_map/ppermute | solution.py:929
  543.0 35.5 %collective-permute-done.8.refs_2_ = bf16[128,2048]{1,0:T(8,128)(2,1)S(1)} collective-permute-done((bf16[128,2048]{1,0:T(8,128)(2,1)S(1)}, bf16[128,2048]{1,0:T(8,128)(2,1)S(1)}, u32[]{:S(2)}, u32[]{:S(2)}) %collective-permute-start.8) | collective-permute-done | bytes 524320 | tf_op jit(solution)/shard_map/ppermute | solution.py:929
  590.6 53.2 %feed.2 = (bf16[1024,2048]{1,0:T(8,128)(2,1)}, bf16[1024,2048]{1,0:T(8,128)(2,1)}, bf16[1024,1408]{1,0:T(8,128)(2,1)}, bf16[1024,1408]{1,0:T(8,128)(2,1)}, bf16[...) custom-call(s32[1]{0:T(128)} %bitcast.62.own_ref, ...), custom_call_target="tpu_custom_call" | custom-call | flops 35433480192 | bytes 46923776 | tf_op jit(solution)/shard_map/feed/pallas_call | solution.py:869
  648.9 53.2 %feed.3 = (bf16[1024,2048]{1,0:T(8,128)(2,1)}, bf16[1024,2048]{1,0:T(8,128)(2,1)}, bf16[1024,1408]{1,0:T(8,128)(2,1)}, bf16[1024,1408]{1,0:T(8,128)(2,1)}, bf16[...) custom-call(s32[1]{0:T(128)} %bitcast.62.own_ref, ...), custom_call_target="tpu_custom_call" | custom-call | flops 35433480192 | bytes 46923776 | tf_op jit(solution)/shard_map/feed/pallas_call | solution.py:869
  707.7 53.5 %all_to_all.122.rows_ref = bf16[4,4,64,2048]{3,2,1,0:T(8,128)(2,1)} all-to-all(bf16[4,4,64,2048]{3,2,1,0:T(8,128)(2,1)} %bitcast.298), channel_id=1, replica_groups=mesh['dp'=8,'expert'=4] {'expert'}, dimensions={0} | all-to-all | bytes 8388608 | tf_op jit(solution)/shard_map/all_to_all | solution.py:921
  776.4 41.4 %all-to-all-done.15.rows_ref = bf16[4,4,64,2048]{3,2,1,0:T(8,128)(2,1)} async-done(((bf16[4,4,64,2048]{3,2,1,0:T(8,128)(2,1)}), bf16[4,4,64,2048]{3,2,1,0:T(8,128)(2,1)}, u32[]{:S(2)}, u32[]{:S(2)}) %all-to-all-start.15) | async-done | bytes 4194336 | tf_op jit(solution)/shard_map/all_to_all | solution.py:921
  837.9 36.0 %feed_grads.1 = (bf16[2048,1408]{1,0:T(8,128)(2,1)}, bf16[2048,1408]{1,0:T(8,128)(2,1)}, f32[2048,256]{1,0:T(8,128)}) custom-call(bf16[1024,2048]{1,0:T(8,128)(2,1)} %bitcast.71.r_ref.refs_0_, bf16[1024,2048]{1,0:T(8,128)(2,1)} %bitcast.63.r_ref.refs_1_, bf16[1024,1408]{1,0:T(8,128)(2,1)} %get-tuple-element.186.refs_2_, ...), custom_call_target="tpu_custom_call" | custom-call | flops 23622320128 | bytes 31457280 | tf_op jit(solution)/shard_map/feed_grads/pallas_call | solution.py:648
  928.3 24.9 %attend_back.2 = (bf16[4,256,512]{2,1,0:T(8,128)(2,1)}, bf16[512,1024]{1,0:T(8,128)(2,1)}, f32[2,512,512]{2,1,0:T(8,128)}) custom-call(s32[1]{0:T(128)S(6)} %copy.235.start_ref, bf16[4,256,512]{2,1,0:T(8,128)(2,1)} %all_to_all.121.q_ref, bf16[4,256,512]{2,1,0:T(8,128)(2,1)} %copy-done.44, f32[4,256,128]{2,1,0:T(8,128)} %get-tuple-element.338.cos_ref, ...), custom_call_target="tpu_custom_call" | custom-call | flops 5368709120 | bytes 6291456 | tf_op jit(solution)/shard_map/attend_back/pallas_call | solution.py:269
  953.2 17.9 %attend_back.3 = (bf16[4,256,512]{2,1,0:T(8,128)(2,1)}, bf16[512,1024]{1,0:T(8,128)(2,1)}) custom-call(s32[1]{0:T(128)S(6)} %copy.235.start_ref, bf16[4,256,512]{2,1,0:T(8,128)(2,1)} %copy-done.42, bf16[4,256,512]{2,1,0:T(8,128)(2,1)} %all-to-all-done.14.dm_ref, f32[4,256,128]{2,1,0:T(8,128)} %get-tuple-element.337.cos_ref, ...), custom_call_target="tpu_custom_call" | custom-call | flops 2684354560 | bytes 6291456 | tf_op jit(solution)/shard_map/attend_back/pallas_call | solution.py:269
  987.1 15.5 %all_to_all.123.dq_ref = bf16[4,256,512]{2,1,0:T(8,128)(2,1)} all-to-all(bf16[4,256,512]{2,1,0:T(8,128)(2,1)S(1)} %copy-done.43), channel_id=1, replica_groups=mesh['dp'=8,'expert'=4] {'expert'}, dimensions={0} | all-to-all | bytes 2097152 | tf_op jit(solution)/shard_map/all_to_all | solution.py:921
  1077.7 20.4 %all-to-all-done.19.rows_ref = bf16[4,4,64,2048]{3,2,1,0:T(8,128)(2,1)} async-done(((bf16[4,4,64,2048]{3,2,1,0:T(8,128)(2,1)}), bf16[4,4,64,2048]{3,2,1,0:T(8,128)(2,1)}, u32[]{:S(2)}, u32[]{:S(2)}) %all-to-all-start.19) | async-done | bytes 4194336 | tf_op jit(solution)/shard_map/all_to_all | solution.py:921
  1101.7 16.5 %fusion.6 = bf16[1408,2048]{1,0:T(8,128)(2,1)S(1)} fusion(bf16[2048,1408]{1,0:T(8,128)(2,1)} %pad_maximum_fusion.1, bf16[1024,2048]{1,0:T(8,128)(2,1)} %get-tuple-element.252, bf16[1024,2048]{1,0:T(8,128)(2,1)} %get-tuple-element.251), kind=kOutput, calls=%fused_computation.10 | convolution fusion | flops 11830820864 | bytes 19922944 | tf_op jit(solution)/shard_map/dot_general | solution.py:33
  1122.5 14.4 %collective-permute-done.18.refs_1_ = bf16[2,256,1408]{2,1,0:T(8,128)(2,1)S(1)} collective-permute-done((bf16[2,256,1408]{2,1,0:T(8,128)(2,1)}, bf16[2,256,1408]{2,1,0:T(8,128)(2,1)S(1)}, u32[]{:S(2)}, u32[]{:S(2)}) %collective-permute-start.18) | collective-permute-done | bytes 1441824 | tf_op jit(solution)/shard_map/ppermute | solution.py:929
  1162.9 56.7 %collective-permute-done.19.refs_2_ = bf16[2,256,1408]{2,1,0:T(8,128)(2,1)} collective-permute-done((bf16[2,256,1408]{2,1,0:T(8,128)(2,1)}, bf16[2,256,1408]{2,1,0:T(8,128)(2,1)}, u32[]{:S(2)}, u32[]{:S(2)}) %collective-permute-start.19) | collective-permute-done | bytes 1441824 | tf_op jit(solution)/shard_map/ppermute | solution.py:929
  1233.3 29.0 %collective-permute-start.23 = (f32[4,128]{1,0:T(4,128)S(1)}, f32[4,128]{1,0:T(4,128)S(1)}, u32[]{:S(2)}, u32[]{:S(2)}) collective-permute-start(f32[4,128]{1,0:T(4,128)S(1)} %pad_maximum_fusion.9), channel_id=1, source_target_pairs={{0,8},{4,12},{8,0},{12,4},{16,24},{20,28},{24,16},{28,20},{1,9},{5... | collective-permute-start | bytes 6152 | tf_op jit(solution)/shard_map/ppermute | solution.py:1287
  1308.5 15.4 %all-reduce.7 = f32[4,16,64]{2,1,0:T(8,128)S(1)} all-reduce(f32[4,16,64]{2,1,0:T(8,128)S(1)} %copy.201), channel_id=11, replica_groups=mesh['dp'=8,'expert'=4] {'expert'}, use_global_device_ids=true, to_apply=%region_15.16.clone | all-reduce | flops 4096 | bytes 32768
  (467 shorter events, 547.8 us)
Async XLA Ops:
  7.2 85.9 %all-gather.6.cloned.1.call-start = ((), (), s32[]{:S(2)}) async-start(), calls=%async_computation.32 | async-start | bytes 5242880 | tf_op jit(solution)/shard_map/all_gather | solution.py:965
  7.9 167.4 %all-gather.8.cloned.1.call-start = ((), (), s32[]{:S(2)}) async-start(), calls=%async_computation.33 | async-start | bytes 9437184 | tf_op jit(solution)/shard_map/all_gather | solution.py:975
  122.2 119.0 %all-gather.12.cloned.1.call-start = ((), (), s32[]{:S(2)}) async-start(), calls=%async_computation.43 | async-start | bytes 5898240 | tf_op jit(solution)/shard_map/all_gather | solution.py:981
  206.8 86.3 %all-to-all-start.4 = ((bf16[4,4,64,2048]{3,2,1,0:T(8,128)(2,1)}), bf16[4,4,64,2048]{3,2,1,0:T(8,128)(2,1)}, u32[]{:S(2)}, u32[]{:S(2)}) async-start(bf16[4,4,64,2048]{3,2,1,0:T(8,128)(2,1)} %dispatch.5), calls=%async_computation.4 | async-start | bytes 8388608 | tf_op jit(solution)/shard_map/all_to_all | solution.py:921
  211.7 222.8 %all-gather.10.cloned.1.call-start = ((), (), s32[]{:S(2)}) async-start(), calls=%async_computation.34 | async-start | bytes 9437184 | tf_op jit(solution)/shard_map/all_gather | solution.py:1085
  211.8 81.3 %collective-permute-start.6 = (bf16[2,256,1408]{2,1,0:T(8,128)(2,1)}, bf16[2,256,1408]{2,1,0:T(8,128)(2,1)}, u32[]{:S(2)}, u32[]{:S(2)}) collective-permute-start(bf16[2,256,1408]{2,1,0:T(8,128)(2,1)} %get-tuple-element.144), channel_id=1, source_target_pairs={{0,24},{4,28},{8,0},{12,4},{16,8},{20,12},{24,16},{28,20},{1,25},{... | collective-permute-start | bytes 4325384 | tf_op jit(solution)/shard_map/ppermute | solution.py:929
  211.9 142.2 %collective-permute-start.5 = (bf16[2,256,1408]{2,1,0:T(8,128)(2,1)}, bf16[2,256,1408]{2,1,0:T(8,128)(2,1)}, u32[]{:S(2)}, u32[]{:S(2)}) collective-permute-start(bf16[2,256,1408]{2,1,0:T(8,128)(2,1)} %get-tuple-element.142), channel_id=1, source_target_pairs={{0,16},{4,20},{8,24},{12,28},{16,0},{20,4},{24,8},{28,12},{1,17},{... | collective-permute-start | bytes 4325384 | tf_op jit(solution)/shard_map/ppermute | solution.py:929
  212.5 141.6 %collective-permute-start.4 = (bf16[2,256,1408]{2,1,0:T(8,128)(2,1)}, bf16[2,256,1408]{2,1,0:T(8,128)(2,1)}, u32[]{:S(2)}, u32[]{:S(2)}) collective-permute-start(bf16[2,256,1408]{2,1,0:T(8,128)(2,1)} %get-tuple-element.140), channel_id=1, source_target_pairs={{0,8},{4,12},{8,16},{12,20},{16,24},{20,28},{24,0},{28,4},{1,9},{5... | collective-permute-start | bytes 4325384 | tf_op jit(solution)/shard_map/ppermute | solution.py:929
  519.7 65.6 %all-to-all-start.10 = ((bf16[4,4,64,2048]{3,2,1,0:T(8,128)(2,1)}), bf16[4,4,64,2048]{3,2,1,0:T(8,128)(2,1)}, u32[]{:S(2)}, u32[]{:S(2)}) async-start(bf16[4,4,64,2048]{3,2,1,0:T(8,128)(2,1)} %dispatch.7), calls=%async_computation.10 | async-start | bytes 8388608 | tf_op jit(solution)/shard_map/all_to_all | solution.py:921
  585.4 58.5 %all-to-all-start.6 = ((bf16[4,4,64,2048]{3,2,1,0:T(8,128)(2,1)}), bf16[4,4,64,2048]{3,2,1,0:T(8,128)(2,1)}, u32[]{:S(2)}, u32[]{:S(2)}) async-start(bf16[4,4,64,2048]{3,2,1,0:T(8,128)(2,1)} %dispatch.6), calls=%async_computation.6 | async-start | bytes 8388608 | tf_op jit(solution)/shard_map/all_to_all | solution.py:921
  643.8 58.3 %all-to-all-start.12 = ((bf16[4,4,64,2048]{3,2,1,0:T(8,128)(2,1)}), bf16[4,4,64,2048]{3,2,1,0:T(8,128)(2,1)}, u32[]{:S(2)}, u32[]{:S(2)}) async-start(bf16[4,4,64,2048]{3,2,1,0:T(8,128)(2,1)} %bitcast.297), calls=%async_computation.12 | async-start | bytes 8388608 | tf_op jit(solution)/shard_map/all_to_all | solution.py:921
  648.7 112.5 %reduce-scatter.9.cloned.1.call-start = ((), (), s32[]{:S(2)}) async-start(), calls=%async_computation.35 | async-start | bytes 2621440 | tf_op jit(solution)/shard_map/reduce_scatter | solution.py:1140
  707.7 113.9 %reduce-scatter.11.cloned.1.call-start = ((), (), s32[]{:S(2)}) async-start(), calls=%async_computation.36 | async-start | bytes 2621440 | tf_op jit(solution)/shard_map/reduce_scatter | solution.py:1140
  821.3 77.4 %reduce-scatter.13.cloned.1.call-start = ((), (), s32[]{:S(2)}) async-start(), calls=%async_computation.37 | async-start | bytes 2621440 | tf_op jit(solution)/shard_map/reduce_scatter | solution.py:1140
  837.9 149.2 %reduce-scatter.15.cloned.1.call-start = ((), (), s32[]{:S(2)}) async-start(), calls=%async_computation.38 | async-start | bytes 9437184 | tf_op jit(solution)/shard_map/reduce_scatter | solution.py:1161
  920.7 117.7 %reduce-scatter.17.cloned.1.call-start = ((), (), s32[]{:S(2)}) async-start(), calls=%async_computation.39 | async-start | bytes 4718592 | tf_op jit(solution)/shard_map/reduce_scatter | solution.py:1161
  1006.2 221.1 %reduce-scatter.19.cloned.1.call-start = ((), (), s32[]{:S(2)}) async-start(), calls=%async_computation.40 | async-start | bytes 9437184 | tf_op jit(solution)/shard_map/reduce_scatter | solution.py:1161
  1069.6 67.3 %collective-permute-start.18 = (bf16[2,256,1408]{2,1,0:T(8,128)(2,1)}, bf16[2,256,1408]{2,1,0:T(8,128)(2,1)S(1)}, u32[]{:S(2)}, u32[]{:S(2)}) collective-permute-start(bf16[2,256,1408]{2,1,0:T(8,128)(2,1)} %get-tuple-element.219), channel_id=1, source_target_pairs={{0,8},{4,12},{8,16},{12,20},{16,24},{20,28},{24,0},{28,4},{1,9},{5... | collective-permute-start | bytes 4325384 | tf_op jit(solution)/shard_map/ppermute | solution.py:929
  1122.5 151.4 %collective-permute-start.21 = (bf16[704,2048]{1,0:T(8,128)(2,1)}, bf16[704,2048]{1,0:T(8,128)(2,1)}, u32[]{:S(2)}, u32[]{:S(2)}) collective-permute-start(bf16[704,2048]{1,0:T(8,128)(2,1)} %dynamic-slice_bitcast_fusion), channel_id=1, source_target_pairs={{0,4},{4,0},{8,12},{12,8},{16,20},{20,16},{24,28},{28,24},{1,5},{5... | collective-permute-start | bytes 8650760 | tf_op jit(solution)/shard_map/ppermute | solution.py:934
  1144.9 78.5 %all-to-all-start.21 = ((bf16[4,128,2048]{2,1,0:T(8,128)(2,1)}), bf16[4,128,2048]{2,1,0:T(8,128)(2,1)}, u32[]{:S(2)}, u32[]{:S(2)}) async-start(bf16[4,128,2048]{2,1,0:T(8,128)(2,1)} %get-tuple-element.221), calls=%async_computation.28 | async-start | bytes 4194304 | tf_op jit(solution)/shard_map/all_to_all | solution.py:921
  1149.5 158.2 %reduce-scatter.23.cloned.1.call-start = ((), (), s32[]{:S(2)}) async-start(), calls=%async_computation.42 | async-start | bytes 147456 | tf_op jit(solution)/shard_map/reduce_scatter | solution.py:1272
  1149.5 70.1 %collective-permute-start.19 = (bf16[2,256,1408]{2,1,0:T(8,128)(2,1)}, bf16[2,256,1408]{2,1,0:T(8,128)(2,1)}, u32[]{:S(2)}, u32[]{:S(2)}) collective-permute-start(bf16[2,256,1408]{2,1,0:T(8,128)(2,1)} %get-tuple-element.229), channel_id=1, source_target_pairs={{0,16},{4,20},{8,24},{12,28},{16,0},{20,4},{24,8},{28,12},{1,17},{... | collective-permute-start | bytes 4325384 | tf_op jit(solution)/shard_map/ppermute | solution.py:929
  1161.2 119.1 %collective-permute-start.20 = (bf16[2,256,1408]{2,1,0:T(8,128)(2,1)}, bf16[2,256,1408]{2,1,0:T(8,128)(2,1)S(1)}, u32[]{:S(2)}, u32[]{:S(2)}) collective-permute-start(bf16[2,256,1408]{2,1,0:T(8,128)(2,1)} %get-tuple-element.245), channel_id=1, source_target_pairs={{0,24},{4,28},{8,0},{12,4},{16,8},{20,12},{24,16},{28,20},{1,25},{... | collective-permute-start | bytes 4325384 | tf_op jit(solution)/shard_map/ppermute | solution.py:929
  1228.9 103.9 %reduce-scatter.21.cloned.1.call-start = ((), (), s32[]{:S(2)}) async-start(), calls=%async_computation.41 | async-start | bytes 2621440 | tf_op jit(solution)/shard_map/reduce_scatter | solution.py:1244
  (106 other events, 1787.2 us)
Sparse Core Ops, SparseCore 0:
  9.6 83.4 all-gather.5
  94.7 80.6 all-gather.7
  177.6 63.5 all-gather.11
  354.2 80.1 all-gather.9
  707.8 42.5 reduce-scatter.8
  766.8 40.5 reduce-scatter.10
  827.3 42.4 reduce-scatter.12
  898.8 88.1 reduce-scatter.14
  990.0 48.3 reduce-scatter.16
  1040.7 124.9 reduce-scatter.18
  1229.0 59.5 reduce-scatter.22
  1290.8 41.9 reduce-scatter.20

commit v3 on v2

--- a/solution.py
+++ b/solution.py
@@ -946,7 +946,7 @@
     )
     length = small.shape[0]
     line = 2 * group
-    extra = -(-length // (16 * line)) * 16
+    extra = -(-length // (8 * line)) * 8
     small = jnp.pad(small, (0, extra * line - length)).reshape(1, extra, line)
     kv_split = kv_weight.reshape(rows_each, 2, experts, group).transpose(2, 0, 1, 3)
     first = jnp.concatenate(
@@ -1148,12 +1148,6 @@
     out_rows = exchange(
         after(outs[ORDER[0]], d_rows[ORDER[1]]).reshape(experts, stages, slots, width)
     )
-    gate_grad, up_grad, router_m_grad = feed_grads(
-        [after(feeds[m].reshape(pairs, width), d_pieces[ORDER[1]]) for m in ORDER],
-        [kept_feed[m][1] for m in ORDER],
-        [kept_feed[m][2] for m in ORDER],
-        [kept_feed[m][4] for m in ORDER],
-    )
     summed, out_sum = over_stages(after(out_rows, d_pieces[ORDER[1]]), ORDER[0])
     out_sums = {ORDER[0]: out_sum}
 
@@ -1174,7 +1168,7 @@
             sent = after(sent, out_rows)
         got = exchange(sent.reshape(experts, slots, width)).reshape(routed, width)
         if m == ORDER[0]:
-            got = after(got, gate_grad, summed)
+            got = after(got, summed)
         d_attn[m], d_heads, logit_grads[m] = back_o(
             got, attn[m], gate_a[m], rest_a[m], turn_a[m], o_full, experts
         )
@@ -1211,7 +1205,13 @@
     kv_mine = scattered(kv_in)
     q_in, kv_mine = lax.optimization_barrier((q_grad, kv_mine))
     q_mine = scattered(q_in)
-    other = partner(other_half(where, gate_grad, after(up_grad, q_grad), stages))
+    gate_grad, up_grad, router_m_grad = feed_grads(
+        [after(feeds[m].reshape(pairs, width), q_grad) for m in ORDER],
+        [kept_feed[m][1] for m in ORDER],
+        [kept_feed[m][2] for m in ORDER],
+        [kept_feed[m][4] for m in ORDER],
+    )
+    other = partner(other_half(where, gate_grad, up_grad, stages))
     total = list(own_half(where, gate_grad, up_grad, other))
     own_ready = total[0]
     total[1] = along(total[1], 1)

time: 1350 us -> 1340 us (level)
  waiting for transfers between devices: 417 us -> 362 us
  blocking collectives: 162 us -> 214 us
    all_to_all x4 -> x5, blocking collectives: 147 us -> 199 us  [exchange(): return lax.all_to_all(blocks, 'expert', 0, 0, tiled=True)]
    all_to_all x20 -> x19, waiting for transfers between devices: 136 us -> 104 us  [exchange(): return lax.all_to_all(blocks, 'expert', 0, 0, tiled=True)]
    ppermute x15, waiting for transfers between devices: 205 us -> 190 us  [along(): lax.ppermute(block, 'dp', [(j, (j // 2 + k) % stages * 2 + j % 2) for j i...]
    all_to_all x20 -> x19, starting transfers between devices: 84.8 us -> 79.2 us  [exchange(): return lax.all_to_all(blocks, 'expert', 0, 0, tiled=True)]
  transfers between devices with their start and end apart: 59 -> 58, of which waited for: 27 -> 26; matrix products, arithmetic and copies ran while one was open for 14% -> 14% of each run, Pallas kernels for 28% -> 28%
where the time goes in v3:
time: 1340 us; the launch traced here: 1330 us
  Pallas kernels  398 us (30%)
  waiting for transfers between devices  362 us (27%)
  blocking collectives  214 us (16%)
  starting transfers between devices  135 us (10%)
  local copies, waits for them, and re-layouts  87.3 us (7%)
  other arithmetic  61.7 us (5%)
  matrix products  52.3 us (4%)
  between operations  24.2 us (2%)
    all_to_all x5, blocking collectives, exchange(): return lax.all_to_all(blocks, 'expert', 0, 0, tiled=True)  199 us
    ppermute x15, waiting for transfers between devices, along(): lax.ppermute(block, 'dp', [(j, (j // 2 + k) % stages * 2 + j % 2) for j i...  190 us
    pallas_call x2, Pallas kernels, feed(): pl.pallas_call(feed_kernel, grid_spec=pltpu.PrefetchScalarGridSpec(num_sc...  106 us
    all_to_all x19, waiting for transfers between devices, exchange(): return lax.all_to_all(blocks, 'expert', 0, 0, tiled=True)  104 us
    all_to_all x19, starting transfers between devices, exchange(): return lax.all_to_all(blocks, 'expert', 0, 0, tiled=True)  79.2 us
    dot_general x5, matrix products, t_mm(): lax.dot_general(left, right, (((0,), (0,)), ((), ())), preferred_element_...  44.2 us
    pallas_call x2, Pallas kernels, attend_back(): pl.pallas_call(kernel, grid_spec=pltpu.PrefetchScalarGridSpec(num_scalar_...  43.1 us
    ppermute x5, starting transfers between devices, per_device(): lax.ppermute(largest, axis, [(j, j ^ hop) for j in range(size)])  36.3 us
  transfers between devices with their start and end apart: 58, of which 26 were waited for; matrix products, arithmetic and copies ran while one was open for 14% of the time, Pallas kernels for 28%

profile of v3, /device:TPU:0, one launch (start us, length us, event | category | flops | bytes accessed | tf_op | source)
XLA Modules:
  0.0 1334.0 jit_solution(5312404219675377282)
XLA Ops:
  15.3 59.9 %all_to_all.120 = bf16[4,292,2048]{2,1,0:T(8,128)(2,1)} all-to-all(bf16[4,292,2048]{2,1,0:T(8,128)(2,1)S(1)} %pad_maximum_fusion.2), channel_id=1, replica_groups=mesh['dp'=8,'expert'=4] {'expert'}, dimensions={0} | all-to-all | bytes 9568256 | tf_op jit(solution)/shard_map/all_to_all | solution.py:921
  75.2 17.9 %all-gather.6.cloned.1.call-done = bf16[4,2,128,2048]{3,2,1,0:T(8,128)(2,1)} async-done(((bf16[1,2,128,2048]{3,2,1,0:T(8,128)(2,1)}), bf16[4,2,128,2048]{3,2,1,0:T(8,128)(2,1)}) %all-gather.6.cloned.1.call-update) | async-done | bytes 4194320 | tf_op jit(solution)/shard_map/all_gather | solution.py:965
  123.8 45.1 %all-to-all-done.1 = bf16[4,4,64,2048]{3,2,1,0:T(8,128)(2,1)} async-done(((bf16[4,4,64,2048]{3,2,1,0:T(8,128)(2,1)}), bf16[4,4,64,2048]{3,2,1,0:T(8,128)(2,1)}, u32[]{:S(2)}, u32[]{:S(2)}) %all-to-all-start.1) | async-done | bytes 4194336 | tf_op jit(solution)/shard_map/all_to_all | solution.py:921
  214.4 18.4 %all-gather.12.cloned.1.call-done = bf16[32,72,1024]{2,1,0:T(8,128)(2,1)} async-done(((bf16[4,72,1024]{2,1,0:T(8,128)(2,1)}), bf16[32,72,1024]{2,1,0:T(8,128)(2,1)}) %all-gather.12.cloned.1.call-update) | async-done | bytes 4718608 | tf_op jit(solution)/shard_map/all_gather | solution.py:981
  253.6 11.8 project_kv.1
  284.2 65.6 %collective-permute-done.5.refs_2_ = bf16[2,256,1408]{2,1,0:T(8,128)(2,1)} collective-permute-done((bf16[2,256,1408]{2,1,0:T(8,128)(2,1)}, bf16[2,256,1408]{2,1,0:T(8,128)(2,1)}, u32[]{:S(2)}, u32[]{:S(2)}) %collective-permute-start.5) | collective-permute-done | bytes 1441824 | tf_op jit(solution)/shard_map/ppermute | solution.py:929
  352.5 17.9 %all_to_all.121.q_ref = bf16[4,256,512]{2,1,0:T(8,128)(2,1)} all-to-all(bf16[4,256,512]{2,1,0:T(8,128)(2,1)S(1)} %get-tuple-element.281), channel_id=1, replica_groups=mesh['dp'=8,'expert'=4] {'expert'}, dimensions={0} | all-to-all | bytes 2097152 | tf_op jit(solution)/shard_map/all_to_all | solution.py:921
  379.5 14.5 %attend.3 = (bf16[4,256,512]{2,1,0:T(8,128)(2,1)}, f32[4,4,8,128]{3,2,1,0:T(8,128)}) custom-call(s32[1]{0:T(128)S(6)} %copy.235.start_ref, bf16[4,256,512]{2,1,0:T(8,128)(2,1)} %all_to_all.121.q_ref, s32[4,256,1]{2,1,0:T(8,128)} %squeeze.308.pos_ref, bf16[2,512,512]{2,1,0:T(8,128)(2,1)} %get-tuple-element.283.rest_0_, ...), custom_call_target="tpu_custom_call" | custom-call | flops 2147483648 | bytes 2097152 | tf_op jit(solution)/shard_map/attend/pallas_call | solution.py:180
  477.3 31.9 %collective-permute-done.15.refs_2_ = bf16[128,2048]{1,0:T(8,128)(2,1)S(1)} collective-permute-done((bf16[128,2048]{1,0:T(8,128)(2,1)}, bf16[128,2048]{1,0:T(8,128)(2,1)S(1)}, u32[]{:S(2)}, u32[]{:S(2)}) %collective-permute-start.15) | collective-permute-done | bytes 524320 | tf_op jit(solution)/shard_map/ppermute | solution.py:929
  538.9 35.5 %collective-permute-done.8.refs_2_ = bf16[128,2048]{1,0:T(8,128)(2,1)S(1)} collective-permute-done((bf16[128,2048]{1,0:T(8,128)(2,1)S(1)}, bf16[128,2048]{1,0:T(8,128)(2,1)S(1)}, u32[]{:S(2)}, u32[]{:S(2)}) %collective-permute-start.8) | collective-permute-done | bytes 524320 | tf_op jit(solution)/shard_map/ppermute | solution.py:929
  586.3 53.2 %feed.2 = (bf16[1024,2048]{1,0:T(8,128)(2,1)}, bf16[1024,2048]{1,0:T(8,128)(2,1)}, bf16[1024,1408]{1,0:T(8,128)(2,1)}, bf16[1024,1408]{1,0:T(8,128)(2,1)}, bf16[...) custom-call(s32[1]{0:T(128)} %bitcast.62.own_ref, ...), custom_call_target="tpu_custom_call" | custom-call | flops 35433480192 | bytes 46923776 | tf_op jit(solution)/shard_map/feed/pallas_call | solution.py:869
  644.9 53.2 %feed.3 = (bf16[1024,2048]{1,0:T(8,128)(2,1)}, bf16[1024,2048]{1,0:T(8,128)(2,1)}, bf16[1024,1408]{1,0:T(8,128)(2,1)}, bf16[1024,1408]{1,0:T(8,128)(2,1)}, bf16[...) custom-call(s32[1]{0:T(128)} %bitcast.62.own_ref, ...), custom_call_target="tpu_custom_call" | custom-call | flops 35433480192 | bytes 46923776 | tf_op jit(solution)/shard_map/feed/pallas_call | solution.py:869
  703.7 53.5 %all_to_all.122.rows_ref = bf16[4,4,64,2048]{3,2,1,0:T(8,128)(2,1)} all-to-all(bf16[4,4,64,2048]{3,2,1,0:T(8,128)(2,1)} %bitcast.298), channel_id=1, replica_groups=mesh['dp'=8,'expert'=4] {'expert'}, dimensions={0} | all-to-all | bytes 8388608 | tf_op jit(solution)/shard_map/all_to_all | solution.py:921
  762.8 52.2 %all_to_all.123.rows_ref = bf16[4,4,64,2048]{3,2,1,0:T(8,128)(2,1)} all-to-all(bf16[4,4,64,2048]{3,2,1,0:T(8,128)(2,1)} %bitcast.296), channel_id=1, replica_groups=mesh['dp'=8,'expert'=4] {'expert'}, dimensions={0} | all-to-all | bytes 8388608 | tf_op jit(solution)/shard_map/all_to_all | solution.py:921
  878.2 11.9 all-to-all-done.17.dm_ref
  902.4 24.9 %attend_back.2 = (bf16[4,256,512]{2,1,0:T(8,128)(2,1)}, bf16[512,1024]{1,0:T(8,128)(2,1)}, f32[2,512,512]{2,1,0:T(8,128)}) custom-call(s32[1]{0:T(128)S(6)} %copy.235.start_ref, bf16[4,256,512]{2,1,0:T(8,128)(2,1)} %all_to_all.121.q_ref, bf16[4,256,512]{2,1,0:T(8,128)(2,1)} %copy-done.45, f32[4,256,128]{2,1,0:T(8,128)} %get-tuple-element.336.cos_ref, ...), custom_call_target="tpu_custom_call" | custom-call | flops 5368709120 | bytes 6291456 | tf_op jit(solution)/shard_map/attend_back/pallas_call | solution.py:269
  927.3 18.2 %attend_back.3 = (bf16[4,256,512]{2,1,0:T(8,128)(2,1)}, bf16[512,1024]{1,0:T(8,128)(2,1)}) custom-call(s32[1]{0:T(128)S(6)} %copy.235.start_ref, bf16[4,256,512]{2,1,0:T(8,128)(2,1)} %copy-done.43, bf16[4,256,512]{2,1,0:T(8,128)(2,1)} %all-to-all-done.14.dm_ref, f32[4,256,128]{2,1,0:T(8,128)} %get-tuple-element.335.cos_ref, ...), custom_call_target="tpu_custom_call" | custom-call | flops 2684354560 | bytes 6291456 | tf_op jit(solution)/shard_map/attend_back/pallas_call | solution.py:269
  960.3 15.5 %all_to_all.124.dq_ref = bf16[4,256,512]{2,1,0:T(8,128)(2,1)} all-to-all(bf16[4,256,512]{2,1,0:T(8,128)(2,1)S(1)} %copy-done.44), channel_id=1, replica_groups=mesh['dp'=8,'expert'=4] {'expert'}, dimensions={0} | all-to-all | bytes 2097152 | tf_op jit(solution)/shard_map/all_to_all | solution.py:921
  1011.6 35.9 %feed_grads.1 = (bf16[2048,1408]{1,0:T(8,128)(2,1)}, bf16[2048,1408]{1,0:T(8,128)(2,1)}, f32[2048,256]{1,0:T(8,128)}) custom-call(bf16[1024,2048]{1,0:T(8,128)(2,1)} %bitcast.71.r_ref.refs_0_, bf16[1024,2048]{1,0:T(8,128)(2,1)} %bitcast.63.r_ref.refs_1_, bf16[1024,1408]{1,0:T(8,128)(2,1)} %get-tuple-element.210.refs_2_, ...), custom_call_target="tpu_custom_call" | custom-call | flops 23622320128 | bytes 31457280 | tf_op jit(solution)/shard_map/feed_grads/pallas_call | solution.py:648
  1086.5 20.7 %all-to-all-done.19.rows_ref = bf16[4,4,64,2048]{3,2,1,0:T(8,128)(2,1)} async-done(((bf16[4,4,64,2048]{3,2,1,0:T(8,128)(2,1)}), bf16[4,4,64,2048]{3,2,1,0:T(8,128)(2,1)}, u32[]{:S(2)}, u32[]{:S(2)}) %all-to-all-start.19) | async-done | bytes 4194336 | tf_op jit(solution)/shard_map/all_to_all | solution.py:921
  1111.0 16.5 %fusion.6 = bf16[1408,2048]{1,0:T(8,128)(2,1)S(1)} fusion(bf16[2048,1408]{1,0:T(8,128)(2,1)} %pad_maximum_fusion.1, bf16[1024,2048]{1,0:T(8,128)(2,1)} %get-tuple-element.250, bf16[1024,2048]{1,0:T(8,128)(2,1)} %get-tuple-element.249), kind=kOutput, calls=%fused_computation.10 | convolution fusion | flops 11830820864 | bytes 19922944 | tf_op jit(solution)/shard_map/dot_general | solution.py:33
  1159.5 51.0 %collective-permute-done.19.refs_2_ = bf16[2,256,1408]{2,1,0:T(8,128)(2,1)S(1)} collective-permute-done((bf16[2,256,1408]{2,1,0:T(8,128)(2,1)}, bf16[2,256,1408]{2,1,0:T(8,128)(2,1)S(1)}, u32[]{:S(2)}, u32[]{:S(2)}) %collective-permute-start.19) | collective-permute-done | bytes 1441824 | tf_op jit(solution)/shard_map/ppermute | solution.py:929
  1224.8 28.9 %collective-permute-start.23 = (f32[4,128]{1,0:T(4,128)S(1)}, f32[4,128]{1,0:T(4,128)S(1)}, u32[]{:S(2)}, u32[]{:S(2)}) collective-permute-start(f32[4,128]{1,0:T(4,128)S(1)} %pad_maximum_fusion.9), channel_id=1, source_target_pairs={{0,8},{4,12},{8,0},{12,4},{16,24},{20,28},{24,16},{28,20},{1,9},{5... | collective-permute-start | bytes 6152 | tf_op jit(solution)/shard_map/ppermute | solution.py:1287
  1299.3 15.4 %all-reduce.7 = f32[4,16,64]{2,1,0:T(8,128)S(1)} all-reduce(f32[4,16,64]{2,1,0:T(8,128)S(1)} %copy.201), channel_id=11, replica_groups=mesh['dp'=8,'expert'=4] {'expert'}, use_global_device_ids=true, to_apply=%region_15.16.clone | all-reduce | flops 4096 | bytes 32768
  (468 shorter events, 540.2 us)
Async XLA Ops:
  7.2 85.9 %all-gather.6.cloned.1.call-start = ((), (), s32[]{:S(2)}) async-start(), calls=%async_computation.32 | async-start | bytes 5242880 | tf_op jit(solution)/shard_map/all_gather | solution.py:965
  7.9 167.4 %all-gather.8.cloned.1.call-start = ((), (), s32[]{:S(2)}) async-start(), calls=%async_computation.33 | async-start | bytes 9437184 | tf_op jit(solution)/shard_map/all_gather | solution.py:975
  122.2 110.7 %all-gather.12.cloned.1.call-start = ((), (), s32[]{:S(2)}) async-start(), calls=%async_computation.43 | async-start | bytes 5308416 | tf_op jit(solution)/shard_map/all_gather | solution.py:981
  206.7 77.5 %all-to-all-start.4 = ((bf16[4,4,64,2048]{3,2,1,0:T(8,128)(2,1)}), bf16[4,4,64,2048]{3,2,1,0:T(8,128)(2,1)}, u32[]{:S(2)}, u32[]{:S(2)}) async-start(bf16[4,4,64,2048]{3,2,1,0:T(8,128)(2,1)} %dispatch.5), calls=%async_computation.4 | async-start | bytes 8388608 | tf_op jit(solution)/shard_map/all_to_all | solution.py:921
  211.5 218.7 %all-gather.10.cloned.1.call-start = ((), (), s32[]{:S(2)}) async-start(), calls=%async_computation.34 | async-start | bytes 9437184 | tf_op jit(solution)/shard_map/all_gather | solution.py:1085
  211.6 72.6 %collective-permute-start.6 = (bf16[2,256,1408]{2,1,0:T(8,128)(2,1)}, bf16[2,256,1408]{2,1,0:T(8,128)(2,1)}, u32[]{:S(2)}, u32[]{:S(2)}) collective-permute-start(bf16[2,256,1408]{2,1,0:T(8,128)(2,1)} %get-tuple-element.143), channel_id=1, source_target_pairs={{0,24},{4,28},{8,0},{12,4},{16,8},{20,12},{24,16},{28,20},{1,25},{... | collective-permute-start | bytes 4325384 | tf_op jit(solution)/shard_map/ppermute | solution.py:929
  211.8 138.0 %collective-permute-start.5 = (bf16[2,256,1408]{2,1,0:T(8,128)(2,1)}, bf16[2,256,1408]{2,1,0:T(8,128)(2,1)}, u32[]{:S(2)}, u32[]{:S(2)}) collective-permute-start(bf16[2,256,1408]{2,1,0:T(8,128)(2,1)} %get-tuple-element.141), channel_id=1, source_target_pairs={{0,16},{4,20},{8,24},{12,28},{16,0},{20,4},{24,8},{28,12},{1,17},{... | collective-permute-start | bytes 4325384 | tf_op jit(solution)/shard_map/ppermute | solution.py:929
  212.3 137.4 %collective-permute-start.4 = (bf16[2,256,1408]{2,1,0:T(8,128)(2,1)}, bf16[2,256,1408]{2,1,0:T(8,128)(2,1)}, u32[]{:S(2)}, u32[]{:S(2)}) collective-permute-start(bf16[2,256,1408]{2,1,0:T(8,128)(2,1)} %get-tuple-element.139), channel_id=1, source_target_pairs={{0,8},{4,12},{8,16},{12,20},{16,24},{20,28},{24,0},{28,4},{1,9},{5... | collective-permute-start | bytes 4325384 | tf_op jit(solution)/shard_map/ppermute | solution.py:929
  515.5 65.8 %all-to-all-start.10 = ((bf16[4,4,64,2048]{3,2,1,0:T(8,128)(2,1)}), bf16[4,4,64,2048]{3,2,1,0:T(8,128)(2,1)}, u32[]{:S(2)}, u32[]{:S(2)}) async-start(bf16[4,4,64,2048]{3,2,1,0:T(8,128)(2,1)} %dispatch.7), calls=%async_computation.10 | async-start | bytes 8388608 | tf_op jit(solution)/shard_map/all_to_all | solution.py:921
  581.3 58.2 %all-to-all-start.6 = ((bf16[4,4,64,2048]{3,2,1,0:T(8,128)(2,1)}), bf16[4,4,64,2048]{3,2,1,0:T(8,128)(2,1)}, u32[]{:S(2)}, u32[]{:S(2)}) async-start(bf16[4,4,64,2048]{3,2,1,0:T(8,128)(2,1)} %dispatch.6), calls=%async_computation.6 | async-start | bytes 8388608 | tf_op jit(solution)/shard_map/all_to_all | solution.py:921
  639.6 58.6 %all-to-all-start.12 = ((bf16[4,4,64,2048]{3,2,1,0:T(8,128)(2,1)}), bf16[4,4,64,2048]{3,2,1,0:T(8,128)(2,1)}, u32[]{:S(2)}, u32[]{:S(2)}) async-start(bf16[4,4,64,2048]{3,2,1,0:T(8,128)(2,1)} %bitcast.297), calls=%async_computation.12 | async-start | bytes 8388608 | tf_op jit(solution)/shard_map/all_to_all | solution.py:921
  644.4 112.8 %reduce-scatter.9.cloned.1.call-start = ((), (), s32[]{:S(2)}) async-start(), calls=%async_computation.35 | async-start | bytes 2621440 | tf_op jit(solution)/shard_map/reduce_scatter | solution.py:1140
  703.7 111.3 %reduce-scatter.11.cloned.1.call-start = ((), (), s32[]{:S(2)}) async-start(), calls=%async_computation.36 | async-start | bytes 2621440 | tf_op jit(solution)/shard_map/reduce_scatter | solution.py:1140
  762.7 110.5 %reduce-scatter.13.cloned.1.call-start = ((), (), s32[]{:S(2)}) async-start(), calls=%async_computation.37 | async-start | bytes 2621440 | tf_op jit(solution)/shard_map/reduce_scatter | solution.py:1140
  843.2 117.0 %reduce-scatter.15.cloned.1.call-start = ((), (), s32[]{:S(2)}) async-start(), calls=%async_computation.38 | async-start | bytes 9437184 | tf_op jit(solution)/shard_map/reduce_scatter | solution.py:1155
  895.3 116.3 %reduce-scatter.17.cloned.1.call-start = ((), (), s32[]{:S(2)}) async-start(), calls=%async_computation.39 | async-start | bytes 4718592 | tf_op jit(solution)/shard_map/reduce_scatter | solution.py:1155
  979.4 239.3 %reduce-scatter.19.cloned.1.call-start = ((), (), s32[]{:S(2)}) async-start(), calls=%async_computation.40 | async-start | bytes 9437184 | tf_op jit(solution)/shard_map/reduce_scatter | solution.py:1155
  1053.9 53.4 %all-to-all-start.19 = ((bf16[4,4,64,2048]{3,2,1,0:T(8,128)(2,1)}), bf16[4,4,64,2048]{3,2,1,0:T(8,128)(2,1)}, u32[]{:S(2)}, u32[]{:S(2)}) async-start(bf16[4,4,64,2048]{3,2,1,0:T(8,128)(2,1)} %bitcast.295), calls=%async_computation.21 | async-start | bytes 8388608 | tf_op jit(solution)/shard_map/all_to_all | solution.py:921
  1131.8 133.9 %collective-permute-start.21 = (bf16[704,2048]{1,0:T(8,128)(2,1)}, bf16[704,2048]{1,0:T(8,128)(2,1)}, u32[]{:S(2)}, u32[]{:S(2)}) collective-permute-start(bf16[704,2048]{1,0:T(8,128)(2,1)} %dynamic-slice_bitcast_fusion), channel_id=1, source_target_pairs={{0,4},{4,0},{8,12},{12,8},{16,20},{20,16},{24,28},{28,24},{1,5},{5... | collective-permute-start | bytes 8650760 | tf_op jit(solution)/shard_map/ppermute | solution.py:934
  1139.7 75.2 %all-to-all-start.21 = ((bf16[4,128,2048]{2,1,0:T(8,128)(2,1)}), bf16[4,128,2048]{2,1,0:T(8,128)(2,1)}, u32[]{:S(2)}, u32[]{:S(2)}) async-start(bf16[4,128,2048]{2,1,0:T(8,128)(2,1)} %get-tuple-element.219), calls=%async_computation.28 | async-start | bytes 4194304 | tf_op jit(solution)/shard_map/all_to_all | solution.py:921
  1144.2 154.3 %reduce-scatter.23.cloned.1.call-start = ((), (), s32[]{:S(2)}) async-start(), calls=%async_computation.42 | async-start | bytes 147456 | tf_op jit(solution)/shard_map/reduce_scatter | solution.py:1272
  1144.8 65.8 %collective-permute-start.19 = (bf16[2,256,1408]{2,1,0:T(8,128)(2,1)}, bf16[2,256,1408]{2,1,0:T(8,128)(2,1)S(1)}, u32[]{:S(2)}, u32[]{:S(2)}) collective-permute-start(bf16[2,256,1408]{2,1,0:T(8,128)(2,1)} %get-tuple-element.227), channel_id=1, source_target_pairs={{0,16},{4,20},{8,24},{12,28},{16,0},{20,4},{24,8},{28,12},{1,17},{... | collective-permute-start | bytes 4325384 | tf_op jit(solution)/shard_map/ppermute | solution.py:929
  1157.0 115.2 %collective-permute-start.20 = (bf16[2,256,1408]{2,1,0:T(8,128)(2,1)}, bf16[2,256,1408]{2,1,0:T(8,128)(2,1)}, u32[]{:S(2)}, u32[]{:S(2)}) collective-permute-start(bf16[2,256,1408]{2,1,0:T(8,128)(2,1)} %get-tuple-element.243), channel_id=1, source_target_pairs={{0,24},{4,28},{8,0},{12,4},{16,8},{20,12},{24,16},{28,20},{1,25},{... | collective-permute-start | bytes 4325384 | tf_op jit(solution)/shard_map/ppermute | solution.py:929
  1220.4 104.3 %reduce-scatter.21.cloned.1.call-start = ((), (), s32[]{:S(2)}) async-start(), calls=%async_computation.41 | async-start | bytes 2621440 | tf_op jit(solution)/shard_map/reduce_scatter | solution.py:1244
  (106 other events, 1691.6 us)
Sparse Core Ops, SparseCore 0:
  9.6 83.4 all-gather.5
  94.7 80.6 all-gather.7
  177.6 55.2 all-gather.11
  349.9 80.2 all-gather.9
  703.8 42.4 reduce-scatter.8
  762.9 40.5 reduce-scatter.10
  820.8 40.5 reduce-scatter.12
  873.4 86.8 reduce-scatter.14
  963.3 48.3 reduce-scatter.16
  1013.9 103.8 reduce-scatter.18
  1220.5 59.9 reduce-scatter.22
  1282.7 41.9 reduce-scatter.20
